TPU v7x, 512 devices: a whole 4x4x16 slice. The times are simulated.
512 devices in a mesh: lon: 32 (over x, y, z_hi), lat: 16 (over z_lo, core).
Axes of the slice: x: 4, y: 4, z: 16 (z_hi: 2, z_lo: 8; z = z_hi * 8 + z_lo), core: 2. Of those that a mesh axis runs over, the one named last changes fastest.
Arguments:
- cells: bfloat16 [1024, 2048, 128], P('lat', 'lon'), may hold values from -6 to 6
- ocean_mask: int32 [1024, 2048], P('lat', 'lon'), may hold values from 0 to 1, as said below
- cotangent: bfloat16 [1024, 2048, 128], P('lat', 'lon'), may hold values from -6 to 6
- kernel: float32 [7, 7, 128], replicated, may hold values from -0.875 to 0.875
- conv_bias: float32 [128], replicated, may hold values from -3 to 3
- gain: float32 [128], replicated, may hold values from 0.1 to 1.9
- shift: float32 [128], replicated, may hold values from -3 to 3
- w_in: bfloat16 [128, 512], replicated, may hold values from -0.5 to 0.5
- b_in: float32 [512], replicated, may hold values from -3 to 3
- w_out: bfloat16 [512, 128], replicated, may hold values from -0.25 to 0.25
Outputs:
- cells_grad: bfloat16 [1024, 2048, 128], P('lat', 'lon')
- grad_kernel: float32 [7, 7, 128], replicated
- grad_bias: float32 [128], replicated
- grad_gain: float32 [128], replicated
- grad_shift: float32 [128], replicated
- grad_in: float32 [128, 512], replicated
- grad_b: float32 [512], replicated
- grad_out: float32 [512, 128], replicated
Inputs may be any that keep to these rules, and one draw needn't show every extreme that they name: `ocean_mask`: within each aligned 64 x 64 block the ocean cells are either all cells, none, or those on one side of a straight line; some blocks are all land and some all ocean.
All inputs are finite; a program needn't handle non-finite values.
Results may differ from a plain program's by a relative error of at most 0.006.
Values may be sent and summed in bfloat16 or wider, within the bound.
No kernel may reach another device: no remote copies, remote signals or barrier semaphores. Data moves between devices by JAX's collectives and lax.ppermute only.
A program may use at most 128 MiB of HBM per device.

v0:
```python
import jax
import jax.numpy as jnp
from jax import lax
from jax.sharding import PartitionSpec as P

KS = 7
HALF = 3


def with_halo(block, sides, width, periodic):
    for axis, dim in sides:
        count = lax.axis_size(axis)
        forward = [(i, i + 1) for i in range(count - 1)]
        if periodic:
            forward.append((count - 1, 0))
        backward = [(target, source) for source, target in forward]
        low = lax.ppermute(
            lax.slice_in_dim(block, block.shape[dim] - width, None, axis=dim), axis, forward
        )
        high = lax.ppermute(lax.slice_in_dim(block, 0, width, axis=dim), axis, backward)
        block = jnp.concatenate([low, block, high], axis=dim)
    return block


def depthwise(padded, kernel, height, across):
    summed = jnp.zeros((height, across, padded.shape[2]), jnp.float32)
    for row_off in range(KS):
        for col_off in range(KS):
            summed = summed + kernel[row_off, col_off] * padded[
                row_off : row_off + height, col_off : col_off + across
            ].astype(jnp.float32)
    return summed


def transposed(padded, kernel, height, across):
    summed = jnp.zeros((height, across, padded.shape[2]), jnp.float32)
    for row_off in range(KS):
        for col_off in range(KS):
            first_row = KS - 1 - row_off
            first_col = KS - 1 - col_off
            summed = summed + kernel[row_off, col_off] * padded[
                first_row : first_row + height, first_col : first_col + across
            ].astype(jnp.float32)
    return summed


def gelu_tanh(value):
    return jax.nn.gelu(value, approximate=True)


def section_one(padded, out_grad, cycle, kernel, conv_bias, gain, shift, w_in, b_in, w_out):
    ext_h, ext_w, channels = out_grad.shape
    height = ext_h - 2 * cycle
    across = ext_w - 2 * cycle
    conv = depthwise(padded, kernel, ext_h, ext_w) + conv_bias
    average = jnp.mean(conv, axis=-1, keepdims=True)
    centred = conv - average
    variance = jnp.mean(centred * centred, axis=-1, keepdims=True)
    inverse_std = lax.rsqrt(variance + 1e-06)
    scaled = centred * inverse_std
    normed = (scaled * gain + shift).astype(jnp.bfloat16).reshape(ext_h * ext_w, channels)
    preact = jnp.dot(normed, w_in, preferred_element_type=jnp.float32) + b_in
    activation = gelu_tanh(preact).astype(jnp.bfloat16)
    flat_grad = out_grad.reshape(ext_h * ext_w, channels)
    act_grad = lax.dot_general(
        flat_grad, w_out, (((1,), (1,)), ((), ())), preferred_element_type=jnp.float32
    )
    hidden_grad = jax.vjp(gelu_tanh, preact)[1](act_grad)[0].astype(jnp.bfloat16)
    inner_act = activation.reshape(ext_h, ext_w, -1).reshape(height * across, -1)
    inner_grad = out_grad.reshape(height * across, channels)
    grad_out = lax.dot_general(
        inner_act, inner_grad, (((0,), (0,)), ((), ())), preferred_element_type=jnp.float32
    )
    return (normed, scaled, inverse_std, hidden_grad, grad_out)


def section_two(padded, normed, scaled, inverse_std, hidden_grad, cycle, gain, w_in):
    ext_h, ext_w, channels = scaled.shape
    height = ext_h - 2 * cycle
    across = ext_w - 2 * cycle
    norm_grad = lax.dot_general(
        hidden_grad, w_in, (((1,), (1,)), ((), ())), preferred_element_type=jnp.float32
    ).reshape(ext_h, ext_w, channels)
    weighted = norm_grad * gain
    conv_grad = (
        inverse_std
        * (
            weighted
            - jnp.mean(weighted, axis=-1, keepdims=True)
            - scaled * jnp.mean(weighted * scaled, axis=-1, keepdims=True)
        )
    ).astype(jnp.bfloat16)
    hidden_in = hidden_grad.reshape(ext_h, ext_w, -1).reshape(height * across, -1)
    normed_in = normed.reshape(ext_h, ext_w, channels).reshape(height * across, channels)
    grad_in = lax.dot_general(
        normed_in, hidden_in, (((0,), (0,)), ((), ())), preferred_element_type=jnp.float32
    )
    grad_b = jnp.sum(hidden_in.astype(jnp.float32), axis=0)
    grad_gain = jnp.sum(norm_grad * scaled, axis=(0, 1))
    grad_shift = jnp.sum(norm_grad, axis=(0, 1))
    conv_wide = conv_grad.astype(jnp.float32)
    grad_bias = jnp.sum(conv_wide, axis=(0, 1))
    rows_list = []
    for row_off in range(KS):
        cols_list = []
        for col_off in range(KS):
            window = padded[row_off : row_off + height, col_off : col_off + across].astype(
                jnp.float32
            )
            cols_list.append(jnp.sum(conv_wide * window, axis=(0, 1)))
        rows_list.append(jnp.stack(cols_list))
    grad_kernel = jnp.stack(rows_list)
    return (conv_grad, grad_kernel, grad_bias, grad_gain, grad_shift, grad_in, grad_b)


def body(cells, ocean_mask, cotangent, kernel, conv_bias, gain, shift, w_in, b_in, w_out):
    height, across, channels = cells.shape
    ocean = ocean_mask.astype(jnp.bfloat16)[..., None]
    masked = cells * ocean
    out_grad = cotangent * ocean
    widened = with_halo(masked, (("lon", 1),), HALF, True)
    padded = with_halo(widened, (("lat", 0),), HALF, False)
    cycle = 0
    normed, scaled, inverse_std, hidden_grad, grad_out = section_one(
        padded, out_grad, cycle, kernel, conv_bias, gain, shift, w_in, b_in, w_out
    )
    conv_grad, grad_kernel, grad_bias, grad_gain, grad_shift, grad_in, grad_b = section_two(
        padded, normed, scaled, inverse_std, hidden_grad, cycle, gain, w_in
    )
    wide_grad = with_halo(conv_grad, (("lon", 1),), HALF, True)
    grad_padded = with_halo(wide_grad, (("lat", 0),), HALF, False)
    grad_kernel, grad_bias, grad_gain, grad_shift, grad_in, grad_b, grad_out = lax.psum(
        (grad_kernel, grad_bias, grad_gain, grad_shift, grad_in, grad_b, grad_out), ("lon", "lat")
    )
    spread_back = transposed(grad_padded, kernel, height, across)
    cells_grad = ((cotangent.astype(jnp.float32) + spread_back) * ocean.astype(jnp.float32)).astype(
        jnp.bfloat16
    )
    factor = lax.rsqrt(jnp.float32(height * across * lax.axis_size("lon") * lax.axis_size("lat")))
    return (
        cells_grad,
        grad_kernel * factor,
        grad_bias * factor,
        grad_gain * factor,
        grad_shift * factor,
        grad_in * factor,
        grad_b * factor,
        grad_out * factor,
    )


def solution(mesh):
    in_specs = (
        P("lat", "lon", None),
        P("lat", "lon"),
        P("lat", "lon", None),
        P(),
        P(),
        P(),
        P(),
        P(),
        P(),
        P(),
    )
    out_specs = (P("lat", "lon", None), P(), P(), P(), P(), P(), P(), P())
    return jax.shard_map(body, mesh=mesh, in_specs=in_specs, out_specs=out_specs, check_vma=False)
```

profile of v0, /device:TPU:1, one launch (start us, length us, event | category | flops | bytes accessed | tf_op | source)
XLA Modules:
  0.0 710.2 jit_solution(10950088295725203361)
XLA Ops:
  7.2 0.0 copy-start
  7.2 0.0 all-reduce.4.cloned.1.call-start
  7.2 0.8 fusion.144
  8.0 1.9 broadcast_multiply_fusion
  10.0 0.0 copy-start.6
  10.0 0.1 fusion.148
  10.0 16.3 %collective-permute-start = (bf16[64,3,128]{2,1,0:T(4,128)(2,1)S(1)}, bf16[64,3,128]{2,1,0:T(4,128)(2,1)S(1)}, u32[]{:S(2)}, u32[]{:S(2)}) collective-permute-start(bf16[64,3,128]{2,1,0:T(4,128)(2,1)S(1)} %get-tuple-element.94), channel_id=1, source_target_pairs={{0,16},{16,32},{32,48},{48,64},{64,80},{80,96},{96,112},{112,128},... | collective-permute-start | bytes 147464 | tf_op jit(solution)/shard_map/ppermute | solution.py:17
  26.3 6.6 collective-permute-start.1
  32.9 0.0 copy-done.9
  32.9 0.0 collective-permute-done
  32.9 7.1 %collective-permute-done.1 = bf16[64,3,128]{2,1,0:T(4,128)(2,1)S(1)} collective-permute-done((bf16[64,3,128]{2,1,0:T(4,128)(2,1)S(1)}, bf16[64,3,128]{2,1,0:T(4,128)(2,1)S(1)}, u32[]{:S(2)}, u32[]{:S(2)}) %collective-permute-start.1) | collective-permute-done | bytes 49184 | tf_op jit(solution)/shard_map/ppermute | solution.py:20
  40.1 0.0 copy-start.11
  40.1 6.5 collective-permute-start.2
  46.6 1.9 collective-permute-start.3
  48.5 0.0 collective-permute-done.2
  48.6 3.5 collective-permute-done.3
  52.1 0.6 maximum_maximum_fusion
  52.7 0.0 copy-done.6
  52.7 0.0 copy-done.11
  52.7 16.3 %fusion.145 = (f32[64,64]{1,0:T(8,128)S(1)}, f32[64,64,128]{2,1,0:T(8,128)S(1)}) fusion(f32[128]{0:T(128)S(1)} %copy-done.11, bf16[67,70,128]{2,1,0:T(8,128)(2,1)S(1)} %get-tuple-element.89, f32[128]{0:T(128)S(1)} %get-tuple-element.143, f32[128]{0:T(128)S(1)} %get-tuple-element.144, f32[128]{0:T(128)S(1)} %get-tuple-element.97, ...), kind=kLoop, calls=%fused_computation.356 | loop fusion | flops 87027712 | bytes 47326208 | tf_op jit(solution)/shard_map/reduce_sum | solution.py:56
  69.0 1.3 multiply_reduce_fusion.3
  70.3 0.0 copy-done.10
  70.3 0.0 copy-done.12
  70.3 1.3 add_convert_fusion
  71.6 0.0 copy-start.14
  71.6 1.2 fusion.149
  72.9 0.0 copy-done.14
  72.9 0.0 copy-start.13
  72.9 4.2 fusion.7
  77.1 6.7 convert_reduce_fusion.1
  83.7 1.9 copy-done.7
  85.6 1.5 fusion.150
  87.1 4.8 fusion.143
  91.9 0.1 div.17
  92.0 4.6 multiply_reduce_fusion
  96.6 6.4 fusion.129
  103.0 0.0 copy-start.1
  103.1 0.9 fusion.84
  104.0 5.3 fusion.101
  109.3 0.0 copy-done.1
  109.3 0.1 fusion.147
  109.4 0.0 copy-start.2
  109.5 8.6 %fusion.128 = (f32[128]{0:T(128)S(1)}, f32[128]{0:T(128)S(1)}, f32[128]{0:T(128)S(1)}, f32[128]{0:T(128)S(1)}, f32[128]{0:T(128)S(1)}, /*index=5*/f32[128]{0:T(1...) fusion(bf16[64,64,128]{2,1,0:T(8,128)(2,1)} %copy-done.1, ...), kind=kLoop, calls=%fused_computation.232 | loop fusion | flops 25688832 | bytes 5346304 | tf_op jit(solution)/shard_map/reduce_sum | solution.py:110
  118.2 105.2 %all-reduce = (f32[7,7,128]{2,1,0:T(8,128)S(1)}, f32[128]{0:T(128)S(1)}, f32[128]{0:T(128)S(1)}, f32[128]{0:T(128)S(1)}, f32[512]{0:T(512)S(1)}) all-reduce(f32[7,7,128]{2,1,0:T(8,128)S(1)} %constant_dynamic-update-slice_fusion, f32[128]{0:T(128)S(1)} %get-tuple-element.64, ...), channel_id=1, replica_groups=mesh['lon'=32,'lat'=16] {'lon','lat'}, use_global_device_ids=true, to_apply=%region_53.0 | all-reduce | flops 7168 | bytes 57344 | tf_op jit(solution)/shard_map/psum | solution.py:132
  223.4 0.6 broadcast_multiply_fusion.6
  224.0 0.6 broadcast_multiply_fusion.8
  224.6 6.7 collective-permute-start.5
  231.3 7.3 %collective-permute-start.4 = (bf16[64,3,128]{2,1,0:T(4,128)(2,1)S(1)}, bf16[64,3,128]{2,1,0:T(4,128)(2,1)S(1)}, u32[]{:S(2)}, u32[]{:S(2)}) collective-permute-start(bf16[64,3,128]{2,1,0:T(4,128)(2,1)S(1)} %get-tuple-element.93), channel_id=1, source_target_pairs={{0,16},{16,32},{32,48},{48,64},{64,80},{80,96},{96,112},{112,128},... | collective-permute-start | bytes 147464 | tf_op jit(solution)/shard_map/ppermute | solution.py:17
  238.6 0.0 all-reduce.4.cloned.1.call-update
  238.6 0.5 broadcast_multiply_fusion.9
  239.1 0.0 collective-permute-done.5
  239.1 13.6 %collective-permute-done.4 = bf16[64,3,128]{2,1,0:T(4,128)(2,1)S(1)} collective-permute-done((bf16[64,3,128]{2,1,0:T(4,128)(2,1)S(1)}, bf16[64,3,128]{2,1,0:T(4,128)(2,1)S(1)}, u32[]{:S(2)}, u32[]{:S(2)}) %collective-permute-start.4) | collective-permute-done | bytes 49184 | tf_op jit(solution)/shard_map/ppermute | solution.py:17
  252.8 0.0 copy-start.8
  252.8 2.5 collective-permute-start.6
  255.3 3.2 collective-permute-start.7
  258.5 0.5 broadcast_multiply_fusion.11
  259.0 0.0 collective-permute-done.6
  259.0 0.7 collective-permute-done.7
  259.7 0.6 pad_maximum_fusion.1
  260.3 0.0 copy-done.8
  260.3 16.7 %multiply_convert_fusion.2 = bf16[64,64,128]{2,1,0:T(8,128)(2,1)} fusion(bf16[64,64,128]{2,1,0:T(8,128)(2,1)S(1)} %copy-done.8, bf16[64,64,128]{2,1,0:T(8,128)(2,1)S(1)} %copy-done.2, bf16[64,3,128]{2,1,0:T(4,128)(2,1)S(1)} %collective-permute-done.4, bf16[64,3,128]{2,1,0:T(4,128)(2,1)S(1)} %collective-permute-done.5, ...), kind=kLoop, calls=%fused_computation.235 | loop fusion | flops 88080384 | bytes 47325696 | tf_op jit(solution)/shard_map/convert_element_type | solution.py:136
  277.0 423.0 %all-reduce.4.cloned.1.call-done = (f32[128,512]{1,0:T(8,128)}, f32[512,128]{1,0:T(8,128)}) async-done(((f32[128,512]{1,0:T(8,128)}, f32[512,128]{1,0:T(8,128)}), (f32[128,512]{1,0:T(8,128)}, f32[512,128]{1,0:T(8,128)})) %all-reduce.4.cloned.1.call-update) | async-done | bytes 524304 | tf_op jit(solution)/shard_map/psum | solution.py:132
  700.0 1.7 broadcast_multiply_fusion.3
  701.7 1.7 broadcast_multiply_fusion.2
  (36 shorter events, 0.4 us)
Async XLA Ops:
  7.2 64.5 %copy-start = (bf16[128,512]{1,0:T(8,128)(2,1)S(1)}, bf16[128,512]{1,0:T(8,128)(2,1)}, u32[]{:S(2)}) copy-start(bf16[128,512]{1,0:T(8,128)(2,1)} %param.17) | copy-start | bytes 393220
  7.2 692.8 %all-reduce.4.cloned.1.call-start = ((), (), s32[]{:S(2)}) async-start(), calls=%async_computation | async-start | bytes 1048576 | tf_op jit(solution)/shard_map/psum | solution.py:132
  8.0 24.9 %copy-start.9 = (f32[7,7,128]{2,1,0:T(8,128)S(1)}, f32[7,7,128]{2,1,0:T(8,128)}, u32[]{:S(2)}) copy-start(f32[7,7,128]{2,1,0:T(8,128)} %param.13) | copy-start | bytes 75268
  10.0 42.7 %copy-start.6 = (bf16[64,64,128]{2,1,0:T(8,128)(2,1)}, bf16[64,64,128]{2,1,0:T(8,128)(2,1)S(1)}, u32[]{:S(2)}) copy-start(bf16[64,64,128]{2,1,0:T(8,128)(2,1)S(1)} %get-tuple-element.146) | copy-start | bytes 3145732
  10.0 22.9 %collective-permute-start = (bf16[64,3,128]{2,1,0:T(4,128)(2,1)S(1)}, bf16[64,3,128]{2,1,0:T(4,128)(2,1)S(1)}, u32[]{:S(2)}, u32[]{:S(2)}) collective-permute-start(bf16[64,3,128]{2,1,0:T(4,128)(2,1)S(1)} %get-tuple-element.94), channel_id=1, source_target_pairs={{0,16},{16,32},{32,48},{48,64},{64,80},{80,96},{96,112},{112,128},... | collective-permute-start | bytes 147464 | tf_op jit(solution)/shard_map/ppermute | solution.py:17
  26.3 13.7 %collective-permute-start.1 = (bf16[64,3,128]{2,1,0:T(4,128)(2,1)S(1)}, bf16[64,3,128]{2,1,0:T(4,128)(2,1)S(1)}, u32[]{:S(2)}, u32[]{:S(2)}) collective-permute-start(bf16[64,3,128]{2,1,0:T(4,128)(2,1)S(1)} %get-tuple-element.95), channel_id=1, source_target_pairs={{16,0},{32,16},{48,32},{64,48},{80,64},{96,80},{112,96},{128,112},... | collective-permute-start | bytes 147464 | tf_op jit(solution)/shard_map/ppermute | solution.py:20
  40.1 12.6 %copy-start.11 = (f32[128]{0:T(128)S(1)}, f32[128]{0:T(128)}, u32[]{:S(2)}) copy-start(f32[128]{0:T(128)} %param.14) | copy-start | bytes 1540
  40.1 8.5 %collective-permute-start.2 = (bf16[3,70,128]{2,1,0:T(8,128)(2,1)S(1)}, bf16[3,70,128]{2,1,0:T(8,128)(2,1)S(1)}, u32[]{:S(2)}, u32[]{:S(2)}) collective-permute-start(bf16[3,70,128]{2,1,0:T(8,128)(2,1)S(1)} %get-tuple-element.90), channel_id=1, source_target_pairs={{0,1},{1,2},{2,3},{3,4},{4,5},{5,6},{6,7},{7,8},{8,9},{9,10},{10,1... | collective-permute-start | bytes 161288 | tf_op jit(solution)/shard_map/ppermute | solution.py:17
  46.6 5.5 collective-permute-start.3
  69.0 2.6 copy-start.3
  69.0 1.4 copy-start.10
  69.0 1.4 copy-start.12
  71.6 1.2 copy-start.14
  72.9 4.2 copy-start.13
  83.7 1.9 copy-start.7
  92.0 4.6 copy-start.4
  92.0 4.6 copy-start.5
  103.0 6.2 copy-start.1
  109.4 143.3 %copy-start.2 = (bf16[64,64,128]{2,1,0:T(8,128)(2,1)S(1)}, bf16[64,64,128]{2,1,0:T(8,128)(2,1)}, u32[]{:S(2)}) copy-start(bf16[64,64,128]{2,1,0:T(8,128)(2,1)} %copy-done.1) | copy-start | bytes 3145732
  224.6 14.5 %collective-permute-start.5 = (bf16[64,3,128]{2,1,0:T(4,128)(2,1)S(1)}, bf16[64,3,128]{2,1,0:T(4,128)(2,1)S(1)}, u32[]{:S(2)}, u32[]{:S(2)}) collective-permute-start(bf16[64,3,128]{2,1,0:T(4,128)(2,1)S(1)} %get-tuple-element.92), channel_id=1, source_target_pairs={{16,0},{32,16},{48,32},{64,48},{80,64},{96,80},{112,96},{128,112},... | collective-permute-start | bytes 147464 | tf_op jit(solution)/shard_map/ppermute | solution.py:20
  231.3 21.4 %collective-permute-start.4 = (bf16[64,3,128]{2,1,0:T(4,128)(2,1)S(1)}, bf16[64,3,128]{2,1,0:T(4,128)(2,1)S(1)}, u32[]{:S(2)}, u32[]{:S(2)}) collective-permute-start(bf16[64,3,128]{2,1,0:T(4,128)(2,1)S(1)} %get-tuple-element.93), channel_id=1, source_target_pairs={{0,16},{16,32},{32,48},{48,64},{64,80},{80,96},{96,112},{112,128},... | collective-permute-start | bytes 147464 | tf_op jit(solution)/shard_map/ppermute | solution.py:17
  252.8 7.6 %copy-start.8 = (bf16[64,64,128]{2,1,0:T(8,128)(2,1)S(1)}, bf16[64,64,128]{2,1,0:T(8,128)(2,1)}, u32[]{:S(2)}) copy-start(bf16[64,64,128]{2,1,0:T(8,128)(2,1)} %param.12) | copy-start | bytes 3145732
  252.8 6.2 collective-permute-start.6
  255.3 4.4 collective-permute-start.7
Sparse Core Ops, SparseCore 0:
  238.7 461.2 all-reduce.3
where the time goes:
time: 711 us; the launch traced here: 710 us
  waiting for transfers between devices  448 us (63%)
  blocking collectives  105 us (15%)
  other arithmetic  70.9 us (10%)
  starting transfers between devices  51 us (7%)
  matrix products  18.3 us (3%)
  between operations  14.5 us (2%)
    psum x1, waiting for transfers between devices, body(): lax.psum((grad_kernel, grad_bias, grad_gain, grad_shift, grad_in, grad_b,...  423 us
    psum x1, blocking collectives, body(): lax.psum((grad_kernel, grad_bias, grad_gain, grad_shift, grad_in, grad_b,...  105 us
    ppermute x4, starting transfers between devices, with_halo(): lax.ppermute(lax.slice_in_dim(block, block.shape[dim] - width, None, axis...  33.2 us
    reduce_sum x4, other arithmetic, section_two(): cols_list.append(jnp.sum(conv_wide * window, axis=(0, 1)))  21.2 us
    ppermute x4, starting transfers between devices, with_halo(): lax.ppermute(lax.slice_in_dim(block, 0, width, axis=dim), axis, backward)  17.7 us
    convert_element_type x1, other arithmetic, body(): ((cotangent.astype(jnp.float32) + spread_back) * ocean.astype(jnp.float32...  16.7 us
    reduce_sum x1, other arithmetic, section_one(): average = jnp.mean(conv, axis=-1, keepdims=True)  16.3 us
    ppermute x4, waiting for transfers between devices, with_halo(): lax.ppermute(lax.slice_in_dim(block, block.shape[dim] - width, None, axis...  14.3 us
  transfers between devices with their start and end apart: 9, of which 5 were waited for; matrix products, arithmetic and copies ran while one was open for 3% of the time, Pallas kernels for 0%

commit v1 on v0

v1 whole, which is shorter than its diff:
```python
import functools

import jax
import jax.numpy as jnp
from jax import lax
from jax.experimental import pallas as pl
from jax.experimental.pallas import tpu as pltpu
from jax.sharding import PartitionSpec as P

KS = 7
HALF = 3
SUB = 8
ROOT = 0.7978845608028654
CUBE = 0.044715
VMEM = pl.BlockSpec(memory_space=pltpu.VMEM)


def spread_rows(src_ref, tiles_ref, buf_ref, rows, taps):
    across = src_ref.shape[1]

    def one(row, _):
        buf_ref[0:across, :] = src_ref[row].astype(jnp.float32)
        for tap in range(taps):
            tiles_ref[row, tap] = buf_ref[pl.ds(tap, SUB, stride=SUB), :]
        return 0

    lax.fori_loop(0, rows, one, 0)


def conv_row(tiles_ref, kernel_ref, row, flip):
    total = [None] * SUB
    for a in range(KS):
        cells = [tiles_ref[row + a, t] for t in range(SUB + KS - 1)]
        for b in range(KS):
            ka, kb = (KS - 1 - a, KS - 1 - b) if flip else (a, b)
            weight = jnp.broadcast_to(kernel_ref[ka, kb : kb + 1, :], (SUB, 128))
            for t in range(SUB):
                term = weight * cells[t + b]
                total[t] = term if total[t] is None else total[t] + term
    return total


def gather_row(tiles, buf_ref):
    for t in range(SUB):
        buf_ref[pl.ds(t, SUB, stride=SUB), :] = tiles[t]
    return buf_ref[0 : SUB * SUB, :]


def block_kernel(
    chunk,
    padded_ref, out_grad_ref, kernel_ref, bias_ref, gain_ref, shift_ref, w_in_ref, b_in_ref, w_out_ref,
    conv_grad_ref, grad_bias_ref, grad_gain_ref, grad_shift_ref, grad_in_ref, grad_b_ref, grad_out_ref,
    tiles_ref, buf_ref, og_buf, conv_buf, og_tiles, grad_out_t,
):
    height = out_grad_ref.shape[0]
    cells = chunk * 64
    spread_rows(padded_ref, tiles_ref, buf_ref, height + KS - 1, SUB + KS - 1)
    for ref in (grad_bias_ref, grad_gain_ref, grad_shift_ref, grad_in_ref, grad_b_ref, grad_out_t):
        ref[...] = jnp.zeros_like(ref)
    bias = bias_ref[...]
    gain = gain_ref[...]
    shift = shift_ref[...]
    b_in = b_in_ref[...]

    def one(step, _):
        first = step * chunk

        def conv_one(r, _):
            row = first + r
            total = conv_row(tiles_ref, kernel_ref, row, False)
            for t in range(SUB):
                conv_buf[r, t] = total[t]
            og_buf[0:64, :] = out_grad_ref[row].astype(jnp.float32)
            for t in range(SUB):
                og_tiles[r, t] = og_buf[pl.ds(t, SUB, stride=SUB), :]
            return 0

        lax.fori_loop(0, chunk, conv_one, 0)
        conv = conv_buf[...].reshape(cells, 128) + bias
        out_grad = og_tiles[...].reshape(cells, 128).astype(jnp.bfloat16)
        average = jnp.mean(conv, axis=-1, keepdims=True)
        centred = conv - average
        variance = jnp.mean(centred * centred, axis=-1, keepdims=True)
        inverse = lax.rsqrt(variance + 1e-06)
        scaled = centred * inverse
        normed = (scaled * gain + shift).astype(jnp.bfloat16)
        v = jnp.dot(normed, w_in_ref[...], preferred_element_type=jnp.float32) + b_in
        act_grad = lax.dot_general(
            out_grad, w_out_ref[...], (((1,), (1,)), ((), ())), preferred_element_type=jnp.float32
        )
        square = v * v
        half = 0.5 + 0.5 * jnp.tanh(v * (ROOT + (ROOT * CUBE) * square))
        activation = (v * half).astype(jnp.bfloat16)
        slope = half + (half - half * half) * (v * (2 * ROOT + (6 * ROOT * CUBE) * square))
        hidden = (act_grad * slope).astype(jnp.bfloat16)
        grad_out_t[...] += lax.dot_general(
            out_grad, activation, (((0,), (0,)), ((), ())), preferred_element_type=jnp.float32
        )
        grad_in_ref[...] += lax.dot_general(
            normed, hidden, (((0,), (0,)), ((), ())), preferred_element_type=jnp.float32
        )
        grad_b_ref[...] += jnp.sum(
            hidden.astype(jnp.float32).reshape(cells // SUB, SUB, 512), axis=0
        )
        norm_grad = lax.dot_general(
            hidden, w_in_ref[...], (((1,), (1,)), ((), ())), preferred_element_type=jnp.float32
        )
        grad_gain_ref[...] += jnp.sum((norm_grad * scaled).reshape(-1, SUB, 128), axis=0)
        grad_shift_ref[...] += jnp.sum(norm_grad.reshape(-1, SUB, 128), axis=0)
        weighted = norm_grad * gain
        conv_grad = inverse * (
            weighted
            - jnp.mean(weighted, axis=-1, keepdims=True)
            - scaled * jnp.mean(weighted * scaled, axis=-1, keepdims=True)
        )
        rounded = conv_grad.astype(jnp.bfloat16).astype(jnp.float32).reshape(chunk, SUB, SUB, 128)
        grad_bias_ref[...] += jnp.sum(rounded, axis=(0, 1))
        for r in range(chunk):
            natural = gather_row([rounded[r, t] for t in range(SUB)], og_buf)
            conv_grad_ref[first + r] = natural.astype(jnp.bfloat16)
        return 0

    lax.fori_loop(0, height // chunk, one, 0)
    grad_out_ref[...] = grad_out_t[...].T


def tap_kernel(padded_ref, grad_ref, out_ref, tiles_ref, buf_ref, sums_ref, pair):
    height = grad_ref.shape[0]
    spread_rows(padded_ref, tiles_ref, buf_ref, height + KS - 1, SUB + KS - 1)
    sums_ref[...] = jnp.zeros_like(sums_ref)

    def one(row, _):
        buf_ref[0:64, :] = grad_ref[row].astype(jnp.float32)
        grads = [buf_ref[pl.ds(t, SUB, stride=SUB), :] for t in range(SUB)]
        for a in range(KS):
            cells = [tiles_ref[row + a, t] for t in range(SUB + KS - 1)]
            for b in range(KS):
                total = sums_ref[a, b]
                for t in range(SUB):
                    total = total + grads[t] * cells[t + b]
                sums_ref[a, b] = total
        return 0

    lax.fori_loop(0, height, one, 0)
    out_ref[...] = jnp.sum(sums_ref[...], axis=2)


def back_kernel(padded_ref, cot_ref, mask_ref, kernel_ref, out_ref, tiles_ref, buf_ref):
    height = cot_ref.shape[0]
    spread_rows(padded_ref, tiles_ref, buf_ref, height + KS - 1, SUB + KS - 1)

    def one(row, _):
        total = conv_row(tiles_ref, kernel_ref, row, True)
        spread = gather_row(total, buf_ref)
        out_ref[row] = (
            (cot_ref[row].astype(jnp.float32) + spread) * mask_ref[row].astype(jnp.float32)
        ).astype(jnp.bfloat16)
        return 0

    lax.fori_loop(0, height, one, 0)


def shifted(piece, axis, up, periodic):
    count = lax.axis_size(axis)
    pairs = [(i, i + 1) for i in range(count - 1)]
    if periodic:
        pairs.append((count - 1, 0))
    if not up:
        pairs = [(target, source) for source, target in pairs]
    return lax.ppermute(piece, axis, pairs)


def with_halo(block):
    west = shifted(block[:, -HALF:], "lon", True, True)
    east = shifted(block[:, :HALF], "lon", False, True)
    wide = jnp.concatenate([west, block, east], axis=1)
    south = shifted(wide[-HALF:], "lat", True, False)
    north = shifted(wide[:HALF], "lat", False, False)
    return jnp.concatenate([south, wide, north], axis=0)


def f32(*shape):
    return jax.ShapeDtypeStruct(shape, jnp.float32)


def body(cells, ocean_mask, cotangent, kernel, conv_bias, gain, shift, w_in, b_in, w_out, chunk=4):
    height, across, channels = cells.shape
    ocean = jnp.broadcast_to(ocean_mask.astype(jnp.bfloat16)[..., None], cells.shape)
    masked = cells * ocean
    out_grad = cotangent * ocean
    padded = with_halo(masked)
    tall = height + 2 * HALF
    tiles = pltpu.VMEM((tall, SUB + KS - 1, SUB, channels), jnp.float32)
    row_buf = pltpu.VMEM((72, channels), jnp.float32)
    hidden = w_in.shape[1]
    conv_grad, bias8, gain8, shift8, grad_in, b8, grad_out = pl.pallas_call(
        functools.partial(block_kernel, chunk),
        out_shape=(
            jax.ShapeDtypeStruct(cells.shape, jnp.bfloat16),
            f32(SUB, channels), f32(SUB, channels), f32(SUB, channels),
            f32(channels, hidden), f32(SUB, hidden), f32(hidden, channels),
        ),
        in_specs=[VMEM] * 9,
        out_specs=[VMEM] * 7,
        scratch_shapes=[
            tiles, row_buf, row_buf,
            pltpu.VMEM((chunk, SUB, SUB, channels), jnp.float32),
            pltpu.VMEM((chunk, SUB, SUB, channels), jnp.float32),
            pltpu.VMEM((channels, hidden), jnp.float32),
        ],
        name="block",
    )(
        padded, out_grad, kernel, conv_bias.reshape(1, -1), gain.reshape(1, -1), shift.reshape(1, -1),
        w_in, b_in.reshape(1, -1), w_out,
    )
    grad_padded = with_halo(conv_grad)
    grad_kernel = pl.pallas_call(
        functools.partial(tap_kernel, pair=None),
        out_shape=f32(KS, KS, channels),
        in_specs=[VMEM] * 2,
        out_specs=VMEM,
        scratch_shapes=[tiles, row_buf, pltpu.VMEM((KS, KS, SUB, channels), jnp.float32)],
        name="taps",
    )(padded, conv_grad)
    grads = (
        grad_kernel, jnp.sum(bias8, 0), jnp.sum(gain8, 0), jnp.sum(shift8, 0), grad_in, jnp.sum(b8, 0), grad_out
    )
    grads = lax.psum(grads, ("lon", "lat"))
    cells_grad = pl.pallas_call(
        back_kernel,
        out_shape=jax.ShapeDtypeStruct(cells.shape, jnp.bfloat16),
        in_specs=[VMEM] * 4,
        out_specs=VMEM,
        scratch_shapes=[tiles, row_buf],
        name="back",
    )(grad_padded, cotangent, ocean, kernel)
    factor = lax.rsqrt(jnp.float32(height * across * lax.axis_size("lon") * lax.axis_size("lat")))
    return (cells_grad,) + tuple(g * factor for g in grads)


def solution(mesh):
    whole = P("lat", "lon", None)
    in_specs = (whole, P("lat", "lon"), whole) + (P(),) * 7
    out_specs = (whole,) + (P(),) * 7
    return jax.shard_map(body, mesh=mesh, in_specs=in_specs, out_specs=out_specs, check_vma=False)
```

time: 711 us -> 684 us (0.962)
  other arithmetic: 70.9 us -> 12.4 us
  Pallas kernels: 0 us -> 51 us
  matrix products: 18.3 us -> 0 us
    pallas_call x0 -> x3, Pallas kernels: none -> 51 us  [the longest x1 27.7 us: body(): pl.pallas_call(functools.partial(block_kernel, chunk), out_shape=(jax.Sha...]
    reduce_sum x7 -> x4, other arithmetic: 43.4 us -> 0.07 us  [the longest x1 0.02 us: body(): jnp.sum(b8, 0)]
    dot_general x5 -> x0, matrix products: 18.3 us -> none  [the longest x1 6.66 us: section_one(): lax.dot_general(flat_grad, w_out, (((1,), (1,)), ((), ())), preferred_ele...]
    convert_element_type x3 -> x1, other arithmetic: 18.7 us -> 0.76 us  [body(): ocean_mask.astype(jnp.bfloat16)[..., None]]
    ppermute x8, waiting for transfers between devices: 24.9 us -> 17.2 us  [shifted(): return lax.ppermute(piece, axis, pairs)]
  transfers between devices with their start and end apart: 9 -> 9, of which waited for: 5 -> 5; matrix products, arithmetic and copies ran while one was open for 3% -> 1% of each run, Pallas kernels for 0% -> 2%
where the time goes in v1:
time: 684 us; the launch traced here: 683 us
  waiting for transfers between devices  441 us (64%)
  blocking collectives  105 us (15%)
  starting transfers between devices  57.9 us (8%)
  Pallas kernels  51 us (7%)
  between operations  14.2 us (2%)
  other arithmetic  12.4 us (2%)
    psum x1, waiting for transfers between devices, body(): grads = lax.psum(grads, ('lon', 'lat'))  424 us
    psum x1, blocking collectives, body(): grads = lax.psum(grads, ('lon', 'lat'))  105 us
    ppermute x8, starting transfers between devices, shifted(): return lax.ppermute(piece, axis, pairs)  57.8 us
    pallas_call x1, Pallas kernels, body(): pl.pallas_call(functools.partial(block_kernel, chunk), out_shape=(jax.Sha...  27.7 us
    ppermute x8, waiting for transfers between devices, shifted(): return lax.ppermute(piece, axis, pairs)  17.2 us
  transfers between devices with their start and end apart: 9, of which 5 were waited for; matrix products, arithmetic and copies ran while one was open for 1% of the time, Pallas kernels for 2%

profile of v1, /device:TPU:1, one launch (start us, length us, event | category | flops | bytes accessed | tf_op | source)
XLA Modules:
  0.0 683.5 jit_solution(17951014013266373919)
XLA Ops:
  7.2 0.0 all-reduce.4.cloned.1.call-start
  7.2 0.8 convert_element_type.3
  8.0 2.7 broadcast_multiply_fusion
  10.7 0.1 fusion.1
  10.7 16.3 %collective-permute-start = (bf16[64,3,128]{2,1,0:T(4,128)(2,1)S(1)}, bf16[64,3,128]{2,1,0:T(4,128)(2,1)S(1)}, u32[]{:S(2)}, u32[]{:S(2)}) collective-permute-start(bf16[64,3,128]{2,1,0:T(4,128)(2,1)S(1)} %get-tuple-element.35), channel_id=1, source_target_pairs={{0,16},{16,32},{32,48},{48,64},{64,80},{80,96},{96,112},{112,128},... | collective-permute-start | bytes 147464 | tf_op jit(solution)/shard_map/ppermute | solution.py:170
  27.0 6.6 collective-permute-start.1
  33.6 0.0 collective-permute-done
  33.6 7.2 %collective-permute-done.1 = bf16[64,3,128]{2,1,0:T(4,128)(2,1)S(1)} collective-permute-done((bf16[64,3,128]{2,1,0:T(4,128)(2,1)S(1)}, bf16[64,3,128]{2,1,0:T(4,128)(2,1)S(1)}, u32[]{:S(2)}, u32[]{:S(2)}) %collective-permute-start.1) | collective-permute-done | bytes 49184 | tf_op jit(solution)/shard_map/ppermute | solution.py:170
  40.8 6.5 collective-permute-start.2
  47.3 1.9 collective-permute-start.3
  49.2 0.0 collective-permute-done.2
  49.2 3.5 collective-permute-done.3
  52.8 1.6 pad_maximum_fusion.padded_ref
  54.4 27.7 %block.1 = (bf16[64,64,128]{2,1,0:T(8,128)(2,1)}, f32[8,128]{1,0:T(8,128)}, f32[8,128]{1,0:T(8,128)}, f32[8,128]{1,0:T(8,128)}, f32[128,512]{1,0:T(8,128)}, /*index=5*/f32[8,512]{1,0:T(8,128)}, f32[512,128]{1,0:T(8,128)}) custom-call(bf16[70,70,128]{2,1,0:T(8,128)(2,1)} %pad_maximum_fusion.padded_ref, bf16[64,64,128]{2,1,0:T(8,128)(2,1)} %get-tuple-element.37.out_grad_ref, ...), custom_call_target="tpu_custom_call" | custom-call | tf_op jit(solution)/shard_map/block/pallas_call | solution.py:196
  82.1 0.0 copy-start
  82.1 0.0 copy-start.1
  82.1 0.0 copy-start.4
  82.1 0.0 copy-start.3
  82.1 0.0 copy-start.2
  82.1 11.4 %taps.1 = f32[7,7,128]{2,1,0:T(8,128)} custom-call(bf16[70,70,128]{2,1,0:T(8,128)(2,1)} %pad_maximum_fusion.padded_ref, bf16[64,64,128]{2,1,0:T(8,128)(2,1)} %get-tuple-element.15.grad_ref), custom_call_target="tpu_custom_call" | custom-call | tf_op jit(solution)/shard_map/taps/pallas_call | solution.py:217
  93.5 0.0 copy-done
  93.5 0.1 fusion
  93.6 0.0 copy-done.1
  93.6 0.0 copy-done.4
  93.7 0.0 copy-done.3
  93.7 0.0 copy-done.2
  93.7 105.2 %all-reduce = (f32[7,7,128]{2,1,0:T(8,128)S(1)}, f32[128]{0:T(128)S(1)}, f32[128]{0:T(128)S(1)}, f32[128]{0:T(128)S(1)}, f32[512]{0:T(512)S(1)}) all-reduce(f32[7,7,128]{2,1,0:T(8,128)} %taps.1, f32[128]{0:T(128)S(1)} %reduce_sum.36, f32[128]{0:T(128)S(1)} %reduce_sum.37, ...), channel_id=1, replica_groups=mesh['lon'=32,'lat'=16] {'lon','lat'}, use_global_device_ids=true, to_apply=%region_0.0 | all-reduce | flops 7168 | bytes 57344 | tf_op jit(solution)/shard_map/psum | solution.py:228
  198.9 0.6 broadcast_multiply_fusion.4
  199.5 0.6 broadcast_multiply_fusion.5
  200.1 5.8 collective-permute-start.4
  205.9 12.4 %collective-permute-start.5 = (bf16[64,3,128]{2,1,0:T(4,128)(2,1)S(1)}, bf16[64,3,128]{2,1,0:T(4,128)(2,1)S(1)}, u32[]{:S(2)}, u32[]{:S(2)}) collective-permute-start(bf16[64,3,128]{2,1,0:T(4,128)(2,1)S(1)} %get-tuple-element.34), channel_id=1, source_target_pairs={{16,0},{32,16},{48,32},{64,48},{80,64},{96,80},{112,96},{128,112},... | collective-permute-start | bytes 147464 | tf_op jit(solution)/shard_map/ppermute | solution.py:170
  218.3 0.0 all-reduce.4.cloned.1.call-update
  218.4 0.5 broadcast_multiply_fusion.6
  218.9 0.0 collective-permute-done.4
  218.9 3.1 collective-permute-done.5
  222.0 6.5 collective-permute-start.6
  228.5 1.9 collective-permute-start.7
  230.4 0.5 broadcast_multiply_fusion.8
  230.9 0.0 collective-permute-done.6
  230.9 3.5 collective-permute-done.7
  234.4 1.6 pad_maximum_fusion.1.padded_ref
  236.0 1.6 broadcast_in_dim.2.mask_ref
  237.5 11.8 %back.1 = bf16[64,64,128]{2,1,0:T(8,128)(2,1)} custom-call(bf16[70,70,128]{2,1,0:T(8,128)(2,1)} %pad_maximum_fusion.1.padded_ref, bf16[64,64,128]{2,1,0:T(8,128)(2,1)} %cot_ref.1, bf16[64,64,128]{2,1,0:T(8,128)(2,1)} %broadcast_in_dim.2.mask_ref, f32[7,7,128]{2,1,0:T(8,128)} %kernel_ref.3), custom_call_target="tpu_custom_call" | custom-call | tf_op jit(solution)/shard_map/back/pallas_call | solution.py:229
  249.4 423.9 %all-reduce.4.cloned.1.call-done = (f32[128,512]{1,0:T(8,128)}, f32[512,128]{1,0:T(8,128)}) async-done(((f32[128,512]{1,0:T(8,128)}, f32[512,128]{1,0:T(8,128)}), (f32[128,512]{1,0:T(8,128)}, f32[512,128]{1,0:T(8,128)})) %all-reduce.4.cloned.1.call-update) | async-done | bytes 524304 | tf_op jit(solution)/shard_map/psum | solution.py:228
  673.3 1.7 broadcast_multiply_fusion.2
  674.9 1.7 broadcast_multiply_fusion.3
  (6 shorter events, 0.2 us)
Async XLA Ops:
  7.2 666.1 %all-reduce.4.cloned.1.call-start = ((), (), s32[]{:S(2)}) async-start(), calls=%async_computation | async-start | bytes 1048576 | tf_op jit(solution)/shard_map/psum | solution.py:228
  10.7 22.8 %collective-permute-start = (bf16[64,3,128]{2,1,0:T(4,128)(2,1)S(1)}, bf16[64,3,128]{2,1,0:T(4,128)(2,1)S(1)}, u32[]{:S(2)}, u32[]{:S(2)}) collective-permute-start(bf16[64,3,128]{2,1,0:T(4,128)(2,1)S(1)} %get-tuple-element.35), channel_id=1, source_target_pairs={{0,16},{16,32},{32,48},{48,64},{64,80},{80,96},{96,112},{112,128},... | collective-permute-start | bytes 147464 | tf_op jit(solution)/shard_map/ppermute | solution.py:170
  27.0 13.7 %collective-permute-start.1 = (bf16[64,3,128]{2,1,0:T(4,128)(2,1)S(1)}, bf16[64,3,128]{2,1,0:T(4,128)(2,1)S(1)}, u32[]{:S(2)}, u32[]{:S(2)}) collective-permute-start(bf16[64,3,128]{2,1,0:T(4,128)(2,1)S(1)} %get-tuple-element.36), channel_id=1, source_target_pairs={{16,0},{32,16},{48,32},{64,48},{80,64},{96,80},{112,96},{128,112},... | collective-permute-start | bytes 147464 | tf_op jit(solution)/shard_map/ppermute | solution.py:170
  40.8 8.4 %collective-permute-start.2 = (bf16[3,70,128]{2,1,0:T(8,128)(2,1)S(1)}, bf16[3,70,128]{2,1,0:T(8,128)(2,1)S(1)}, u32[]{:S(2)}, u32[]{:S(2)}) collective-permute-start(bf16[3,70,128]{2,1,0:T(8,128)(2,1)S(1)} %get-tuple-element.31), channel_id=1, source_target_pairs={{0,1},{1,2},{2,3},{3,4},{4,5},{5,6},{6,7},{7,8},{8,9},{9,10},{10,1... | collective-permute-start | bytes 161288 | tf_op jit(solution)/shard_map/ppermute | solution.py:170
  47.3 5.5 collective-permute-start.3
  82.1 11.5 %copy-start = (bf16[64,64,128]{2,1,0:T(8,128)(2,1)S(1)}, bf16[64,64,128]{2,1,0:T(8,128)(2,1)}, u32[]{:S(2)}) copy-start(bf16[64,64,128]{2,1,0:T(8,128)(2,1)} %get-tuple-element.15.grad_ref) | copy-start | bytes 3145732
  82.1 11.5 %copy-start.1 = (f32[8,512]{1,0:T(8,128)S(1)}, f32[8,512]{1,0:T(8,128)}, u32[]{:S(2)}) copy-start(f32[8,512]{1,0:T(8,128)} %get-tuple-element.20) | copy-start | bytes 49156
  82.1 11.5 %copy-start.4 = (f32[8,128]{1,0:T(8,128)S(1)}, f32[8,128]{1,0:T(8,128)}, u32[]{:S(2)}) copy-start(f32[8,128]{1,0:T(8,128)} %get-tuple-element.16) | copy-start | bytes 12292
  82.1 11.6 %copy-start.3 = (f32[8,128]{1,0:T(8,128)S(1)}, f32[8,128]{1,0:T(8,128)}, u32[]{:S(2)}) copy-start(f32[8,128]{1,0:T(8,128)} %get-tuple-element.17) | copy-start | bytes 12292
  82.1 11.6 %copy-start.2 = (f32[8,128]{1,0:T(8,128)S(1)}, f32[8,128]{1,0:T(8,128)}, u32[]{:S(2)}) copy-start(f32[8,128]{1,0:T(8,128)} %get-tuple-element.18) | copy-start | bytes 12292
  200.1 18.8 %collective-permute-start.4 = (bf16[64,3,128]{2,1,0:T(4,128)(2,1)S(1)}, bf16[64,3,128]{2,1,0:T(4,128)(2,1)S(1)}, u32[]{:S(2)}, u32[]{:S(2)}) collective-permute-start(bf16[64,3,128]{2,1,0:T(4,128)(2,1)S(1)} %get-tuple-element.33), channel_id=1, source_target_pairs={{0,16},{16,32},{32,48},{48,64},{64,80},{80,96},{96,112},{112,128},... | collective-permute-start | bytes 147464 | tf_op jit(solution)/shard_map/ppermute | solution.py:170
  205.9 16.0 %collective-permute-start.5 = (bf16[64,3,128]{2,1,0:T(4,128)(2,1)S(1)}, bf16[64,3,128]{2,1,0:T(4,128)(2,1)S(1)}, u32[]{:S(2)}, u32[]{:S(2)}) collective-permute-start(bf16[64,3,128]{2,1,0:T(4,128)(2,1)S(1)} %get-tuple-element.34), channel_id=1, source_target_pairs={{16,0},{32,16},{48,32},{64,48},{80,64},{96,80},{112,96},{128,112},... | collective-permute-start | bytes 147464 | tf_op jit(solution)/shard_map/ppermute | solution.py:170
  222.0 8.9 %collective-permute-start.6 = (bf16[3,70,128]{2,1,0:T(8,128)(2,1)S(1)}, bf16[3,70,128]{2,1,0:T(8,128)(2,1)S(1)}, u32[]{:S(2)}, u32[]{:S(2)}) collective-permute-start(bf16[3,70,128]{2,1,0:T(8,128)(2,1)S(1)} %get-tuple-element.29), channel_id=1, source_target_pairs={{0,1},{1,2},{2,3},{3,4},{4,5},{5,6},{6,7},{7,8},{8,9},{9,10},{10,1... | collective-permute-start | bytes 161288 | tf_op jit(solution)/shard_map/ppermute | solution.py:170
  228.5 5.9 collective-permute-start.7
Sparse Core Ops, SparseCore 0:
  218.5 454.7 all-reduce.3

commit v2 on v1

--- a/solution.py
+++ b/solution.py
@@ -9,6 +9,7 @@
 
 KS = 7
 HALF = 3
+SMALL = 64
 SUB = 8
 ROOT = 0.7978845608028654
 CUBE = 0.044715
@@ -124,7 +125,10 @@
     grad_out_ref[...] = grad_out_t[...].T
 
 
-def tap_kernel(padded_ref, grad_ref, out_ref, tiles_ref, buf_ref, sums_ref, pair):
+def tap_kernel(
+    padded_ref, grad_ref, grad_in_ref, grad_out_ref, bias_ref, gain_ref, shift_ref, b_ref,
+    out_ref, tiles_ref, buf_ref, sums_ref, small_ref,
+):
     height = grad_ref.shape[0]
     spread_rows(padded_ref, tiles_ref, buf_ref, height + KS - 1, SUB + KS - 1)
     sums_ref[...] = jnp.zeros_like(sums_ref)
@@ -142,7 +146,88 @@
         return 0
 
     lax.fori_loop(0, height, one, 0)
-    out_ref[...] = jnp.sum(sums_ref[...], axis=2)
+    small_ref[...] = jnp.zeros_like(small_ref)
+    for a in range(KS):
+        for b in range(KS):
+            small_ref[a * KS + b] = jnp.sum(sums_ref[a, b], axis=0)
+    for at, ref in enumerate((bias_ref, gain_ref, shift_ref)):
+        small_ref[KS * KS + at] = jnp.sum(ref[...], axis=0)
+    for q in range(4):
+        small_ref[KS * KS + 3 + q] = jnp.sum(b_ref[:, q * 128 : (q + 1) * 128], axis=0)
+    parts = out_ref.shape[0]
+    rows = 1024 // parts
+    each = 128 // rows
+    for q in range(4):
+        block = grad_in_ref[:, q * 128 : (q + 1) * 128].reshape(each, rows, 128)
+        out_ref[q * each : (q + 1) * each, 0:rows, :] = block.astype(jnp.bfloat16)
+    block = grad_out_ref[...].reshape(parts // 2, rows, 128)
+    out_ref[parts // 2 :, 0:rows, :] = block.astype(jnp.bfloat16)
+    tail = small_ref[...].reshape(parts, SMALL // parts, 128)
+    spare = out_ref.shape[1] - rows - SMALL // parts
+    if spare:
+        tail = jnp.concatenate([tail, jnp.zeros((parts, spare, 128), jnp.float32)], axis=1)
+    out_ref[:, rows:, :] = tail.astype(jnp.bfloat16)
+
+
+def fold_kernel(parts_ref, out_ref):
+    total = jnp.sum(parts_ref[...].astype(jnp.float32), axis=0).astype(jnp.bfloat16)
+    out_ref[...] = jnp.broadcast_to(total[None], out_ref.shape)
+
+
+def unpack_kernel(factor, all_ref, kernel_ref, bias_ref, gain_ref, shift_ref, in_ref, b_ref, out_ref):
+    parts = all_ref.shape[0]
+    rows = 1024 // parts
+    each = 128 // rows
+    for q in range(4):
+        block = all_ref[q * each : (q + 1) * each, 0:rows, :].astype(jnp.float32)
+        in_ref[:, q * 128 : (q + 1) * 128] = block.reshape(128, 128) * factor
+    block = all_ref[parts // 2 :, 0:rows, :].astype(jnp.float32)
+    out_ref[...] = block.reshape(512, 128) * factor
+    small = all_ref[:, rows:, :].astype(jnp.float32) * factor
+
+    def row(r):
+        return small[r // (SMALL // parts), r % (SMALL // parts)]
+
+    for a in range(KS):
+        for b in range(KS):
+            kernel_ref[a, b] = row(a * KS + b)
+    for at, ref in enumerate((bias_ref, gain_ref, shift_ref)):
+        ref[0] = row(KS * KS + at)
+    for q in range(4):
+        b_ref[0, q * 128 : (q + 1) * 128] = row(KS * KS + 3 + q)
+
+
+def groups():
+    count_lon, count_lat = lax.axis_size("lon"), lax.axis_size("lat")
+    plane = [[[] for _ in range(count_lat // 2)] for _ in range(2)]
+    column = [[[] for _ in range(2)] for _ in range(count_lon // 2)]
+    for lon in range(count_lon):
+        for lat in range(count_lat):
+            at = lon * count_lat + lat
+            plane[lon % 2][lat // 2].append(at)
+            column[lon // 2][lat % 2].append(at)
+    return [g for part in plane for g in part], [g for part in column for g in part]
+
+
+def exchange(parts, members):
+    return lax.all_to_all(parts, ("lon", "lat"), 0, 0, tiled=True, axis_index_groups=members)
+
+
+def summed(packed):
+    plane, column = groups()
+
+    def fold(parts, count):
+        return pl.pallas_call(
+            fold_kernel,
+            out_shape=jax.ShapeDtypeStruct((count,) + parts.shape[1:], jnp.bfloat16),
+            in_specs=[VMEM],
+            out_specs=VMEM,
+            name="fold",
+        )(parts)
+
+    held = exchange(packed, plane)
+    held = exchange(fold(held, len(column[0])), column)
+    return exchange(fold(held, len(plane[0])), plane)
 
 
 def back_kernel(padded_ref, cot_ref, mask_ref, kernel_ref, out_ref, tiles_ref, buf_ref):
@@ -214,18 +299,19 @@
         w_in, b_in.reshape(1, -1), w_out,
     )
     grad_padded = with_halo(conv_grad)
-    grad_kernel = pl.pallas_call(
-        functools.partial(tap_kernel, pair=None),
-        out_shape=f32(KS, KS, channels),
-        in_specs=[VMEM] * 2,
+    parts = lax.axis_size("lon")
+    packed = pl.pallas_call(
+        tap_kernel,
+        out_shape=jax.ShapeDtypeStruct((parts, 1024 // parts + max(8, SMALL // parts), channels), jnp.bfloat16),
+        in_specs=[VMEM] * 8,
         out_specs=VMEM,
-        scratch_shapes=[tiles, row_buf, pltpu.VMEM((KS, KS, SUB, channels), jnp.float32)],
+        scratch_shapes=[
+            tiles, row_buf, pltpu.VMEM((KS, KS, SUB, channels), jnp.float32),
+            pltpu.VMEM((64, channels), jnp.float32),
+        ],
         name="taps",
-    )(padded, conv_grad)
-    grads = (
-        grad_kernel, jnp.sum(bias8, 0), jnp.sum(gain8, 0), jnp.sum(shift8, 0), grad_in, jnp.sum(b8, 0), grad_out
-    )
-    grads = lax.psum(grads, ("lon", "lat"))
+    )(padded, conv_grad, grad_in, grad_out, bias8, gain8, shift8, b8)
+    total = summed(packed)
     cells_grad = pl.pallas_call(
         back_kernel,
         out_shape=jax.ShapeDtypeStruct(cells.shape, jnp.bfloat16),
@@ -234,8 +320,18 @@
         scratch_shapes=[tiles, row_buf],
         name="back",
     )(grad_padded, cotangent, ocean, kernel)
-    factor = lax.rsqrt(jnp.float32(height * across * lax.axis_size("lon") * lax.axis_size("lat")))
-    return (cells_grad,) + tuple(g * factor for g in grads)
+    count = height * across * lax.axis_size("lon") * lax.axis_size("lat")
+    gk, gb, gg, gs, gi, gh, go = pl.pallas_call(
+        functools.partial(unpack_kernel, count ** -0.5),
+        out_shape=(
+            f32(KS, KS, channels), f32(1, channels), f32(1, channels), f32(1, channels),
+            f32(channels, hidden), f32(1, hidden), f32(hidden, channels),
+        ),
+        in_specs=[VMEM],
+        out_specs=[VMEM] * 7,
+        name="unpack",
+    )(total)
+    return cells_grad, gk, gb[0], gg[0], gs[0], gi, gh[0], go
 
 
 def solution(mesh):

time: 684 us -> 172 us (0.25)
  waiting for transfers between devices: 441 us -> 15 us
  blocking collectives: 105 us -> 17.1 us
  starting transfers between devices: 57.9 us -> 72.2 us
  between operations: 14.2 us -> 0.79 us
    psum x1 -> x0, waiting for transfers between devices: 424 us -> none  [body(): grads = lax.psum(grads, ('lon', 'lat'))]
    psum x1 -> x0, blocking collectives: 105 us -> none  [body(): grads = lax.psum(grads, ('lon', 'lat'))]
    all_to_all x0 -> x1, blocking collectives: none -> 17.1 us  [exchange(): lax.all_to_all(parts, ('lon', 'lat'), 0, 0, tiled=True, axis_index_groups...]
    all_to_all x0 -> x2, starting transfers between devices: none -> 13.5 us  [exchange(): lax.all_to_all(parts, ('lon', 'lat'), 0, 0, tiled=True, axis_index_groups...]
    pallas_call x1 -> x4, Pallas kernels: 11.4 us -> 16.8 us  [the longest x1 11.6 us: body(): pl.pallas_call(tap_kernel, out_shape=jax.ShapeDtypeStruct((parts, 1024 //...]
  transfers between devices with their start and end apart: 9 -> 10, of which waited for: 5 -> 5; matrix products, arithmetic and copies ran while one was open for 1% -> 2% of each run, Pallas kernels for 2% -> 8%
where the time goes in v2:
time: 172 us; the launch traced here: 171 us
  starting transfers between devices  72.2 us (42%)
  Pallas kernels  56.3 us (33%)
  blocking collectives  17.1 us (10%)
  waiting for transfers between devices  15 us (9%)
  other arithmetic  6.78 us (4%)
  local copies, waits for them, and re-layouts  3.07 us (2%)
    ppermute x8, starting transfers between devices, shifted(): return lax.ppermute(piece, axis, pairs)  58.7 us
    pallas_call x1, Pallas kernels, body(): pl.pallas_call(functools.partial(block_kernel, chunk), out_shape=(jax.Sha...  27.7 us
    all_to_all x1, blocking collectives, exchange(): lax.all_to_all(parts, ('lon', 'lat'), 0, 0, tiled=True, axis_index_groups...  17.1 us
    ppermute x8, waiting for transfers between devices, shifted(): return lax.ppermute(piece, axis, pairs)  15 us
    all_to_all x2, starting transfers between devices, exchange(): lax.all_to_all(parts, ('lon', 'lat'), 0, 0, tiled=True, axis_index_groups...  13.5 us
    pallas_call x1, Pallas kernels, body(): pl.pallas_call(back_kernel, out_shape=jax.ShapeDtypeStruct(cells.shape, j...  11.8 us
    pallas_call x1, Pallas kernels, body(): pl.pallas_call(tap_kernel, out_shape=jax.ShapeDtypeStruct((parts, 1024 //...  11.6 us
  transfers between devices with their start and end apart: 10, of which 5 were waited for; matrix products, arithmetic and copies ran while one was open for 2% of the time, Pallas kernels for 8%

profile of v2, /device:TPU:1, one launch (start us, length us, event | category | flops | bytes accessed | tf_op | source)
XLA Modules:
  0.0 171.2 jit_solution(8978001276973546569)
XLA Ops:
  0.6 0.8 convert_element_type.3
  1.4 2.7 %broadcast_multiply_fusion = (bf16[64,64,128]{2,1,0:T(8,128)(2,1)}, bf16[64,64,128]{2,1,0:T(8,128)(2,1)S(1)}) fusion(bf16[64,64,128]{2,1,0:T(8,128)(2,1)} %cot_ref.1, bf16[64,64]{1,0:T(8,128)(2,1)S(1)} %convert_element_type.3, bf16[64,64,128]{2,1,0:T(8,128)(2,1)} %param.10), kind=kLoop, calls=%fused_computation.2 | loop fusion | flops 1048576 | bytes 4202496 | tf_op jit(solution)/shard_map/mul | solution.py:275
  4.1 0.1 fusion.1
  4.1 16.3 %collective-permute-start = (bf16[64,3,128]{2,1,0:T(4,128)(2,1)S(1)}, bf16[64,3,128]{2,1,0:T(4,128)(2,1)S(1)}, u32[]{:S(2)}, u32[]{:S(2)}) collective-permute-start(bf16[64,3,128]{2,1,0:T(4,128)(2,1)S(1)} %get-tuple-element.42), channel_id=1, source_target_pairs={{0,16},{16,32},{32,48},{48,64},{64,80},{80,96},{96,112},{112,128},... | collective-permute-start | bytes 147464 | tf_op jit(solution)/shard_map/ppermute | solution.py:255
  20.4 6.6 %collective-permute-start.1 = (bf16[64,3,128]{2,1,0:T(4,128)(2,1)S(1)}, bf16[64,3,128]{2,1,0:T(4,128)(2,1)S(1)}, u32[]{:S(2)}, u32[]{:S(2)}) collective-permute-start(bf16[64,3,128]{2,1,0:T(4,128)(2,1)S(1)} %get-tuple-element.43), channel_id=1, source_target_pairs={{16,0},{32,16},{48,32},{64,48},{80,64},{96,80},{112,96},{128,112},... | collective-permute-start | bytes 147464 | tf_op jit(solution)/shard_map/ppermute | solution.py:255
  27.0 0.0 collective-permute-done
  27.0 7.2 %collective-permute-done.1 = bf16[64,3,128]{2,1,0:T(4,128)(2,1)S(1)} collective-permute-done((bf16[64,3,128]{2,1,0:T(4,128)(2,1)S(1)}, bf16[64,3,128]{2,1,0:T(4,128)(2,1)S(1)}, u32[]{:S(2)}, u32[]{:S(2)}) %collective-permute-start.1) | collective-permute-done | bytes 49184 | tf_op jit(solution)/shard_map/ppermute | solution.py:255
  34.2 6.5 %collective-permute-start.2 = (bf16[3,70,128]{2,1,0:T(8,128)(2,1)S(1)}, bf16[3,70,128]{2,1,0:T(8,128)(2,1)S(1)}, u32[]{:S(2)}, u32[]{:S(2)}) collective-permute-start(bf16[3,70,128]{2,1,0:T(8,128)(2,1)S(1)} %get-tuple-element.38), channel_id=1, source_target_pairs={{0,1},{1,2},{2,3},{3,4},{4,5},{5,6},{6,7},{7,8},{8,9},{9,10},{10,1... | collective-permute-start | bytes 161288 | tf_op jit(solution)/shard_map/ppermute | solution.py:255
  40.7 1.9 %collective-permute-start.3 = (bf16[3,70,128]{2,1,0:T(8,128)(2,1)S(1)}, bf16[3,70,128]{2,1,0:T(8,128)(2,1)S(1)}, u32[]{:S(2)}, u32[]{:S(2)}) collective-permute-start(bf16[3,70,128]{2,1,0:T(8,128)(2,1)S(1)} %get-tuple-element.39), channel_id=1, source_target_pairs={{1,0},{2,1},{3,2},{4,3},{5,4},{6,5},{7,6},{8,7},{9,8},{10,9},{11,1... | collective-permute-start | bytes 161288 | tf_op jit(solution)/shard_map/ppermute | solution.py:255
  42.6 0.0 collective-permute-done.2
  42.6 3.5 %collective-permute-done.3 = bf16[3,70,128]{2,1,0:T(8,128)(2,1)S(1)} collective-permute-done((bf16[3,70,128]{2,1,0:T(8,128)(2,1)S(1)}, bf16[3,70,128]{2,1,0:T(8,128)(2,1)S(1)}, u32[]{:S(2)}, u32[]{:S(2)}) %collective-permute-start.3) | collective-permute-done | bytes 53792 | tf_op jit(solution)/shard_map/ppermute | solution.py:255
  46.2 1.6 pad_maximum_fusion.padded_ref
  47.8 27.7 %block.1 = (bf16[64,64,128]{2,1,0:T(8,128)(2,1)}, f32[8,128]{1,0:T(8,128)}, f32[8,128]{1,0:T(8,128)}, f32[8,128]{1,0:T(8,128)}, f32[128,512]{1,0:T(8,128)}, /*index=5*/f32[8,512]{1,0:T(8,128)}, f32[512,128]{1,0:T(8,128)}) custom-call(bf16[70,70,128]{2,1,0:T(8,128)(2,1)} %pad_maximum_fusion.padded_ref, bf16[64,64,128]{2,1,0:T(8,128)(2,1)} %get-tuple-element.44.out_grad_ref, ...), custom_call_target="tpu_custom_call" | custom-call | tf_op jit(solution)/shard_map/block/pallas_call | solution.py:281
  75.5 11.6 %taps.1 = bf16[32,40,128]{2,1,0:T(8,128)(2,1)} custom-call(bf16[70,70,128]{2,1,0:T(8,128)(2,1)} %pad_maximum_fusion.padded_ref, bf16[64,64,128]{2,1,0:T(8,128)(2,1)} %get-tuple-element.22.grad_ref, f32[128,512]{1,0:T(8,128)} %get-tuple-element.23.grad_in_ref, f32[512,128]{1,0:T(8,128)} %get-tuple-element.24.grad_out_ref, ...), custom_call_target="tpu_custom_call" | custom-call | tf_op jit(solution)/shard_map/taps/pallas_call | solution.py:303
  87.1 0.0 copy-start
  87.1 17.1 %all_to_all.15.parts_ref = bf16[32,40,128]{2,1,0:T(8,128)(2,1)} all-to-all(bf16[32,40,128]{2,1,0:T(8,128)(2,1)} %taps.1), channel_id=1, replica_groups={{0,1,32,33,64,65,96,97,128,129,160,161,192,193,224,225,256,257,288,289,..., dimensions={0} | all-to-all | bytes 655360 | tf_op jit(solution)/shard_map/all_to_all | solution.py:213
  104.2 1.7 fold.2
  105.9 9.0 %all-to-all-start.1 = ((bf16[16,40,128]{2,1,0:T(8,128)(2,1)}), bf16[16,40,128]{2,1,0:T(8,128)(2,1)S(1)}, u32[]{:S(2)}, u32[]{:S(2)}) async-start(bf16[16,40,128]{2,1,0:T(8,128)(2,1)} %fold.2), calls=%async_computation.1 | async-start | bytes 327680 | tf_op jit(solution)/shard_map/all_to_all | solution.py:213
  114.9 0.0 copy-done
  114.9 0.1 fusion
  115.0 12.0 %collective-permute-start.4 = (bf16[64,3,128]{2,1,0:T(4,128)(2,1)S(1)}, bf16[64,3,128]{2,1,0:T(4,128)(2,1)S(1)}, u32[]{:S(2)}, u32[]{:S(2)}) collective-permute-start(bf16[64,3,128]{2,1,0:T(4,128)(2,1)S(1)} %get-tuple-element.40), channel_id=1, source_target_pairs={{0,16},{16,32},{32,48},{48,64},{64,80},{80,96},{96,112},{112,128},... | collective-permute-start | bytes 147464 | tf_op jit(solution)/shard_map/ppermute | solution.py:255
  127.0 6.2 %collective-permute-start.5 = (bf16[64,3,128]{2,1,0:T(4,128)(2,1)S(1)}, bf16[64,3,128]{2,1,0:T(4,128)(2,1)S(1)}, u32[]{:S(2)}, u32[]{:S(2)}) collective-permute-start(bf16[64,3,128]{2,1,0:T(4,128)(2,1)S(1)} %get-tuple-element.41), channel_id=1, source_target_pairs={{16,0},{32,16},{48,32},{64,48},{80,64},{96,80},{112,96},{128,112},... | collective-permute-start | bytes 147464 | tf_op jit(solution)/shard_map/ppermute | solution.py:255
  133.2 0.0 all-to-all-done.1.parts_ref
  133.2 0.0 copy-start.2
  133.2 0.7 copy-done.2
  133.9 1.7 fold.3
  135.6 4.5 %all-to-all-start.2 = ((bf16[32,40,128]{2,1,0:T(8,128)(2,1)}), bf16[32,40,128]{2,1,0:T(8,128)(2,1)S(1)}, u32[]{:S(2)}, u32[]{:S(2)}) async-start(bf16[32,40,128]{2,1,0:T(8,128)(2,1)} %fold.3), calls=%async_computation.2 | async-start | bytes 655360 | tf_op jit(solution)/shard_map/all_to_all | solution.py:213
  140.1 0.1 collective-permute-done.4
  140.2 0.6 collective-permute-done.5
  140.8 7.4 %collective-permute-start.6 = (bf16[3,70,128]{2,1,0:T(8,128)(2,1)S(1)}, bf16[3,70,128]{2,1,0:T(8,128)(2,1)S(1)}, u32[]{:S(2)}, u32[]{:S(2)}) collective-permute-start(bf16[3,70,128]{2,1,0:T(8,128)(2,1)S(1)} %get-tuple-element.36), channel_id=1, source_target_pairs={{0,1},{1,2},{2,3},{3,4},{4,5},{5,6},{6,7},{7,8},{8,9},{9,10},{10,1... | collective-permute-start | bytes 161288 | tf_op jit(solution)/shard_map/ppermute | solution.py:255
  148.2 1.9 %collective-permute-start.7 = (bf16[3,70,128]{2,1,0:T(8,128)(2,1)S(1)}, bf16[3,70,128]{2,1,0:T(8,128)(2,1)S(1)}, u32[]{:S(2)}, u32[]{:S(2)}) collective-permute-start(bf16[3,70,128]{2,1,0:T(8,128)(2,1)S(1)} %get-tuple-element.37), channel_id=1, source_target_pairs={{1,0},{2,1},{3,2},{4,3},{5,4},{6,5},{7,6},{8,7},{9,8},{10,9},{11,1... | collective-permute-start | bytes 161288 | tf_op jit(solution)/shard_map/ppermute | solution.py:255
  150.1 0.0 collective-permute-done.6
  150.1 3.5 %collective-permute-done.7 = bf16[3,70,128]{2,1,0:T(8,128)(2,1)S(1)} collective-permute-done((bf16[3,70,128]{2,1,0:T(8,128)(2,1)S(1)}, bf16[3,70,128]{2,1,0:T(8,128)(2,1)S(1)}, u32[]{:S(2)}, u32[]{:S(2)}) %collective-permute-start.7) | collective-permute-done | bytes 53792 | tf_op jit(solution)/shard_map/ppermute | solution.py:255
  153.7 1.6 pad_maximum_fusion.1.padded_ref
  155.3 1.6 broadcast_in_dim.2.mask_ref
  156.9 11.8 %back.1 = bf16[64,64,128]{2,1,0:T(8,128)(2,1)} custom-call(bf16[70,70,128]{2,1,0:T(8,128)(2,1)} %pad_maximum_fusion.1.padded_ref, bf16[64,64,128]{2,1,0:T(8,128)(2,1)} %cot_ref.1, bf16[64,64,128]{2,1,0:T(8,128)(2,1)} %broadcast_in_dim.2.mask_ref, f32[7,7,128]{2,1,0:T(8,128)} %kernel_ref.3), custom_call_target="tpu_custom_call" | custom-call | tf_op jit(solution)/shard_map/back/pallas_call | solution.py:315
  168.7 0.0 all-to-all-done.2.all_ref
  168.7 0.0 copy-start.1
  168.7 0.7 copy-done.1
  169.4 1.8 %unpack.1 = (f32[7,7,128]{2,1,0:T(8,128)}, f32[1,128]{1,0:T(1,128)}, f32[1,128]{1,0:T(1,128)}, f32[1,128]{1,0:T(1,128)}, f32[128,512]{1,0:T(8,128)}, /*index=5*/f32[1,512]{1,0:T(1,128)}, f32[512,128]{1,0:T(8,128)}) custom-call(bf16[32,40,128]{2,1,0:T(8,128)(2,1)} %copy-done.1), custom_call_target="tpu_custom_call" | custom-call | tf_op jit(solution)/shard_map/unpack/pallas_call | solution.py:324
  (2 shorter events, 0.1 us)
Async XLA Ops:
  4.1 22.8 %collective-permute-start = (bf16[64,3,128]{2,1,0:T(4,128)(2,1)S(1)}, bf16[64,3,128]{2,1,0:T(4,128)(2,1)S(1)}, u32[]{:S(2)}, u32[]{:S(2)}) collective-permute-start(bf16[64,3,128]{2,1,0:T(4,128)(2,1)S(1)} %get-tuple-element.42), channel_id=1, source_target_pairs={{0,16},{16,32},{32,48},{48,64},{64,80},{80,96},{96,112},{112,128},... | collective-permute-start | bytes 147464 | tf_op jit(solution)/shard_map/ppermute | solution.py:255
  20.4 13.7 %collective-permute-start.1 = (bf16[64,3,128]{2,1,0:T(4,128)(2,1)S(1)}, bf16[64,3,128]{2,1,0:T(4,128)(2,1)S(1)}, u32[]{:S(2)}, u32[]{:S(2)}) collective-permute-start(bf16[64,3,128]{2,1,0:T(4,128)(2,1)S(1)} %get-tuple-element.43), channel_id=1, source_target_pairs={{16,0},{32,16},{48,32},{64,48},{80,64},{96,80},{112,96},{128,112},... | collective-permute-start | bytes 147464 | tf_op jit(solution)/shard_map/ppermute | solution.py:255
  34.2 8.4 %collective-permute-start.2 = (bf16[3,70,128]{2,1,0:T(8,128)(2,1)S(1)}, bf16[3,70,128]{2,1,0:T(8,128)(2,1)S(1)}, u32[]{:S(2)}, u32[]{:S(2)}) collective-permute-start(bf16[3,70,128]{2,1,0:T(8,128)(2,1)S(1)} %get-tuple-element.38), channel_id=1, source_target_pairs={{0,1},{1,2},{2,3},{3,4},{4,5},{5,6},{6,7},{7,8},{8,9},{9,10},{10,1... | collective-permute-start | bytes 161288 | tf_op jit(solution)/shard_map/ppermute | solution.py:255
  40.7 5.5 %collective-permute-start.3 = (bf16[3,70,128]{2,1,0:T(8,128)(2,1)S(1)}, bf16[3,70,128]{2,1,0:T(8,128)(2,1)S(1)}, u32[]{:S(2)}, u32[]{:S(2)}) collective-permute-start(bf16[3,70,128]{2,1,0:T(8,128)(2,1)S(1)} %get-tuple-element.39), channel_id=1, source_target_pairs={{1,0},{2,1},{3,2},{4,3},{5,4},{6,5},{7,6},{8,7},{9,8},{10,9},{11,1... | collective-permute-start | bytes 161288 | tf_op jit(solution)/shard_map/ppermute | solution.py:255
  87.1 27.8 %copy-start = (bf16[64,64,128]{2,1,0:T(8,128)(2,1)S(1)}, bf16[64,64,128]{2,1,0:T(8,128)(2,1)}, u32[]{:S(2)}) copy-start(bf16[64,64,128]{2,1,0:T(8,128)(2,1)} %get-tuple-element.22.grad_ref) | copy-start | bytes 3145732
  105.9 27.3 %all-to-all-start.1 = ((bf16[16,40,128]{2,1,0:T(8,128)(2,1)}), bf16[16,40,128]{2,1,0:T(8,128)(2,1)S(1)}, u32[]{:S(2)}, u32[]{:S(2)}) async-start(bf16[16,40,128]{2,1,0:T(8,128)(2,1)} %fold.2), calls=%async_computation.1 | async-start | bytes 327680 | tf_op jit(solution)/shard_map/all_to_all | solution.py:213
  115.0 25.2 %collective-permute-start.4 = (bf16[64,3,128]{2,1,0:T(4,128)(2,1)S(1)}, bf16[64,3,128]{2,1,0:T(4,128)(2,1)S(1)}, u32[]{:S(2)}, u32[]{:S(2)}) collective-permute-start(bf16[64,3,128]{2,1,0:T(4,128)(2,1)S(1)} %get-tuple-element.40), channel_id=1, source_target_pairs={{0,16},{16,32},{32,48},{48,64},{64,80},{80,96},{96,112},{112,128},... | collective-permute-start | bytes 147464 | tf_op jit(solution)/shard_map/ppermute | solution.py:255
  127.0 13.8 %collective-permute-start.5 = (bf16[64,3,128]{2,1,0:T(4,128)(2,1)S(1)}, bf16[64,3,128]{2,1,0:T(4,128)(2,1)S(1)}, u32[]{:S(2)}, u32[]{:S(2)}) collective-permute-start(bf16[64,3,128]{2,1,0:T(4,128)(2,1)S(1)} %get-tuple-element.41), channel_id=1, source_target_pairs={{16,0},{32,16},{48,32},{64,48},{80,64},{96,80},{112,96},{128,112},... | collective-permute-start | bytes 147464 | tf_op jit(solution)/shard_map/ppermute | solution.py:255
  133.2 0.7 copy-start.2
  135.6 33.1 %all-to-all-start.2 = ((bf16[32,40,128]{2,1,0:T(8,128)(2,1)}), bf16[32,40,128]{2,1,0:T(8,128)(2,1)S(1)}, u32[]{:S(2)}, u32[]{:S(2)}) async-start(bf16[32,40,128]{2,1,0:T(8,128)(2,1)} %fold.3), calls=%async_computation.2 | async-start | bytes 655360 | tf_op jit(solution)/shard_map/all_to_all | solution.py:213
  140.8 9.3 %collective-permute-start.6 = (bf16[3,70,128]{2,1,0:T(8,128)(2,1)S(1)}, bf16[3,70,128]{2,1,0:T(8,128)(2,1)S(1)}, u32[]{:S(2)}, u32[]{:S(2)}) collective-permute-start(bf16[3,70,128]{2,1,0:T(8,128)(2,1)S(1)} %get-tuple-element.36), channel_id=1, source_target_pairs={{0,1},{1,2},{2,3},{3,4},{4,5},{5,6},{6,7},{7,8},{8,9},{9,10},{10,1... | collective-permute-start | bytes 161288 | tf_op jit(solution)/shard_map/ppermute | solution.py:255
  148.2 5.5 %collective-permute-start.7 = (bf16[3,70,128]{2,1,0:T(8,128)(2,1)S(1)}, bf16[3,70,128]{2,1,0:T(8,128)(2,1)S(1)}, u32[]{:S(2)}, u32[]{:S(2)}) collective-permute-start(bf16[3,70,128]{2,1,0:T(8,128)(2,1)S(1)} %get-tuple-element.37), channel_id=1, source_target_pairs={{1,0},{2,1},{3,2},{4,3},{5,4},{6,5},{7,6},{8,7},{9,8},{10,9},{11,1... | collective-permute-start | bytes 161288 | tf_op jit(solution)/shard_map/ppermute | solution.py:255
  168.7 0.7 copy-start.1

commit v3 on v2

v3 whole, which is shorter than its diff:
```python
import functools

import jax
import jax.numpy as jnp
from jax import lax
from jax.experimental import pallas as pl
from jax.experimental.pallas import tpu as pltpu
from jax.sharding import PartitionSpec as P

KS = 7
HALF = 3
SMALL = 64
WIDE = 14
SUB = 8
ROOT = 0.7978845608028654
CUBE = 0.044715
VMEM = pl.BlockSpec(memory_space=pltpu.VMEM)
PARAMS = pltpu.CompilerParams(vmem_limit_bytes=28 << 20)
SMEM = pl.BlockSpec(memory_space=pltpu.SMEM)


def spread_row(row_of, row, tiles_ref, buf_ref):
    buf_ref[HALF : HALF + 64, :] = row_of.astype(jnp.float32)
    for tap in range(WIDE):
        tiles_ref[pl.ds(row * (WIDE * SUB) + tap * SUB, SUB), :] = buf_ref[pl.ds(tap, SUB, stride=SUB), :]


def spread_all(south_ref, block_ref, north_ref, tiles_ref, buf_ref):
    height = block_ref.shape[0]
    buf_ref[...] = jnp.zeros_like(buf_ref)
    for row in range(HALF):
        spread_row(south_ref[row], row, tiles_ref, buf_ref)
        spread_row(north_ref[row], height + HALF + row, tiles_ref, buf_ref)

    def one(row, _):
        spread_row(block_ref[row], row + HALF, tiles_ref, buf_ref)
        return 0

    lax.fori_loop(0, height, one, 0)
    last = (height + 2 * HALF) * WIDE * SUB
    tiles_ref[last:, :] = jnp.zeros((2 * WIDE * SUB, 128), jnp.float32)


def tile(tiles_ref, row, t):
    return tiles_ref[pl.ds(row * (WIDE * SUB) + t * SUB, SUB), :]


def tap_weight(kernel_ref, a, b, flip):
    if flip:
        a, b = KS - 1 - a, KS - 1 - b
    return jnp.broadcast_to(kernel_ref[a, b : b + 1, :], (SUB, 128))


def conv_rows(tiles_ref, kernel_ref, out_ref, height, flip):
    def one(row, _):
        total = [None] * SUB
        for a in range(KS):
            cells = [tile(tiles_ref, row + a, t) for t in range(WIDE)]
            for b in range(KS):
                weight = tap_weight(kernel_ref, a, b, flip)
                for t in range(SUB):
                    term = weight * cells[t + b]
                    total[t] = term if total[t] is None else total[t] + term
        for t in range(SUB):
            out_ref[pl.ds(row * 64 + t * SUB, SUB), :] = total[t]
        return 0

    lax.fori_loop(0, height, one, 0)


def edge_columns(even, keep_ref, got_ref, cols_ref):
    for c in range(HALF):
        keep = keep_ref[c].astype(jnp.float32)
        got = got_ref[c].astype(jnp.float32)
        cols_ref[c] = jnp.where(even, got, keep)
        cols_ref[HALF + c] = jnp.where(even, keep, got)


def add_edges(cols_ref, kernel_ref, out_ref, height, flip):
    for west in (True, False):
        for at in range(HALF):
            t = at if west else SUB - HALF + at
            totals = [None] * (height // SUB)
            for a in range(KS):
                for b in range(KS):
                    c = t + b if west else t + b - SUB
                    if not ((0 <= c < HALF) if west else (HALF <= c < 2 * HALF)):
                        continue
                    weight = tap_weight(kernel_ref, a, b, flip)
                    for block in range(height // SUB):
                        term = weight * cols_ref[c, pl.ds(block * SUB + a, SUB), :]
                        totals[block] = term if totals[block] is None else totals[block] + term
            for block in range(height // SUB):
                place = pl.ds(block * SUB * 64 + t * SUB + (0 if west else SUB - 1), SUB, stride=64)
                out_ref[place, :] = out_ref[place, :] + totals[block]


def gather_row(tiles, buf_ref):
    for t in range(SUB):
        buf_ref[pl.ds(t, SUB, stride=SUB), :] = tiles[t]
    return buf_ref[0 : SUB * SUB, :]


def strip_kernel(even_ref, south_ref, block_ref, north_ref, out_ref, low_ref, high_ref):
    height = block_ref.shape[0]

    def put(at, row_of):
        low_ref[pl.ds(at * SUB, SUB), :] = row_of[0:SUB].astype(jnp.float32)
        high_ref[pl.ds(at * SUB, SUB), :] = row_of[64 - SUB : 64].astype(jnp.float32)

    for row in range(HALF):
        put(row, south_ref[row])
        put(row + height + HALF, north_ref[row])

    def one(step, _):
        for r in range(SUB):
            put(step * SUB + r + HALF, block_ref[step * SUB + r])
        return 0

    lax.fori_loop(0, height // SUB, one, 0)
    tall = height + 2 * HALF + 2
    low_ref[(tall - 2) * SUB :, :] = jnp.zeros((2 * SUB, 128), jnp.float32)
    high_ref[(tall - 2) * SUB :, :] = jnp.zeros((2 * SUB, 128), jnp.float32)
    even = even_ref[0] == 1
    for c in range(HALF):
        west = low_ref[pl.ds(c, tall, stride=SUB), :]
        east = high_ref[pl.ds(SUB - HALF + c, tall, stride=SUB), :]
        out_ref[0, c] = jnp.where(even, east, west).astype(jnp.bfloat16)
        out_ref[1, c] = jnp.where(even, west, east).astype(jnp.bfloat16)


def conv_kernel(flip, keep_tiles, south_ref, block_ref, north_ref, kernel_ref, out_ref, tiles_ref, buf_ref):
    del keep_tiles
    spread_all(south_ref, block_ref, north_ref, tiles_ref, buf_ref)
    conv_rows(tiles_ref, kernel_ref, out_ref, block_ref.shape[0], flip)


def block_kernel(
    chunk,
    even_ref, conv_in, tiles_in, keep_ref, got_ref, out_grad_ref,
    kernel_ref, bias_ref, gain_ref, shift_ref, w_in_ref, b_in_ref, w_out_ref,
    conv_ref, tiles_ref, conv_grad_ref, packed_ref,
    cols_ref, buf_ref, og_tiles, round_ref, taps_ref, small_ref,
    bias_sum, gain_sum, shift_sum, b_sum, grad_in, grad_out,
):
    del conv_in, tiles_in
    height = out_grad_ref.shape[0]
    cells = chunk * 64
    edge_columns(even_ref[0] == 1, keep_ref, got_ref, cols_ref)
    span = WIDE * SUB
    for c in range(HALF):
        for block in range((height + 2 * HALF + 2) // SUB):
            rows = pl.ds(block * SUB, SUB)
            start = block * SUB * span
            tiles_ref[pl.ds(start + c * SUB, SUB, stride=span), :] = cols_ref[c, rows, :]
            tiles_ref[pl.ds(start + (SUB + HALF + c) * SUB + SUB - 1, SUB, stride=span), :] = cols_ref[HALF + c, rows, :]
    add_edges(cols_ref, kernel_ref, conv_ref, height, False)
    for ref in (bias_sum, gain_sum, shift_sum, b_sum, grad_in, grad_out, taps_ref, round_ref):
        ref[...] = jnp.zeros_like(ref)
    bias = bias_ref[...]
    gain = gain_ref[...]
    shift = shift_ref[...]
    b_in = b_in_ref[...]

    def taps(first):
        for r in range(chunk):
            row = first + r
            grads = [round_ref[r * 64 + t * SUB : r * 64 + (t + 1) * SUB, :] for t in range(SUB)]
            for a in range(KS):
                near = [tile(tiles_ref, row + a, t) for t in range(WIDE)]
                for b in range(KS):
                    total = taps_ref[a, b]
                    for t in range(SUB):
                        total = total + grads[t] * near[t + b]
                    taps_ref[a, b] = total

    def one(step, _):
        first = step * chunk
        taps(jnp.maximum(first - chunk, 0))
        for r in range(chunk):
            buf_ref[0:64, :] = out_grad_ref[first + r].astype(jnp.float32)
            for t in range(SUB):
                og_tiles[r, t] = buf_ref[pl.ds(t, SUB, stride=SUB), :]
        conv = conv_ref[pl.ds(first * 64, cells), :] + bias
        out_grad = og_tiles[...].reshape(cells, 128).astype(jnp.bfloat16)
        average = jnp.mean(conv, axis=-1, keepdims=True)
        centred = conv - average
        variance = jnp.mean(centred * centred, axis=-1, keepdims=True)
        inverse = lax.rsqrt(variance + 1e-06)
        scaled = centred * inverse
        normed = (scaled * gain + shift).astype(jnp.bfloat16)
        v = jnp.dot(normed, w_in_ref[...], preferred_element_type=jnp.float32) + b_in
        act_grad = lax.dot_general(
            out_grad, w_out_ref[...], (((1,), (1,)), ((), ())), preferred_element_type=jnp.float32
        )
        square = v * v
        half = 0.5 + 0.5 * jnp.tanh(v * (ROOT + (ROOT * CUBE) * square))
        activation = (v * half).astype(jnp.bfloat16)
        slope = half + (half - half * half) * (v * (2 * ROOT + (6 * ROOT * CUBE) * square))
        hidden = (act_grad * slope).astype(jnp.bfloat16)
        grad_out[...] += lax.dot_general(
            out_grad, activation, (((0,), (0,)), ((), ())), preferred_element_type=jnp.float32
        )
        grad_in[...] += lax.dot_general(
            normed, hidden, (((0,), (0,)), ((), ())), preferred_element_type=jnp.float32
        )
        b_sum[...] += jnp.sum(hidden.astype(jnp.float32).reshape(cells // SUB, SUB, 512), axis=0)
        norm_grad = lax.dot_general(
            hidden, w_in_ref[...], (((1,), (1,)), ((), ())), preferred_element_type=jnp.float32
        )
        gain_sum[...] += jnp.sum((norm_grad * scaled).reshape(-1, SUB, 128), axis=0)
        shift_sum[...] += jnp.sum(norm_grad.reshape(-1, SUB, 128), axis=0)
        weighted = norm_grad * gain
        conv_grad = inverse * (
            weighted
            - jnp.mean(weighted, axis=-1, keepdims=True)
            - scaled * jnp.mean(weighted * scaled, axis=-1, keepdims=True)
        )
        rounded = conv_grad.astype(jnp.bfloat16).astype(jnp.float32)
        bias_sum[...] += jnp.sum(rounded.reshape(-1, SUB, 128), axis=0)
        round_ref[...] = rounded
        for r in range(chunk):
            natural = gather_row(
                [rounded[r * 64 + t * SUB : r * 64 + (t + 1) * SUB] for t in range(SUB)], buf_ref
            )
            conv_grad_ref[first + r] = natural.astype(jnp.bfloat16)
        return 0

    lax.fori_loop(0, height // chunk, one, 0)
    taps(height - chunk)
    pack(taps_ref, bias_sum, gain_sum, shift_sum, b_sum, grad_in, grad_out, packed_ref, small_ref)


def pack(taps_ref, bias_sum, gain_sum, shift_sum, b_sum, grad_in, grad_out, out_ref, small_ref):
    small_ref[...] = jnp.zeros_like(small_ref)
    for a in range(KS):
        for b in range(KS):
            small_ref[a * KS + b] = jnp.sum(taps_ref[a, b], axis=0)
    for at, ref in enumerate((bias_sum, gain_sum, shift_sum)):
        small_ref[KS * KS + at] = jnp.sum(ref[...], axis=0)
    for q in range(4):
        small_ref[KS * KS + 3 + q] = jnp.sum(b_sum[:, q * 128 : (q + 1) * 128], axis=0)
    parts = out_ref.shape[0]
    rows = 1024 // parts
    each = 128 // rows
    for at, ref in ((0, grad_in), (4, grad_out)):
        for q in range(4):
            block = ref[:, q * 128 : (q + 1) * 128].reshape(each, rows, 128)
            out_ref[(at + q) * each : (at + q + 1) * each, 0:rows, :] = block.astype(jnp.bfloat16)
    tail = small_ref[...].reshape(parts, SMALL // parts, 128)
    spare = out_ref.shape[1] - rows - SMALL // parts
    if spare:
        tail = jnp.concatenate([tail, jnp.zeros((parts, spare, 128), jnp.float32)], axis=1)
    out_ref[:, rows:, :] = tail.astype(jnp.bfloat16)


def back_kernel(even_ref, spread_in, keep_ref, got_ref, cot_ref, mask_ref, kernel_ref, spread_ref, out_ref, cols_ref, buf_ref):
    del spread_in
    height = cot_ref.shape[0]
    edge_columns(even_ref[0] == 1, keep_ref, got_ref, cols_ref)
    add_edges(cols_ref, kernel_ref, spread_ref, height, True)

    def one(row, _):
        spread = gather_row([spread_ref[pl.ds(row * 64 + t * SUB, SUB), :] for t in range(SUB)], buf_ref)
        out_ref[row] = (
            (cot_ref[row].astype(jnp.float32) + spread) * mask_ref[row].astype(jnp.float32)
        ).astype(jnp.bfloat16)
        return 0

    lax.fori_loop(0, height, one, 0)


def fold_kernel(parts_ref, out_ref):
    total = jnp.sum(parts_ref[...].astype(jnp.float32), axis=0).astype(jnp.bfloat16)
    out_ref[...] = jnp.broadcast_to(total[None], out_ref.shape)


def unpack_kernel(factor, all_ref, kernel_ref, bias_ref, gain_ref, shift_ref, in_ref, b_ref, out_ref):
    parts = all_ref.shape[0]
    rows = 1024 // parts
    each = 128 // rows
    for q in range(4):
        block = all_ref[q * each : (q + 1) * each, 0:rows, :].astype(jnp.float32)
        in_ref[:, q * 128 : (q + 1) * 128] = block.reshape(128, 128) * factor
    for q in range(4):
        block = all_ref[(4 + q) * each : (5 + q) * each, 0:rows, :].astype(jnp.float32)
        out_ref[q * 128 : (q + 1) * 128, :] = block.reshape(128, 128).T * factor
    small = all_ref[:, rows:, :].astype(jnp.float32) * factor

    def row(r):
        return small[r // (SMALL // parts), r % (SMALL // parts)]

    for a in range(KS):
        for b in range(KS):
            kernel_ref[a, b] = row(a * KS + b)
    for at, ref in enumerate((bias_ref, gain_ref, shift_ref)):
        ref[0] = row(KS * KS + at)
    for q in range(4):
        b_ref[0, q * 128 : (q + 1) * 128] = row(KS * KS + 3 + q)


def groups():
    count_lon, count_lat = lax.axis_size("lon"), lax.axis_size("lat")
    plane = [[[] for _ in range(count_lat // 2)] for _ in range(2)]
    column = [[[] for _ in range(2)] for _ in range(count_lon // 2)]
    for lon in range(count_lon):
        for lat in range(count_lat):
            at = lon * count_lat + lat
            plane[lon % 2][lat // 2].append(at)
            column[lon // 2][lat % 2].append(at)
    return [g for part in plane for g in part], [g for part in column for g in part]


def exchange(parts, members):
    return lax.all_to_all(parts, ("lon", "lat"), 0, 0, tiled=True, axis_index_groups=members)


def summed(packed):
    plane, column = groups()

    def fold(parts, count):
        return pl.pallas_call(
            fold_kernel,
            out_shape=jax.ShapeDtypeStruct((count,) + parts.shape[1:], jnp.bfloat16),
            in_specs=[VMEM],
            out_specs=VMEM,
            name="fold",
        compiler_params=PARAMS,
        )(parts)

    held = exchange(packed, plane)
    held = exchange(fold(held, len(column[0])), column)
    return exchange(fold(held, len(plane[0])), plane)


def lat_halo(block):
    count = lax.axis_size("lat")
    up = [(i, i + 1) for i in range(count - 1)]
    down = [(i + 1, i) for i in range(count - 1)]
    return lax.ppermute(block[-HALF:], "lat", up), lax.ppermute(block[:HALF], "lat", down)


def lon_halo(even, south, block, north):
    count = lax.axis_size("lon")
    tall = block.shape[0] + 2 * HALF + 2
    strips = pl.pallas_call(
        strip_kernel,
        out_shape=jax.ShapeDtypeStruct((2, HALF, tall, 128), jnp.bfloat16),
        in_specs=[SMEM, VMEM, VMEM, VMEM],
        out_specs=VMEM,
        scratch_shapes=[pltpu.VMEM((tall * SUB, 128), jnp.float32)] * 2,
        name="strips",
        compiler_params=PARAMS,
    )(even, south, block, north)
    swapped = lax.ppermute(strips, "lon", [(i, i ^ 1) for i in range(count)])
    onward = [(i, (i + 2) % count) for i in range(0, count, 2)] + [(i, (i - 2) % count) for i in range(1, count, 2)]
    return swapped[0], lax.ppermute(swapped[1], "lon", onward)


def first_conv(flip, south, block, north, kernel, keep_tiles):
    height, across, channels = block.shape
    tiles = (height + 2 * HALF + 2) * WIDE * SUB
    out = (pltpu.VMEM((height * across, channels), jnp.float32),)
    scratch = [pltpu.VMEM((SUB * SUB + 2 * SUB, channels), jnp.float32)]
    if keep_tiles:
        out = out + (pltpu.VMEM((tiles, channels), jnp.float32),)
    else:
        scratch = [pltpu.VMEM((tiles, channels), jnp.float32)] + scratch
    return pl.pallas_call(
        functools.partial(conv_kernel, flip, keep_tiles),
        out_shape=out,
        in_specs=[VMEM] * 4,
        out_specs=[VMEM] * len(out),
        scratch_shapes=scratch,
        name="back_conv" if flip else "conv",
        compiler_params=PARAMS,
    )(south, block, north, kernel)


def f32(*shape):
    return jax.ShapeDtypeStruct(shape, jnp.float32)


def body(cells, ocean_mask, cotangent, kernel, conv_bias, gain, shift, w_in, b_in, w_out, chunk=4):
    height, across, channels = cells.shape
    ocean = jnp.broadcast_to(ocean_mask.astype(jnp.bfloat16)[..., None], cells.shape)
    masked = cells * ocean
    out_grad = cotangent * ocean
    even = (1 - lax.axis_index("lon") % 2).astype(jnp.int32).reshape(1)
    south, north = lat_halo(masked)
    keep, got = lon_halo(even, south, masked, north)
    conv, tiles = first_conv(False, south, masked, north, kernel, True)
    parts = lax.axis_size("lon")
    hidden = w_in.shape[1]
    _, _, conv_grad, packed = pl.pallas_call(
        functools.partial(block_kernel, chunk),
        out_shape=(
            pltpu.VMEM(conv.shape, jnp.float32), pltpu.VMEM(tiles.shape, jnp.float32),
            jax.ShapeDtypeStruct(cells.shape, jnp.bfloat16),
            jax.ShapeDtypeStruct((parts, 1024 // parts + max(8, SMALL // parts), channels), jnp.bfloat16),
        ),
        in_specs=[SMEM] + [VMEM] * 12,
        out_specs=[VMEM] * 4,
        scratch_shapes=[
            pltpu.VMEM((2 * HALF, height + 2 * HALF + 2, channels), jnp.float32),
            pltpu.VMEM((80, channels), jnp.float32),
            pltpu.VMEM((chunk, SUB, SUB, channels), jnp.float32),
            pltpu.VMEM((chunk * 64, channels), jnp.float32),
            pltpu.VMEM((KS, KS, SUB, channels), jnp.float32),
            pltpu.VMEM((SMALL, channels), jnp.float32),
            pltpu.VMEM((SUB, channels), jnp.float32),
            pltpu.VMEM((SUB, channels), jnp.float32),
            pltpu.VMEM((SUB, channels), jnp.float32),
            pltpu.VMEM((SUB, hidden), jnp.float32),
            pltpu.VMEM((channels, hidden), jnp.float32),
            pltpu.VMEM((channels, hidden), jnp.float32),
        ],
        input_output_aliases={1: 0, 2: 1},
        name="block",
        compiler_params=PARAMS,
    )(
        even, *[pltpu.with_memory_space_constraint(x, pltpu.VMEM) for x in (conv, tiles)], keep, got, out_grad, kernel, conv_bias.reshape(1, -1), gain.reshape(1, -1),
        shift.reshape(1, -1), w_in, b_in.reshape(1, -1), w_out,
    )
    total = summed(packed)
    south, north = lat_halo(conv_grad)
    keep, got = lon_halo(even, south, conv_grad, north)
    (spread,) = first_conv(True, south, conv_grad, north, kernel, False)
    _, cells_grad = pl.pallas_call(
        back_kernel,
        out_shape=(pltpu.VMEM(spread.shape, jnp.float32), jax.ShapeDtypeStruct(cells.shape, jnp.bfloat16)),
        in_specs=[SMEM] + [VMEM] * 6,
        out_specs=[VMEM] * 2,
        scratch_shapes=[
            pltpu.VMEM((2 * HALF, height + 2 * HALF + 2, channels), jnp.float32),
            pltpu.VMEM((80, channels), jnp.float32),
        ],
        input_output_aliases={1: 0},
        name="back",
        compiler_params=PARAMS,
    )(even, pltpu.with_memory_space_constraint(spread, pltpu.VMEM), keep, got, cotangent, ocean, kernel)
    count = height * across * lax.axis_size("lon") * lax.axis_size("lat")
    gk, gb, gg, gs, gi, gh, go = pl.pallas_call(
        functools.partial(unpack_kernel, count ** -0.5),
        out_shape=(
            f32(KS, KS, channels), f32(1, channels), f32(1, channels), f32(1, channels),
            f32(channels, hidden), f32(1, hidden), f32(hidden, channels),
        ),
        in_specs=[VMEM],
        out_specs=[VMEM] * 7,
        name="unpack",
        compiler_params=PARAMS,
    )(total)
    return cells_grad, gk, gb[0], gg[0], gs[0], gi, gh[0], go


def solution(mesh):
    whole = P("lat", "lon", None)
    in_specs = (whole, P("lat", "lon"), whole) + (P(),) * 7
    out_specs = (whole,) + (P(),) * 7
    return jax.shard_map(body, mesh=mesh, in_specs=in_specs, out_specs=out_specs, check_vma=False)
```

time: 172 us -> 154 us (0.90)
  the two profiles are of different devices: /device:TPU:1 before, /device:TPU:33 now
where the time goes in v3:
time: 154 us; the launch traced here: 153 us
  starting transfers between devices  58.7 us (38%)
  Pallas kernels  50.2 us (33%)
  waiting for transfers between devices  23.6 us (15%)
  blocking collectives  16.3 us (11%)
  other arithmetic  2.68 us (2%)
    ppermute x2, starting transfers between devices, lon_halo(): swapped = lax.ppermute(strips, 'lon', [(i, i ^ 1) for i in range(count)])  23.9 us
    pallas_call x1, Pallas kernels, body(): pl.pallas_call(functools.partial(block_kernel, chunk), out_shape=(pltpu.V...  23.4 us
    pallas_call x2, Pallas kernels, first_conv(): pl.pallas_call(functools.partial(conv_kernel, flip, keep_tiles), out_shap...  21.7 us
    all_to_all x2, starting transfers between devices, exchange(): lax.all_to_all(parts, ('lon', 'lat'), 0, 0, tiled=True, axis_index_groups...  17.7 us
    all_to_all x1, blocking collectives, exchange(): lax.all_to_all(parts, ('lon', 'lat'), 0, 0, tiled=True, axis_index_groups...  16.3 us
    ppermute x2, waiting for transfers between devices, lon_halo(): swapped = lax.ppermute(strips, 'lon', [(i, i ^ 1) for i in range(count)])  15.8 us
    ppermute x2, starting transfers between devices, lat_halo(): lax.ppermute(block[-HALF:], 'lat', up)  7.89 us
    ppermute x2, waiting for transfers between devices, lat_halo(): lax.ppermute(block[:HALF], 'lat', down)  7.44 us
  transfers between devices with their start and end apart: 10, of which 5 were waited for; matrix products, arithmetic and copies ran while one was open for 0% of the time, Pallas kernels for 16%

profile of v3, /device:TPU:33, one launch (start us, length us, event | category | flops | bytes accessed | tf_op | source)
XLA Modules:
  0.0 153.1 jit_solution(11820828818825915740)
XLA Ops:
  0.6 0.8 convert_element_type.3
  1.4 0.0 copy-start.1
  1.4 1.9 %broadcast_multiply_fusion = (bf16[64,64,128]{2,1,0:T(8,128)(2,1)S(1)}, bf16[64,64,128]{2,1,0:T(8,128)(2,1)S(1)}) fusion(bf16[64,64,128]{2,1,0:T(8,128)(2,1)} %cot_ref.1, bf16[64,64]{1,0:T(8,128)(2,1)S(1)} %convert_element_type.3, bf16[64,64,128]{2,1,0:T(8,128)(2,1)} %param.10), kind=kLoop, calls=%fused_computation | loop fusion | flops 1048576 | bytes 4202496 | tf_op jit(solution)/shard_map/mul | solution.py:388
  3.3 0.0 copy-start.2
  3.3 0.0 copy-start.3
  3.4 0.0 copy-start.4
  3.4 0.0 copy-start.5
  3.4 0.0 copy-start.6
  3.4 0.0 copy-start.7
  3.4 4.2 %collective-permute-start = (bf16[3,64,128]{2,1,0:T(8,128)(2,1)S(1)}, bf16[3,64,128]{2,1,0:T(8,128)(2,1)S(1)}, u32[]{:S(2)}, u32[]{:S(2)}) collective-permute-start(bf16[3,64,128]{2,1,0:T(8,128)(2,1)S(1)} %get-tuple-element.35), channel_id=1, source_target_pairs={{0,1},{1,2},{2,3},{3,4},{4,5},{5,6},{6,7},{7,8},{8,9},{9,10},{10,1... | collective-permute-start | bytes 147464 | tf_op jit(solution)/shard_map/ppermute | solution.py:340
  7.7 1.9 %collective-permute-start.1 = (bf16[3,64,128]{2,1,0:T(8,128)(2,1)S(1)}, bf16[3,64,128]{2,1,0:T(8,128)(2,1)S(1)}, u32[]{:S(2)}, u32[]{:S(2)}) collective-permute-start(bf16[3,64,128]{2,1,0:T(8,128)(2,1)S(1)} %get-tuple-element.34), channel_id=1, source_target_pairs={{1,0},{2,1},{3,2},{4,3},{5,4},{6,5},{7,6},{8,7},{9,8},{10,9},{11,1... | collective-permute-start | bytes 147464 | tf_op jit(solution)/shard_map/ppermute | solution.py:340
  9.6 0.0 collective-permute-done.south_ref
  9.6 3.5 %collective-permute-done.1.north_ref = bf16[3,64,128]{2,1,0:T(8,128)(2,1)S(1)} collective-permute-done((bf16[3,64,128]{2,1,0:T(8,128)(2,1)S(1)}, bf16[3,64,128]{2,1,0:T(8,128)(2,1)S(1)}, u32[]{:S(2)}, u32[]{:S(2)}) %collective-permute-start.1) | collective-permute-done | bytes 49184 | tf_op jit(solution)/shard_map/ppermute | solution.py:340
  13.1 0.1 strips.2
  13.2 13.6 %collective-permute-start.2 = (bf16[2,3,72,128]{3,2,1,0:T(8,128)(2,1)S(1)}, bf16[2,3,72,128]{3,2,1,0:T(8,128)(2,1)S(1)}, u32[]{:S(2)}, u32[]{:S(2)}) collective-permute-start(bf16[2,3,72,128]{3,2,1,0:T(8,128)(2,1)S(1)} %strips.2), channel_id=1, source_target_pairs={{0,16},{16,0},{32,48},{48,32},{64,80},{80,64},{96,112},{112,96},{1... | collective-permute-start | bytes 331784 | tf_op jit(solution)/shard_map/ppermute | solution.py:355
  26.8 9.8 %collective-permute-done.2 = bf16[2,3,72,128]{3,2,1,0:T(8,128)(2,1)S(1)} collective-permute-done((bf16[2,3,72,128]{3,2,1,0:T(8,128)(2,1)S(1)}, bf16[2,3,72,128]{3,2,1,0:T(8,128)(2,1)S(1)}, u32[]{:S(2)}, u32[]{:S(2)}) %collective-permute-start.2) | collective-permute-done | bytes 110624 | tf_op jit(solution)/shard_map/ppermute | solution.py:355
  36.6 3.2 %collective-permute-start.3 = (bf16[3,72,128]{2,1,0:T(8,128)(2,1)S(1)}, bf16[3,72,128]{2,1,0:T(8,128)(2,1)S(1)}, u32[]{:S(2)}, u32[]{:S(2)}) collective-permute-start(bf16[3,72,128]{2,1,0:T(8,128)(2,1)S(1)} %get-tuple-element.38), channel_id=1, source_target_pairs={{0,32},{32,64},{64,96},{96,128},{128,160},{160,192},{192,224},{224... | collective-permute-start | bytes 165896 | tf_op jit(solution)/shard_map/ppermute | solution.py:357
  39.8 0.0 copy-done.1
  39.8 10.8 %conv.1 = (f32[4096,128]{1,0:T(8,128)S(1)}, f32[8064,128]{1,0:T(8,128)S(1)}) custom-call(bf16[3,64,128]{2,1,0:T(8,128)(2,1)S(1)} %collective-permute-done.south_ref, bf16[64,64,128]{2,1,0:T(8,128)(2,1)S(1)} %get-tuple-element.41.block_ref, bf16[3,64,128]{2,1,0:T(8,128)(2,1)S(1)} %collective-permute-done.1.north_ref, f32[7,7,128]{2,1,0:T(8,128)S(1)} %copy-done.1), custom_call_target="tpu_custom_call" | custom-call | tf_op jit(solution)/shard_map/conv/pallas_call | solution.py:369
  50.6 0.0 collective-permute-done.3.got_ref
  50.7 0.0 copy-done.2
  50.7 0.0 copy-done.3
  50.7 0.0 copy-done.4
  50.7 0.0 copy-done.5
  50.7 0.0 copy-done.6
  50.7 0.0 copy-done.7
  50.7 23.4 %block.1 = (f32[4096,128]{1,0:T(8,128)S(1)}, f32[8064,128]{1,0:T(8,128)S(1)}, bf16[64,64,128]{2,1,0:T(8,128)(2,1)S(1)}, bf16[32,40,128]{2,1,0:T(8,128)(2,1)S(1)}) custom-call(s32[1]{0:T(128)} %bitcast.even_ref, f32[4096,128]{1,0:T(8,128)S(1)} %get-tuple-element.20.conv_in, ...), custom_call_target="tpu_custom_call", output_to_operand_aliasing={{0}: (1, {}), {1}: (2, {})} | custom-call | tf_op jit(solution)/shard_map/block/pallas_call | solution.py:395
  74.1 16.3 %all_to_all.15.parts_ref = bf16[32,40,128]{2,1,0:T(8,128)(2,1)S(1)} all-to-all(bf16[32,40,128]{2,1,0:T(8,128)(2,1)S(1)} %get-tuple-element.24), channel_id=1, replica_groups={{0,1,32,33,64,65,96,97,128,129,160,161,192,193,224,225,256,257,288,289,..., dimensions={0} | all-to-all | bytes 655360 | tf_op jit(solution)/shard_map/all_to_all | solution.py:315
  90.5 0.7 fold.2
  91.2 12.6 %all-to-all-start.1 = ((bf16[16,40,128]{2,1,0:T(8,128)(2,1)}), bf16[16,40,128]{2,1,0:T(8,128)(2,1)S(1)}, u32[]{:S(2)}, u32[]{:S(2)}) async-start(bf16[16,40,128]{2,1,0:T(8,128)(2,1)} %fold.2), calls=%async_computation.1 | async-start | bytes 327680 | tf_op jit(solution)/shard_map/all_to_all | solution.py:315
  103.8 3.6 %collective-permute-start.4 = (bf16[3,64,128]{2,1,0:T(8,128)(2,1)S(1)}, bf16[3,64,128]{2,1,0:T(8,128)(2,1)S(1)}, u32[]{:S(2)}, u32[]{:S(2)}) collective-permute-start(bf16[3,64,128]{2,1,0:T(8,128)(2,1)S(1)} %get-tuple-element.33), channel_id=1, source_target_pairs={{0,1},{1,2},{2,3},{3,4},{4,5},{5,6},{6,7},{7,8},{8,9},{9,10},{10,1... | collective-permute-start | bytes 147464 | tf_op jit(solution)/shard_map/ppermute | solution.py:340
  107.5 1.9 %collective-permute-start.5 = (bf16[3,64,128]{2,1,0:T(8,128)(2,1)S(1)}, bf16[3,64,128]{2,1,0:T(8,128)(2,1)S(1)}, u32[]{:S(2)}, u32[]{:S(2)}) collective-permute-start(bf16[3,64,128]{2,1,0:T(8,128)(2,1)S(1)} %get-tuple-element.32), channel_id=1, source_target_pairs={{1,0},{2,1},{3,2},{4,3},{5,4},{6,5},{7,6},{8,7},{9,8},{10,9},{11,1... | collective-permute-start | bytes 147464 | tf_op jit(solution)/shard_map/ppermute | solution.py:340
  109.4 0.3 collective-permute-done.4.south_ref
  109.8 4.0 %collective-permute-done.5.north_ref = bf16[3,64,128]{2,1,0:T(8,128)(2,1)S(1)} collective-permute-done((bf16[3,64,128]{2,1,0:T(8,128)(2,1)S(1)}, bf16[3,64,128]{2,1,0:T(8,128)(2,1)S(1)}, u32[]{:S(2)}, u32[]{:S(2)}) %collective-permute-start.5) | collective-permute-done | bytes 49184 | tf_op jit(solution)/shard_map/ppermute | solution.py:340
  113.7 0.1 strips.3
  113.9 10.3 %collective-permute-start.6 = (bf16[2,3,72,128]{3,2,1,0:T(8,128)(2,1)S(1)}, bf16[2,3,72,128]{3,2,1,0:T(8,128)(2,1)S(1)}, u32[]{:S(2)}, u32[]{:S(2)}) collective-permute-start(bf16[2,3,72,128]{3,2,1,0:T(8,128)(2,1)S(1)} %strips.3), channel_id=1, source_target_pairs={{0,16},{16,0},{32,48},{48,32},{64,80},{80,64},{96,112},{112,96},{1... | collective-permute-start | bytes 331784 | tf_op jit(solution)/shard_map/ppermute | solution.py:355
  124.1 0.0 all-to-all-done.1.parts_ref
  124.1 0.8 fold.3
  124.9 5.1 %all-to-all-start.2 = ((bf16[32,40,128]{2,1,0:T(8,128)(2,1)}), bf16[32,40,128]{2,1,0:T(8,128)(2,1)S(1)}, u32[]{:S(2)}, u32[]{:S(2)}) async-start(bf16[32,40,128]{2,1,0:T(8,128)(2,1)} %fold.3), calls=%async_computation.2 | async-start | bytes 655360 | tf_op jit(solution)/shard_map/all_to_all | solution.py:315
  130.0 6.0 %collective-permute-done.6 = bf16[2,3,72,128]{3,2,1,0:T(8,128)(2,1)S(1)} collective-permute-done((bf16[2,3,72,128]{3,2,1,0:T(8,128)(2,1)S(1)}, bf16[2,3,72,128]{3,2,1,0:T(8,128)(2,1)S(1)}, u32[]{:S(2)}, u32[]{:S(2)}) %collective-permute-start.6) | collective-permute-done | bytes 110624 | tf_op jit(solution)/shard_map/ppermute | solution.py:355
  136.0 0.0 copy-start
  136.1 2.1 %collective-permute-start.7 = (bf16[3,72,128]{2,1,0:T(8,128)(2,1)S(1)}, bf16[3,72,128]{2,1,0:T(8,128)(2,1)S(1)}, u32[]{:S(2)}, u32[]{:S(2)}) collective-permute-start(bf16[3,72,128]{2,1,0:T(8,128)(2,1)S(1)} %get-tuple-element.36), channel_id=1, source_target_pairs={{0,32},{32,64},{64,96},{96,128},{128,160},{160,192},{192,224},{224... | collective-permute-start | bytes 165896 | tf_op jit(solution)/shard_map/ppermute | solution.py:357
  138.1 10.9 %back_conv.1.spread_in = f32[4096,128]{1,0:T(8,128)S(1)} custom-call(bf16[3,64,128]{2,1,0:T(8,128)(2,1)S(1)} %collective-permute-done.4.south_ref, bf16[64,64,128]{2,1,0:T(8,128)(2,1)S(1)} %get-tuple-element.22.block_ref, bf16[3,64,128]{2,1,0:T(8,128)(2,1)S(1)} %collective-permute-done.5.north_ref, f32[7,7,128]{2,1,0:T(8,128)S(1)} %copy-done.1), custom_call_target="tpu_custom_call" | custom-call | tf_op jit(solution)/shard_map/back_conv/pallas_call | solution.py:369
  149.0 0.0 collective-permute-done.7.got_ref
  149.0 0.6 broadcast_in_dim.2.mask_ref
  149.6 0.0 copy-done
  149.6 2.6 %back.1 = (f32[4096,128]{1,0:T(8,128)S(1)}, bf16[64,64,128]{2,1,0:T(8,128)(2,1)}) custom-call(s32[1]{0:T(128)} %bitcast.even_ref, f32[4096,128]{1,0:T(8,128)S(1)} %back_conv.1.spread_in, bf16[3,72,128]{2,1,0:T(8,128)(2,1)S(1)} %get-tuple-element.37.keep_ref, bf16[3,72,128]{2,1,0:T(8,128)(2,1)S(1)} %collective-permute-done.7.got_ref, ...), custom_call_target="tpu_custom_call", output_to_operand_aliasing={{0}: (1, {})} | custom-call | tf_op jit(solution)/shard_map/back/pallas_call | solution.py:429
  152.2 0.0 all-to-all-done.2.all_ref
  152.2 0.9 unpack.1
  (4 shorter events, 0.0 us)
Async XLA Ops:
  1.4 38.4 %copy-start.1 = (f32[7,7,128]{2,1,0:T(8,128)S(1)}, f32[7,7,128]{2,1,0:T(8,128)}, u32[]{:S(2)}) copy-start(f32[7,7,128]{2,1,0:T(8,128)} %kernel_ref.7) | copy-start | bytes 75268
  3.3 47.3 %copy-start.2 = (bf16[128,512]{1,0:T(8,128)(2,1)S(1)}, bf16[128,512]{1,0:T(8,128)(2,1)}, u32[]{:S(2)}) copy-start(bf16[128,512]{1,0:T(8,128)(2,1)} %w_in_ref.1) | copy-start | bytes 393220
  3.3 47.3 %copy-start.3 = (bf16[512,128]{1,0:T(8,128)(2,1)S(1)}, bf16[512,128]{1,0:T(8,128)(2,1)}, u32[]{:S(2)}) copy-start(bf16[512,128]{1,0:T(8,128)(2,1)} %w_out_ref.1) | copy-start | bytes 393220
  3.4 47.3 %copy-start.4 = (f32[512]{0:T(512)S(1)}, f32[512]{0:T(512)}, u32[]{:S(2)}) copy-start(f32[512]{0:T(512)} %param.18) | copy-start | bytes 6148
  3.4 47.3 %copy-start.5 = (f32[128]{0:T(128)S(1)}, f32[128]{0:T(128)}, u32[]{:S(2)}) copy-start(f32[128]{0:T(128)} %param.14) | copy-start | bytes 1540
  3.4 47.3 %copy-start.6 = (f32[128]{0:T(128)S(1)}, f32[128]{0:T(128)}, u32[]{:S(2)}) copy-start(f32[128]{0:T(128)} %param.15) | copy-start | bytes 1540
  3.4 47.3 %copy-start.7 = (f32[128]{0:T(128)S(1)}, f32[128]{0:T(128)}, u32[]{:S(2)}) copy-start(f32[128]{0:T(128)} %param.16) | copy-start | bytes 1540
  3.4 6.2 %collective-permute-start = (bf16[3,64,128]{2,1,0:T(8,128)(2,1)S(1)}, bf16[3,64,128]{2,1,0:T(8,128)(2,1)S(1)}, u32[]{:S(2)}, u32[]{:S(2)}) collective-permute-start(bf16[3,64,128]{2,1,0:T(8,128)(2,1)S(1)} %get-tuple-element.35), channel_id=1, source_target_pairs={{0,1},{1,2},{2,3},{3,4},{4,5},{5,6},{6,7},{7,8},{8,9},{9,10},{10,1... | collective-permute-start | bytes 147464 | tf_op jit(solution)/shard_map/ppermute | solution.py:340
  7.7 5.4 %collective-permute-start.1 = (bf16[3,64,128]{2,1,0:T(8,128)(2,1)S(1)}, bf16[3,64,128]{2,1,0:T(8,128)(2,1)S(1)}, u32[]{:S(2)}, u32[]{:S(2)}) collective-permute-start(bf16[3,64,128]{2,1,0:T(8,128)(2,1)S(1)} %get-tuple-element.34), channel_id=1, source_target_pairs={{1,0},{2,1},{3,2},{4,3},{5,4},{6,5},{7,6},{8,7},{9,8},{10,9},{11,1... | collective-permute-start | bytes 147464 | tf_op jit(solution)/shard_map/ppermute | solution.py:340
  13.2 23.4 %collective-permute-start.2 = (bf16[2,3,72,128]{3,2,1,0:T(8,128)(2,1)S(1)}, bf16[2,3,72,128]{3,2,1,0:T(8,128)(2,1)S(1)}, u32[]{:S(2)}, u32[]{:S(2)}) collective-permute-start(bf16[2,3,72,128]{3,2,1,0:T(8,128)(2,1)S(1)} %strips.2), channel_id=1, source_target_pairs={{0,16},{16,0},{32,48},{48,32},{64,80},{80,64},{96,112},{112,96},{1... | collective-permute-start | bytes 331784 | tf_op jit(solution)/shard_map/ppermute | solution.py:355
  36.6 14.0 %collective-permute-start.3 = (bf16[3,72,128]{2,1,0:T(8,128)(2,1)S(1)}, bf16[3,72,128]{2,1,0:T(8,128)(2,1)S(1)}, u32[]{:S(2)}, u32[]{:S(2)}) collective-permute-start(bf16[3,72,128]{2,1,0:T(8,128)(2,1)S(1)} %get-tuple-element.38), channel_id=1, source_target_pairs={{0,32},{32,64},{64,96},{96,128},{128,160},{160,192},{192,224},{224... | collective-permute-start | bytes 165896 | tf_op jit(solution)/shard_map/ppermute | solution.py:357
  91.2 32.9 %all-to-all-start.1 = ((bf16[16,40,128]{2,1,0:T(8,128)(2,1)}), bf16[16,40,128]{2,1,0:T(8,128)(2,1)S(1)}, u32[]{:S(2)}, u32[]{:S(2)}) async-start(bf16[16,40,128]{2,1,0:T(8,128)(2,1)} %fold.2), calls=%async_computation.1 | async-start | bytes 327680 | tf_op jit(solution)/shard_map/all_to_all | solution.py:315
  103.8 5.9 %collective-permute-start.4 = (bf16[3,64,128]{2,1,0:T(8,128)(2,1)S(1)}, bf16[3,64,128]{2,1,0:T(8,128)(2,1)S(1)}, u32[]{:S(2)}, u32[]{:S(2)}) collective-permute-start(bf16[3,64,128]{2,1,0:T(8,128)(2,1)S(1)} %get-tuple-element.33), channel_id=1, source_target_pairs={{0,1},{1,2},{2,3},{3,4},{4,5},{5,6},{6,7},{7,8},{8,9},{9,10},{10,1... | collective-permute-start | bytes 147464 | tf_op jit(solution)/shard_map/ppermute | solution.py:340
  107.5 6.2 %collective-permute-start.5 = (bf16[3,64,128]{2,1,0:T(8,128)(2,1)S(1)}, bf16[3,64,128]{2,1,0:T(8,128)(2,1)S(1)}, u32[]{:S(2)}, u32[]{:S(2)}) collective-permute-start(bf16[3,64,128]{2,1,0:T(8,128)(2,1)S(1)} %get-tuple-element.32), channel_id=1, source_target_pairs={{1,0},{2,1},{3,2},{4,3},{5,4},{6,5},{7,6},{8,7},{9,8},{10,9},{11,1... | collective-permute-start | bytes 147464 | tf_op jit(solution)/shard_map/ppermute | solution.py:340
  113.9 22.2 %collective-permute-start.6 = (bf16[2,3,72,128]{3,2,1,0:T(8,128)(2,1)S(1)}, bf16[2,3,72,128]{3,2,1,0:T(8,128)(2,1)S(1)}, u32[]{:S(2)}, u32[]{:S(2)}) collective-permute-start(bf16[2,3,72,128]{3,2,1,0:T(8,128)(2,1)S(1)} %strips.3), channel_id=1, source_target_pairs={{0,16},{16,0},{32,48},{48,32},{64,80},{80,64},{96,112},{112,96},{1... | collective-permute-start | bytes 331784 | tf_op jit(solution)/shard_map/ppermute | solution.py:355
  124.9 27.3 %all-to-all-start.2 = ((bf16[32,40,128]{2,1,0:T(8,128)(2,1)}), bf16[32,40,128]{2,1,0:T(8,128)(2,1)S(1)}, u32[]{:S(2)}, u32[]{:S(2)}) async-start(bf16[32,40,128]{2,1,0:T(8,128)(2,1)} %fold.3), calls=%async_computation.2 | async-start | bytes 655360 | tf_op jit(solution)/shard_map/all_to_all | solution.py:315
  136.0 13.6 %copy-start = (bf16[64,64,128]{2,1,0:T(8,128)(2,1)S(1)}, bf16[64,64,128]{2,1,0:T(8,128)(2,1)}, u32[]{:S(2)}) copy-start(bf16[64,64,128]{2,1,0:T(8,128)(2,1)} %cot_ref.1) | copy-start | bytes 3145732
  136.1 12.9 %collective-permute-start.7 = (bf16[3,72,128]{2,1,0:T(8,128)(2,1)S(1)}, bf16[3,72,128]{2,1,0:T(8,128)(2,1)S(1)}, u32[]{:S(2)}, u32[]{:S(2)}) collective-permute-start(bf16[3,72,128]{2,1,0:T(8,128)(2,1)S(1)} %get-tuple-element.36), channel_id=1, source_target_pairs={{0,32},{32,64},{64,96},{96,128},{128,160},{160,192},{192,224},{224... | collective-permute-start | bytes 165896 | tf_op jit(solution)/shard_map/ppermute | solution.py:357

commit v4 on v3

--- a/solution.py
+++ b/solution.py
@@ -6,6 +6,7 @@
 from jax.experimental import pallas as pl
 from jax.experimental.pallas import tpu as pltpu
 from jax.sharding import PartitionSpec as P
+
 
 KS = 7
 HALF = 3
@@ -141,7 +142,7 @@
     kernel_ref, bias_ref, gain_ref, shift_ref, w_in_ref, b_in_ref, w_out_ref,
     conv_ref, tiles_ref, conv_grad_ref, packed_ref,
     cols_ref, buf_ref, og_tiles, round_ref, taps_ref, small_ref,
-    bias_sum, gain_sum, shift_sum, b_sum, grad_in, grad_out,
+    bias_sum, gain_sum, shift_sum, grad_in, grad_out,
 ):
     del conv_in, tiles_in
     height = out_grad_ref.shape[0]
@@ -155,12 +156,17 @@
             tiles_ref[pl.ds(start + c * SUB, SUB, stride=span), :] = cols_ref[c, rows, :]
             tiles_ref[pl.ds(start + (SUB + HALF + c) * SUB + SUB - 1, SUB, stride=span), :] = cols_ref[HALF + c, rows, :]
     add_edges(cols_ref, kernel_ref, conv_ref, height, False)
-    for ref in (bias_sum, gain_sum, shift_sum, b_sum, grad_in, grad_out, taps_ref, round_ref):
+    for ref in (bias_sum, gain_sum, shift_sum, grad_in, grad_out, taps_ref):
         ref[...] = jnp.zeros_like(ref)
     bias = bias_ref[...]
     gain = gain_ref[...]
     shift = shift_ref[...]
     b_in = b_in_ref[...]
+    w_half = w_out_ref[...] * jnp.bfloat16(0.5)
+
+    ones = jnp.where(
+        lax.broadcasted_iota(jnp.int32, (16, cells), 0) == 0, 1.0, 0.0
+    ).astype(jnp.bfloat16)
 
     def taps(first):
         for r in range(chunk):
@@ -174,9 +180,10 @@
                         total = total + grads[t] * near[t + b]
                     taps_ref[a, b] = total
 
-    def one(step, _):
+    def one(step, pending):
         first = step * chunk
-        taps(jnp.maximum(first - chunk, 0))
+        if pending is not None:
+            taps(first - chunk)
         for r in range(chunk):
             buf_ref[0:64, :] = out_grad_ref[first + r].astype(jnp.float32)
             for t in range(SUB):
@@ -191,20 +198,20 @@
         normed = (scaled * gain + shift).astype(jnp.bfloat16)
         v = jnp.dot(normed, w_in_ref[...], preferred_element_type=jnp.float32) + b_in
         act_grad = lax.dot_general(
-            out_grad, w_out_ref[...], (((1,), (1,)), ((), ())), preferred_element_type=jnp.float32
+            out_grad, w_half, (((1,), (1,)), ((), ())), preferred_element_type=jnp.float32
         )
         square = v * v
-        half = 0.5 + 0.5 * jnp.tanh(v * (ROOT + (ROOT * CUBE) * square))
-        activation = (v * half).astype(jnp.bfloat16)
-        slope = half + (half - half * half) * (v * (2 * ROOT + (6 * ROOT * CUBE) * square))
-        hidden = (act_grad * slope).astype(jnp.bfloat16)
+        curve = jnp.tanh(v * (ROOT + (ROOT * CUBE) * square))
+        above = 1.0 + curve
+        twice = (v * above).astype(jnp.bfloat16)
+        rise = v * (ROOT + (3 * ROOT * CUBE) * square)
+        hidden = (act_grad * (above * (1.0 + (1.0 - curve) * rise))).astype(jnp.bfloat16)
         grad_out[...] += lax.dot_general(
-            out_grad, activation, (((0,), (0,)), ((), ())), preferred_element_type=jnp.float32
+            out_grad, twice, (((0,), (0,)), ((), ())), preferred_element_type=jnp.float32
         )
-        grad_in[...] += lax.dot_general(
-            normed, hidden, (((0,), (0,)), ((), ())), preferred_element_type=jnp.float32
+        grad_in[...] += jnp.dot(
+            jnp.concatenate([normed.T, ones], axis=0), hidden, preferred_element_type=jnp.float32
         )
-        b_sum[...] += jnp.sum(hidden.astype(jnp.float32).reshape(cells // SUB, SUB, 512), axis=0)
         norm_grad = lax.dot_general(
             hidden, w_in_ref[...], (((1,), (1,)), ((), ())), preferred_element_type=jnp.float32
         )
@@ -226,12 +233,13 @@
             conv_grad_ref[first + r] = natural.astype(jnp.bfloat16)
         return 0
 
-    lax.fori_loop(0, height // chunk, one, 0)
+    one(0, None)
+    lax.fori_loop(1, height // chunk, one, 0)
     taps(height - chunk)
-    pack(taps_ref, bias_sum, gain_sum, shift_sum, b_sum, grad_in, grad_out, packed_ref, small_ref)
-
-
-def pack(taps_ref, bias_sum, gain_sum, shift_sum, b_sum, grad_in, grad_out, out_ref, small_ref):
+    pack(taps_ref, bias_sum, gain_sum, shift_sum, grad_in, grad_out, packed_ref, small_ref)
+
+
+def pack(taps_ref, bias_sum, gain_sum, shift_sum, grad_in, grad_out, out_ref, small_ref):
     small_ref[...] = jnp.zeros_like(small_ref)
     for a in range(KS):
         for b in range(KS):
@@ -239,14 +247,14 @@
     for at, ref in enumerate((bias_sum, gain_sum, shift_sum)):
         small_ref[KS * KS + at] = jnp.sum(ref[...], axis=0)
     for q in range(4):
-        small_ref[KS * KS + 3 + q] = jnp.sum(b_sum[:, q * 128 : (q + 1) * 128], axis=0)
+        small_ref[KS * KS + 3 + q] = grad_in[128, q * 128 : (q + 1) * 128]
     parts = out_ref.shape[0]
     rows = 1024 // parts
     each = 128 // rows
-    for at, ref in ((0, grad_in), (4, grad_out)):
+    for at, ref, scale in ((0, grad_in, 1.0), (4, grad_out, 0.5)):
         for q in range(4):
-            block = ref[:, q * 128 : (q + 1) * 128].reshape(each, rows, 128)
-            out_ref[(at + q) * each : (at + q + 1) * each, 0:rows, :] = block.astype(jnp.bfloat16)
+            block = ref[0:128, q * 128 : (q + 1) * 128].reshape(each, rows, 128)
+            out_ref[(at + q) * each : (at + q + 1) * each, 0:rows, :] = (block * scale).astype(jnp.bfloat16)
     tail = small_ref[...].reshape(parts, SMALL // parts, 128)
     spare = out_ref.shape[1] - rows - SMALL // parts
     if spare:
@@ -329,15 +337,19 @@
         )(parts)
 
     held = exchange(packed, plane)
-    held = exchange(fold(held, len(column[0])), column)
-    return exchange(fold(held, len(plane[0])), plane)
+    held = fold(held, len(column[0]))
+    held = exchange(held, column)
+    held = fold(held, len(plane[0]))
+    return exchange(held, plane)
 
 
 def lat_halo(block):
     count = lax.axis_size("lat")
     up = [(i, i + 1) for i in range(count - 1)]
     down = [(i + 1, i) for i in range(count - 1)]
-    return lax.ppermute(block[-HALF:], "lat", up), lax.ppermute(block[:HALF], "lat", down)
+    south = lax.ppermute(block[-HALF:], "lat", up)
+    north = lax.ppermute(block[:HALF], "lat", down)
+    return south, north
 
 
 def lon_halo(even, south, block, north):
@@ -354,7 +366,8 @@
     )(even, south, block, north)
     swapped = lax.ppermute(strips, "lon", [(i, i ^ 1) for i in range(count)])
     onward = [(i, (i + 2) % count) for i in range(0, count, 2)] + [(i, (i - 2) % count) for i in range(1, count, 2)]
-    return swapped[0], lax.ppermute(swapped[1], "lon", onward)
+    got = lax.ppermute(swapped[1], "lon", onward)
+    return swapped[0], got
 
 
 def first_conv(flip, south, block, north, kernel, keep_tiles):
@@ -381,7 +394,7 @@
     return jax.ShapeDtypeStruct(shape, jnp.float32)
 
 
-def body(cells, ocean_mask, cotangent, kernel, conv_bias, gain, shift, w_in, b_in, w_out, chunk=4):
+def body(cells, ocean_mask, cotangent, kernel, conv_bias, gain, shift, w_in, b_in, w_out, chunk=8):
     height, across, channels = cells.shape
     ocean = jnp.broadcast_to(ocean_mask.astype(jnp.bfloat16)[..., None], cells.shape)
     masked = cells * ocean
@@ -411,8 +424,7 @@
             pltpu.VMEM((SUB, channels), jnp.float32),
             pltpu.VMEM((SUB, channels), jnp.float32),
             pltpu.VMEM((SUB, channels), jnp.float32),
-            pltpu.VMEM((SUB, hidden), jnp.float32),
-            pltpu.VMEM((channels, hidden), jnp.float32),
+            pltpu.VMEM((channels + 16, hidden), jnp.float32),
             pltpu.VMEM((channels, hidden), jnp.float32),
         ],
         input_output_aliases={1: 0, 2: 1},

time: 154 us -> 149 us (0.968)
  Pallas kernels: 50.2 us -> 45.7 us
    pallas_call x1, Pallas kernels: 23.4 us -> 18.9 us  [body(): pl.pallas_call(functools.partial(block_kernel, chunk), out_shape=(pltpu.V...]
  transfers between devices with their start and end apart: 10 -> 10, of which waited for: 5 -> 5; matrix products, arithmetic and copies ran while one was open for 0% -> 0% of each run, Pallas kernels for 16% -> 17%
where the time goes in v4:
time: 149 us
  starting transfers between devices  58.7 us (39%)
  Pallas kernels  45.7 us (31%)
  waiting for transfers between devices  23.6 us (16%)
  blocking collectives  16.3 us (11%)
  other arithmetic  2.68 us (2%)
    ppermute x2, starting transfers between devices, lon_halo(): swapped = lax.ppermute(strips, 'lon', [(i, i ^ 1) for i in range(count)])  23.9 us
    pallas_call x2, Pallas kernels, first_conv(): pl.pallas_call(functools.partial(conv_kernel, flip, keep_tiles), out_shap...  21.7 us
    pallas_call x1, Pallas kernels, body(): pl.pallas_call(functools.partial(block_kernel, chunk), out_shape=(pltpu.V...  18.9 us
    all_to_all x2, starting transfers between devices, exchange(): lax.all_to_all(parts, ('lon', 'lat'), 0, 0, tiled=True, axis_index_groups...  17.7 us
    all_to_all x1, blocking collectives, exchange(): lax.all_to_all(parts, ('lon', 'lat'), 0, 0, tiled=True, axis_index_groups...  16.3 us
    ppermute x2, waiting for transfers between devices, lon_halo(): swapped = lax.ppermute(strips, 'lon', [(i, i ^ 1) for i in range(count)])  15.8 us
    ppermute x2, starting transfers between devices, lat_halo(): south = lax.ppermute(block[-HALF:], 'lat', up)  7.89 us
    ppermute x2, waiting for transfers between devices, lat_halo(): north = lax.ppermute(block[:HALF], 'lat', down)  7.44 us
  transfers between devices with their start and end apart: 10, of which 5 were waited for; matrix products, arithmetic and copies ran while one was open for 0% of the time, Pallas kernels for 17%

profile of v4, /device:TPU:33, one launch (start us, length us, event | category | flops | bytes accessed | tf_op | source)
XLA Modules:
  0.0 148.6 jit_solution(17678919385693335779)
XLA Ops:
  0.6 0.8 convert_element_type.3
  1.4 0.0 copy-start.1
  1.4 1.9 %broadcast_multiply_fusion = (bf16[64,64,128]{2,1,0:T(8,128)(2,1)S(1)}, bf16[64,64,128]{2,1,0:T(8,128)(2,1)S(1)}) fusion(bf16[64,64,128]{2,1,0:T(8,128)(2,1)} %cot_ref.1, bf16[64,64]{1,0:T(8,128)(2,1)S(1)} %convert_element_type.3, bf16[64,64,128]{2,1,0:T(8,128)(2,1)} %param.10), kind=kLoop, calls=%fused_computation | loop fusion | flops 1048576 | bytes 4202496 | tf_op jit(solution)/shard_map/mul | solution.py:401
  3.3 0.0 copy-start.2
  3.3 0.0 copy-start.3
  3.4 0.0 copy-start.4
  3.4 0.0 copy-start.5
  3.4 0.0 copy-start.6
  3.4 0.0 copy-start.7
  3.4 4.2 %collective-permute-start = (bf16[3,64,128]{2,1,0:T(8,128)(2,1)S(1)}, bf16[3,64,128]{2,1,0:T(8,128)(2,1)S(1)}, u32[]{:S(2)}, u32[]{:S(2)}) collective-permute-start(bf16[3,64,128]{2,1,0:T(8,128)(2,1)S(1)} %get-tuple-element.35), channel_id=1, source_target_pairs={{0,1},{1,2},{2,3},{3,4},{4,5},{5,6},{6,7},{7,8},{8,9},{9,10},{10,1... | collective-permute-start | bytes 147464 | tf_op jit(solution)/shard_map/ppermute | solution.py:350
  7.7 1.9 %collective-permute-start.1 = (bf16[3,64,128]{2,1,0:T(8,128)(2,1)S(1)}, bf16[3,64,128]{2,1,0:T(8,128)(2,1)S(1)}, u32[]{:S(2)}, u32[]{:S(2)}) collective-permute-start(bf16[3,64,128]{2,1,0:T(8,128)(2,1)S(1)} %get-tuple-element.34), channel_id=1, source_target_pairs={{1,0},{2,1},{3,2},{4,3},{5,4},{6,5},{7,6},{8,7},{9,8},{10,9},{11,1... | collective-permute-start | bytes 147464 | tf_op jit(solution)/shard_map/ppermute | solution.py:351
  9.6 0.0 collective-permute-done.south_ref
  9.6 3.5 %collective-permute-done.1.north_ref = bf16[3,64,128]{2,1,0:T(8,128)(2,1)S(1)} collective-permute-done((bf16[3,64,128]{2,1,0:T(8,128)(2,1)S(1)}, bf16[3,64,128]{2,1,0:T(8,128)(2,1)S(1)}, u32[]{:S(2)}, u32[]{:S(2)}) %collective-permute-start.1) | collective-permute-done | bytes 49184 | tf_op jit(solution)/shard_map/ppermute | solution.py:351
  13.1 0.1 strips.2
  13.2 13.6 %collective-permute-start.2 = (bf16[2,3,72,128]{3,2,1,0:T(8,128)(2,1)S(1)}, bf16[2,3,72,128]{3,2,1,0:T(8,128)(2,1)S(1)}, u32[]{:S(2)}, u32[]{:S(2)}) collective-permute-start(bf16[2,3,72,128]{3,2,1,0:T(8,128)(2,1)S(1)} %strips.2), channel_id=1, source_target_pairs={{0,16},{16,0},{32,48},{48,32},{64,80},{80,64},{96,112},{112,96},{1... | collective-permute-start | bytes 331784 | tf_op jit(solution)/shard_map/ppermute | solution.py:367
  26.8 9.8 %collective-permute-done.2 = bf16[2,3,72,128]{3,2,1,0:T(8,128)(2,1)S(1)} collective-permute-done((bf16[2,3,72,128]{3,2,1,0:T(8,128)(2,1)S(1)}, bf16[2,3,72,128]{3,2,1,0:T(8,128)(2,1)S(1)}, u32[]{:S(2)}, u32[]{:S(2)}) %collective-permute-start.2) | collective-permute-done | bytes 110624 | tf_op jit(solution)/shard_map/ppermute | solution.py:367
  36.6 3.2 %collective-permute-start.3 = (bf16[3,72,128]{2,1,0:T(8,128)(2,1)S(1)}, bf16[3,72,128]{2,1,0:T(8,128)(2,1)S(1)}, u32[]{:S(2)}, u32[]{:S(2)}) collective-permute-start(bf16[3,72,128]{2,1,0:T(8,128)(2,1)S(1)} %get-tuple-element.38), channel_id=1, source_target_pairs={{0,32},{32,64},{64,96},{96,128},{128,160},{160,192},{192,224},{224... | collective-permute-start | bytes 165896 | tf_op jit(solution)/shard_map/ppermute | solution.py:369
  39.8 0.0 copy-done.1
  39.8 10.8 %conv.1 = (f32[4096,128]{1,0:T(8,128)S(1)}, f32[8064,128]{1,0:T(8,128)S(1)}) custom-call(bf16[3,64,128]{2,1,0:T(8,128)(2,1)S(1)} %collective-permute-done.south_ref, bf16[64,64,128]{2,1,0:T(8,128)(2,1)S(1)} %get-tuple-element.41.block_ref, bf16[3,64,128]{2,1,0:T(8,128)(2,1)S(1)} %collective-permute-done.1.north_ref, f32[7,7,128]{2,1,0:T(8,128)S(1)} %copy-done.1), custom_call_target="tpu_custom_call" | custom-call | tf_op jit(solution)/shard_map/conv/pallas_call | solution.py:382
  50.6 0.0 collective-permute-done.3.got_ref
  50.7 0.0 copy-done.2
  50.7 0.0 copy-done.3
  50.7 0.0 copy-done.4
  50.7 0.0 copy-done.5
  50.7 0.0 copy-done.6
  50.7 0.0 copy-done.7
  50.7 18.9 %block.1 = (f32[4096,128]{1,0:T(8,128)S(1)}, f32[8064,128]{1,0:T(8,128)S(1)}, bf16[64,64,128]{2,1,0:T(8,128)(2,1)S(1)}, bf16[32,40,128]{2,1,0:T(8,128)(2,1)S(1)}) custom-call(s32[1]{0:T(128)} %bitcast.even_ref, f32[4096,128]{1,0:T(8,128)S(1)} %get-tuple-element.20.conv_in, ...), custom_call_target="tpu_custom_call", output_to_operand_aliasing={{0}: (1, {}), {1}: (2, {})} | custom-call | tf_op jit(solution)/shard_map/block/pallas_call | solution.py:408
  69.6 16.3 %all_to_all.15.parts_ref = bf16[32,40,128]{2,1,0:T(8,128)(2,1)S(1)} all-to-all(bf16[32,40,128]{2,1,0:T(8,128)(2,1)S(1)} %get-tuple-element.24), channel_id=1, replica_groups={{0,1,32,33,64,65,96,97,128,129,160,161,192,193,224,225,256,257,288,289,..., dimensions={0} | all-to-all | bytes 655360 | tf_op jit(solution)/shard_map/all_to_all | solution.py:323
  86.0 0.7 fold.2
  86.7 12.6 %all-to-all-start.1 = ((bf16[16,40,128]{2,1,0:T(8,128)(2,1)}), bf16[16,40,128]{2,1,0:T(8,128)(2,1)S(1)}, u32[]{:S(2)}, u32[]{:S(2)}) async-start(bf16[16,40,128]{2,1,0:T(8,128)(2,1)} %fold.2), calls=%async_computation.1 | async-start | bytes 327680 | tf_op jit(solution)/shard_map/all_to_all | solution.py:323
  99.3 3.6 %collective-permute-start.4 = (bf16[3,64,128]{2,1,0:T(8,128)(2,1)S(1)}, bf16[3,64,128]{2,1,0:T(8,128)(2,1)S(1)}, u32[]{:S(2)}, u32[]{:S(2)}) collective-permute-start(bf16[3,64,128]{2,1,0:T(8,128)(2,1)S(1)} %get-tuple-element.33), channel_id=1, source_target_pairs={{0,1},{1,2},{2,3},{3,4},{4,5},{5,6},{6,7},{7,8},{8,9},{9,10},{10,1... | collective-permute-start | bytes 147464 | tf_op jit(solution)/shard_map/ppermute | solution.py:350
  103.0 1.9 %collective-permute-start.5 = (bf16[3,64,128]{2,1,0:T(8,128)(2,1)S(1)}, bf16[3,64,128]{2,1,0:T(8,128)(2,1)S(1)}, u32[]{:S(2)}, u32[]{:S(2)}) collective-permute-start(bf16[3,64,128]{2,1,0:T(8,128)(2,1)S(1)} %get-tuple-element.32), channel_id=1, source_target_pairs={{1,0},{2,1},{3,2},{4,3},{5,4},{6,5},{7,6},{8,7},{9,8},{10,9},{11,1... | collective-permute-start | bytes 147464 | tf_op jit(solution)/shard_map/ppermute | solution.py:351
  104.9 0.3 collective-permute-done.4.south_ref
  105.3 4.0 %collective-permute-done.5.north_ref = bf16[3,64,128]{2,1,0:T(8,128)(2,1)S(1)} collective-permute-done((bf16[3,64,128]{2,1,0:T(8,128)(2,1)S(1)}, bf16[3,64,128]{2,1,0:T(8,128)(2,1)S(1)}, u32[]{:S(2)}, u32[]{:S(2)}) %collective-permute-start.5) | collective-permute-done | bytes 49184 | tf_op jit(solution)/shard_map/ppermute | solution.py:351
  109.2 0.1 strips.3
  109.3 10.3 %collective-permute-start.6 = (bf16[2,3,72,128]{3,2,1,0:T(8,128)(2,1)S(1)}, bf16[2,3,72,128]{3,2,1,0:T(8,128)(2,1)S(1)}, u32[]{:S(2)}, u32[]{:S(2)}) collective-permute-start(bf16[2,3,72,128]{3,2,1,0:T(8,128)(2,1)S(1)} %strips.3), channel_id=1, source_target_pairs={{0,16},{16,0},{32,48},{48,32},{64,80},{80,64},{96,112},{112,96},{1... | collective-permute-start | bytes 331784 | tf_op jit(solution)/shard_map/ppermute | solution.py:367
  119.6 0.0 all-to-all-done.1.parts_ref
  119.6 0.8 fold.3
  120.4 5.1 %all-to-all-start.2 = ((bf16[32,40,128]{2,1,0:T(8,128)(2,1)}), bf16[32,40,128]{2,1,0:T(8,128)(2,1)S(1)}, u32[]{:S(2)}, u32[]{:S(2)}) async-start(bf16[32,40,128]{2,1,0:T(8,128)(2,1)} %fold.3), calls=%async_computation.2 | async-start | bytes 655360 | tf_op jit(solution)/shard_map/all_to_all | solution.py:323
  125.5 6.0 %collective-permute-done.6 = bf16[2,3,72,128]{3,2,1,0:T(8,128)(2,1)S(1)} collective-permute-done((bf16[2,3,72,128]{3,2,1,0:T(8,128)(2,1)S(1)}, bf16[2,3,72,128]{3,2,1,0:T(8,128)(2,1)S(1)}, u32[]{:S(2)}, u32[]{:S(2)}) %collective-permute-start.6) | collective-permute-done | bytes 110624 | tf_op jit(solution)/shard_map/ppermute | solution.py:367
  131.5 0.0 copy-start
  131.6 2.1 %collective-permute-start.7 = (bf16[3,72,128]{2,1,0:T(8,128)(2,1)S(1)}, bf16[3,72,128]{2,1,0:T(8,128)(2,1)S(1)}, u32[]{:S(2)}, u32[]{:S(2)}) collective-permute-start(bf16[3,72,128]{2,1,0:T(8,128)(2,1)S(1)} %get-tuple-element.36), channel_id=1, source_target_pairs={{0,32},{32,64},{64,96},{96,128},{128,160},{160,192},{192,224},{224... | collective-permute-start | bytes 165896 | tf_op jit(solution)/shard_map/ppermute | solution.py:369
  133.6 10.9 %back_conv.1.spread_in = f32[4096,128]{1,0:T(8,128)S(1)} custom-call(bf16[3,64,128]{2,1,0:T(8,128)(2,1)S(1)} %collective-permute-done.4.south_ref, bf16[64,64,128]{2,1,0:T(8,128)(2,1)S(1)} %get-tuple-element.22.block_ref, bf16[3,64,128]{2,1,0:T(8,128)(2,1)S(1)} %collective-permute-done.5.north_ref, f32[7,7,128]{2,1,0:T(8,128)S(1)} %copy-done.1), custom_call_target="tpu_custom_call" | custom-call | tf_op jit(solution)/shard_map/back_conv/pallas_call | solution.py:382
  144.5 0.0 collective-permute-done.7.got_ref
  144.5 0.6 broadcast_in_dim.2.mask_ref
  145.1 0.0 copy-done
  145.1 2.6 %back.1 = (f32[4096,128]{1,0:T(8,128)S(1)}, bf16[64,64,128]{2,1,0:T(8,128)(2,1)}) custom-call(s32[1]{0:T(128)} %bitcast.even_ref, f32[4096,128]{1,0:T(8,128)S(1)} %back_conv.1.spread_in, bf16[3,72,128]{2,1,0:T(8,128)(2,1)S(1)} %get-tuple-element.37.keep_ref, bf16[3,72,128]{2,1,0:T(8,128)(2,1)S(1)} %collective-permute-done.7.got_ref, ...), custom_call_target="tpu_custom_call", output_to_operand_aliasing={{0}: (1, {})} | custom-call | tf_op jit(solution)/shard_map/back/pallas_call | solution.py:441
  147.7 0.0 all-to-all-done.2.all_ref
  147.7 0.9 unpack.1
  (4 shorter events, 0.0 us)
Async XLA Ops:
  1.4 38.4 %copy-start.1 = (f32[7,7,128]{2,1,0:T(8,128)S(1)}, f32[7,7,128]{2,1,0:T(8,128)}, u32[]{:S(2)}) copy-start(f32[7,7,128]{2,1,0:T(8,128)} %kernel_ref.7) | copy-start | bytes 75268
  3.3 47.3 %copy-start.2 = (bf16[128,512]{1,0:T(8,128)(2,1)S(1)}, bf16[128,512]{1,0:T(8,128)(2,1)}, u32[]{:S(2)}) copy-start(bf16[128,512]{1,0:T(8,128)(2,1)} %w_in_ref.1) | copy-start | bytes 393220
  3.3 47.3 %copy-start.3 = (bf16[512,128]{1,0:T(8,128)(2,1)S(1)}, bf16[512,128]{1,0:T(8,128)(2,1)}, u32[]{:S(2)}) copy-start(bf16[512,128]{1,0:T(8,128)(2,1)} %w_out_ref.1) | copy-start | bytes 393220
  3.4 47.3 %copy-start.4 = (f32[512]{0:T(512)S(1)}, f32[512]{0:T(512)}, u32[]{:S(2)}) copy-start(f32[512]{0:T(512)} %param.18) | copy-start | bytes 6148
  3.4 47.3 %copy-start.5 = (f32[128]{0:T(128)S(1)}, f32[128]{0:T(128)}, u32[]{:S(2)}) copy-start(f32[128]{0:T(128)} %param.14) | copy-start | bytes 1540
  3.4 47.3 %copy-start.6 = (f32[128]{0:T(128)S(1)}, f32[128]{0:T(128)}, u32[]{:S(2)}) copy-start(f32[128]{0:T(128)} %param.15) | copy-start | bytes 1540
  3.4 47.3 %copy-start.7 = (f32[128]{0:T(128)S(1)}, f32[128]{0:T(128)}, u32[]{:S(2)}) copy-start(f32[128]{0:T(128)} %param.16) | copy-start | bytes 1540
  3.4 6.2 %collective-permute-start = (bf16[3,64,128]{2,1,0:T(8,128)(2,1)S(1)}, bf16[3,64,128]{2,1,0:T(8,128)(2,1)S(1)}, u32[]{:S(2)}, u32[]{:S(2)}) collective-permute-start(bf16[3,64,128]{2,1,0:T(8,128)(2,1)S(1)} %get-tuple-element.35), channel_id=1, source_target_pairs={{0,1},{1,2},{2,3},{3,4},{4,5},{5,6},{6,7},{7,8},{8,9},{9,10},{10,1... | collective-permute-start | bytes 147464 | tf_op jit(solution)/shard_map/ppermute | solution.py:350
  7.7 5.4 %collective-permute-start.1 = (bf16[3,64,128]{2,1,0:T(8,128)(2,1)S(1)}, bf16[3,64,128]{2,1,0:T(8,128)(2,1)S(1)}, u32[]{:S(2)}, u32[]{:S(2)}) collective-permute-start(bf16[3,64,128]{2,1,0:T(8,128)(2,1)S(1)} %get-tuple-element.34), channel_id=1, source_target_pairs={{1,0},{2,1},{3,2},{4,3},{5,4},{6,5},{7,6},{8,7},{9,8},{10,9},{11,1... | collective-permute-start | bytes 147464 | tf_op jit(solution)/shard_map/ppermute | solution.py:351
  13.2 23.4 %collective-permute-start.2 = (bf16[2,3,72,128]{3,2,1,0:T(8,128)(2,1)S(1)}, bf16[2,3,72,128]{3,2,1,0:T(8,128)(2,1)S(1)}, u32[]{:S(2)}, u32[]{:S(2)}) collective-permute-start(bf16[2,3,72,128]{3,2,1,0:T(8,128)(2,1)S(1)} %strips.2), channel_id=1, source_target_pairs={{0,16},{16,0},{32,48},{48,32},{64,80},{80,64},{96,112},{112,96},{1... | collective-permute-start | bytes 331784 | tf_op jit(solution)/shard_map/ppermute | solution.py:367
  36.6 14.0 %collective-permute-start.3 = (bf16[3,72,128]{2,1,0:T(8,128)(2,1)S(1)}, bf16[3,72,128]{2,1,0:T(8,128)(2,1)S(1)}, u32[]{:S(2)}, u32[]{:S(2)}) collective-permute-start(bf16[3,72,128]{2,1,0:T(8,128)(2,1)S(1)} %get-tuple-element.38), channel_id=1, source_target_pairs={{0,32},{32,64},{64,96},{96,128},{128,160},{160,192},{192,224},{224... | collective-permute-start | bytes 165896 | tf_op jit(solution)/shard_map/ppermute | solution.py:369
  86.7 32.9 %all-to-all-start.1 = ((bf16[16,40,128]{2,1,0:T(8,128)(2,1)}), bf16[16,40,128]{2,1,0:T(8,128)(2,1)S(1)}, u32[]{:S(2)}, u32[]{:S(2)}) async-start(bf16[16,40,128]{2,1,0:T(8,128)(2,1)} %fold.2), calls=%async_computation.1 | async-start | bytes 327680 | tf_op jit(solution)/shard_map/all_to_all | solution.py:323
  99.3 5.9 %collective-permute-start.4 = (bf16[3,64,128]{2,1,0:T(8,128)(2,1)S(1)}, bf16[3,64,128]{2,1,0:T(8,128)(2,1)S(1)}, u32[]{:S(2)}, u32[]{:S(2)}) collective-permute-start(bf16[3,64,128]{2,1,0:T(8,128)(2,1)S(1)} %get-tuple-element.33), channel_id=1, source_target_pairs={{0,1},{1,2},{2,3},{3,4},{4,5},{5,6},{6,7},{7,8},{8,9},{9,10},{10,1... | collective-permute-start | bytes 147464 | tf_op jit(solution)/shard_map/ppermute | solution.py:350
  103.0 6.2 %collective-permute-start.5 = (bf16[3,64,128]{2,1,0:T(8,128)(2,1)S(1)}, bf16[3,64,128]{2,1,0:T(8,128)(2,1)S(1)}, u32[]{:S(2)}, u32[]{:S(2)}) collective-permute-start(bf16[3,64,128]{2,1,0:T(8,128)(2,1)S(1)} %get-tuple-element.32), channel_id=1, source_target_pairs={{1,0},{2,1},{3,2},{4,3},{5,4},{6,5},{7,6},{8,7},{9,8},{10,9},{11,1... | collective-permute-start | bytes 147464 | tf_op jit(solution)/shard_map/ppermute | solution.py:351
  109.3 22.2 %collective-permute-start.6 = (bf16[2,3,72,128]{3,2,1,0:T(8,128)(2,1)S(1)}, bf16[2,3,72,128]{3,2,1,0:T(8,128)(2,1)S(1)}, u32[]{:S(2)}, u32[]{:S(2)}) collective-permute-start(bf16[2,3,72,128]{3,2,1,0:T(8,128)(2,1)S(1)} %strips.3), channel_id=1, source_target_pairs={{0,16},{16,0},{32,48},{48,32},{64,80},{80,64},{96,112},{112,96},{1... | collective-permute-start | bytes 331784 | tf_op jit(solution)/shard_map/ppermute | solution.py:367
  120.4 27.3 %all-to-all-start.2 = ((bf16[32,40,128]{2,1,0:T(8,128)(2,1)}), bf16[32,40,128]{2,1,0:T(8,128)(2,1)S(1)}, u32[]{:S(2)}, u32[]{:S(2)}) async-start(bf16[32,40,128]{2,1,0:T(8,128)(2,1)} %fold.3), calls=%async_computation.2 | async-start | bytes 655360 | tf_op jit(solution)/shard_map/all_to_all | solution.py:323
  131.5 13.6 %copy-start = (bf16[64,64,128]{2,1,0:T(8,128)(2,1)S(1)}, bf16[64,64,128]{2,1,0:T(8,128)(2,1)}, u32[]{:S(2)}) copy-start(bf16[64,64,128]{2,1,0:T(8,128)(2,1)} %cot_ref.1) | copy-start | bytes 3145732
  131.6 12.9 %collective-permute-start.7 = (bf16[3,72,128]{2,1,0:T(8,128)(2,1)S(1)}, bf16[3,72,128]{2,1,0:T(8,128)(2,1)S(1)}, u32[]{:S(2)}, u32[]{:S(2)}) collective-permute-start(bf16[3,72,128]{2,1,0:T(8,128)(2,1)S(1)} %get-tuple-element.36), channel_id=1, source_target_pairs={{0,32},{32,64},{64,96},{96,128},{128,160},{160,192},{192,224},{224... | collective-permute-start | bytes 165896 | tf_op jit(solution)/shard_map/ppermute | solution.py:369

commit v5 on v4

--- a/solution.py
+++ b/solution.py
@@ -12,6 +12,7 @@
 HALF = 3
 SMALL = 64
 WIDE = 14
+DEEP = 8
 SUB = 8
 ROOT = 0.7978845608028654
 CUBE = 0.044715
@@ -52,7 +53,7 @@
     return jnp.broadcast_to(kernel_ref[a, b : b + 1, :], (SUB, 128))
 
 
-def conv_rows(tiles_ref, kernel_ref, out_ref, height, flip):
+def conv_rows(tiles_ref, kernel_ref, out_ref, start, stop, flip):
     def one(row, _):
         total = [None] * SUB
         for a in range(KS):
@@ -66,7 +67,7 @@
             out_ref[pl.ds(row * 64 + t * SUB, SUB), :] = total[t]
         return 0
 
-    lax.fori_loop(0, height, one, 0)
+    lax.fori_loop(start, stop, one, 0)
 
 
 def edge_columns(even, keep_ref, got_ref, cols_ref):
@@ -77,14 +78,15 @@
         cols_ref[HALF + c] = jnp.where(even, keep, got)
 
 
-def add_edges(cols_ref, kernel_ref, out_ref, height, flip):
+def add_edges(cols_ref, kernel_ref, out_ref, height, flip, depth=SUB):
     for west in (True, False):
         for at in range(HALF):
-            t = at if west else SUB - HALF + at
+            across = 64 // depth
+            first = at * depth if west else (across - HALF + at) * depth + depth - 1
             totals = [None] * (height // SUB)
             for a in range(KS):
                 for b in range(KS):
-                    c = t + b if west else t + b - SUB
+                    c = at + b if west else at + b - HALF
                     if not ((0 <= c < HALF) if west else (HALF <= c < 2 * HALF)):
                         continue
                     weight = tap_weight(kernel_ref, a, b, flip)
@@ -92,7 +94,7 @@
                         term = weight * cols_ref[c, pl.ds(block * SUB + a, SUB), :]
                         totals[block] = term if totals[block] is None else totals[block] + term
             for block in range(height // SUB):
-                place = pl.ds(block * SUB * 64 + t * SUB + (0 if west else SUB - 1), SUB, stride=64)
+                place = pl.ds(block * SUB * 64 + first, SUB, stride=64)
                 out_ref[place, :] = out_ref[place, :] + totals[block]
 
 
@@ -100,6 +102,15 @@
     for t in range(SUB):
         buf_ref[pl.ds(t, SUB, stride=SUB), :] = tiles[t]
     return buf_ref[0 : SUB * SUB, :]
+
+
+def put_sides(low_ref, high_ref, out_ref, rows):
+    for c in range(HALF):
+        west = low_ref[pl.ds(c, rows, stride=SUB), :].astype(jnp.bfloat16)
+        east = high_ref[pl.ds(SUB - HALF + c, rows, stride=SUB), :].astype(jnp.bfloat16)
+        for member in range(2):
+            out_ref[member, 0, c] = west
+            out_ref[member, 1, c] = east
 
 
 def strip_kernel(even_ref, south_ref, block_ref, north_ref, out_ref, low_ref, high_ref):
@@ -130,10 +141,49 @@
         out_ref[1, c] = jnp.where(even, west, east).astype(jnp.bfloat16)
 
 
-def conv_kernel(flip, keep_tiles, south_ref, block_ref, north_ref, kernel_ref, out_ref, tiles_ref, buf_ref):
-    del keep_tiles
+def back_conv_kernel(south_ref, block_ref, north_ref, kernel_ref, out_ref, tiles_ref, buf_ref):
     spread_all(south_ref, block_ref, north_ref, tiles_ref, buf_ref)
-    conv_rows(tiles_ref, kernel_ref, out_ref, block_ref.shape[0], flip)
+    conv_rows(tiles_ref, kernel_ref, out_ref, 0, block_ref.shape[0], True)
+
+
+def side_kernel(block_ref, out_ref, low_ref, high_ref):
+    height = block_ref.shape[0]
+
+    def one(step, _):
+        for r in range(SUB):
+            row_of = block_ref[step * SUB + r]
+            at = pl.ds((step * SUB + r) * SUB, SUB)
+            low_ref[at, :] = row_of[0:SUB].astype(jnp.float32)
+            high_ref[at, :] = row_of[64 - SUB : 64].astype(jnp.float32)
+        return 0
+
+    lax.fori_loop(0, height // SUB, one, 0)
+    put_sides(low_ref, high_ref, out_ref, height)
+
+
+def tall_kernel(even_ref, body_ref, south_ref, north_ref, keep_ref, pass_ref, buf_ref):
+    height = body_ref.shape[3]
+    even = even_ref[0] == 1
+    buf_ref[...] = jnp.zeros_like(buf_ref)
+    for at, ref in enumerate((keep_ref, pass_ref)):
+        for c in range(HALF):
+            def pick(of_ref):
+                return jnp.where(even, of_ref[1, at, c].astype(jnp.float32), of_ref[0, 1 - at, c].astype(jnp.float32))
+
+            buf_ref[0:HALF, :] = pick(south_ref)
+            buf_ref[HALF : HALF + height, :] = pick(body_ref)
+            buf_ref[HALF + height : 2 * HALF + height, :] = pick(north_ref)
+            ref[c] = buf_ref[...].astype(jnp.bfloat16)
+
+
+def rest_kernel(start, conv_in, tiles_ref, kernel_ref, out_ref):
+    del conv_in
+    conv_rows(tiles_ref, kernel_ref, out_ref, start, out_ref.shape[0] // 64, False)
+
+
+def conv_kernel(rows, south_ref, block_ref, north_ref, kernel_ref, out_ref, tiles_ref, buf_ref):
+    spread_all(south_ref, block_ref, north_ref, tiles_ref, buf_ref)
+    conv_rows(tiles_ref, kernel_ref, out_ref, 0, rows, False)
 
 
 def block_kernel(
@@ -255,21 +305,24 @@
         for q in range(4):
             block = ref[0:128, q * 128 : (q + 1) * 128].reshape(each, rows, 128)
             out_ref[(at + q) * each : (at + q + 1) * each, 0:rows, :] = (block * scale).astype(jnp.bfloat16)
-    tail = small_ref[...].reshape(parts, SMALL // parts, 128)
-    spare = out_ref.shape[1] - rows - SMALL // parts
-    if spare:
-        tail = jnp.concatenate([tail, jnp.zeros((parts, spare, 128), jnp.float32)], axis=1)
-    out_ref[:, rows:, :] = tail.astype(jnp.bfloat16)
+    per = SMALL // parts
+    spare = out_ref.shape[1] - rows - 2 * per
+    small = small_ref[...].reshape(parts, per, 128)
+    high = small.astype(jnp.bfloat16).astype(jnp.float32)
+    pieces = [high, small - high] + ([jnp.zeros((parts, spare, 128), jnp.float32)] if spare else [])
+    out_ref[:, rows:, :] = jnp.concatenate(pieces, axis=1).astype(jnp.bfloat16)
 
 
 def back_kernel(even_ref, spread_in, keep_ref, got_ref, cot_ref, mask_ref, kernel_ref, spread_ref, out_ref, cols_ref, buf_ref):
     del spread_in
     height = cot_ref.shape[0]
     edge_columns(even_ref[0] == 1, keep_ref, got_ref, cols_ref)
-    add_edges(cols_ref, kernel_ref, spread_ref, height, True)
+    add_edges(cols_ref, kernel_ref, spread_ref, height, True, DEEP)
 
     def one(row, _):
-        spread = gather_row([spread_ref[pl.ds(row * 64 + t * SUB, SUB), :] for t in range(SUB)], buf_ref)
+        for t in range(64 // DEEP):
+            buf_ref[pl.ds(t, DEEP, stride=64 // DEEP), :] = spread_ref[pl.ds(row * 64 + t * DEEP, DEEP), :]
+        spread = buf_ref[0:64, :]
         out_ref[row] = (
             (cot_ref[row].astype(jnp.float32) + spread) * mask_ref[row].astype(jnp.float32)
         ).astype(jnp.bfloat16)
@@ -278,8 +331,14 @@
     lax.fori_loop(0, height, one, 0)
 
 
-def fold_kernel(parts_ref, out_ref):
-    total = jnp.sum(parts_ref[...].astype(jnp.float32), axis=0).astype(jnp.bfloat16)
+def fold_kernel(rows, per, parts_ref, out_ref):
+    total = jnp.sum(parts_ref[...].astype(jnp.float32), axis=0)
+    small = total[rows : rows + per] + total[rows + per : rows + 2 * per]
+    high = small.astype(jnp.bfloat16).astype(jnp.float32)
+    pieces = [total[0:rows], high, small - high]
+    if total.shape[0] > rows + 2 * per:
+        pieces.append(jnp.zeros((total.shape[0] - rows - 2 * per, 128), jnp.float32))
+    total = jnp.concatenate(pieces, axis=0).astype(jnp.bfloat16)
     out_ref[...] = jnp.broadcast_to(total[None], out_ref.shape)
 
 
@@ -293,7 +352,9 @@
     for q in range(4):
         block = all_ref[(4 + q) * each : (5 + q) * each, 0:rows, :].astype(jnp.float32)
         out_ref[q * 128 : (q + 1) * 128, :] = block.reshape(128, 128).T * factor
-    small = all_ref[:, rows:, :].astype(jnp.float32) * factor
+    per = SMALL // parts
+    both = all_ref[:, rows:, :].astype(jnp.float32)
+    small = (both[:, 0:per] + both[:, per : 2 * per]) * factor
 
     def row(r):
         return small[r // (SMALL // parts), r % (SMALL // parts)]
@@ -324,11 +385,12 @@
 
 
 def summed(packed):
+    count_lon = lax.axis_size("lon")
     plane, column = groups()
 
     def fold(parts, count):
         return pl.pallas_call(
-            fold_kernel,
+            functools.partial(fold_kernel, 1024 // count_lon, SMALL // count_lon),
             out_shape=jax.ShapeDtypeStruct((count,) + parts.shape[1:], jnp.bfloat16),
             in_specs=[VMEM],
             out_specs=VMEM,
@@ -343,17 +405,26 @@
     return exchange(held, plane)
 
 
-def lat_halo(block):
+def lat_halo(top, bottom):
     count = lax.axis_size("lat")
     up = [(i, i + 1) for i in range(count - 1)]
     down = [(i + 1, i) for i in range(count - 1)]
-    south = lax.ppermute(block[-HALF:], "lat", up)
-    north = lax.ppermute(block[:HALF], "lat", down)
+    south = lax.ppermute(top, "lat", up)
+    north = lax.ppermute(bottom, "lat", down)
     return south, north
 
 
+def swap(sides):
+    pairs = [[i, i + 1] for i in range(0, lax.axis_size("lon"), 2)]
+    return lax.all_to_all(sides, "lon", 0, 0, tiled=True, axis_index_groups=pairs)
+
+
+def onward_pairs():
+    count = lax.axis_size("lon")
+    return [(i, (i + 2) % count) for i in range(0, count, 2)] + [(i, (i - 2) % count) for i in range(1, count, 2)]
+
+
 def lon_halo(even, south, block, north):
-    count = lax.axis_size("lon")
     tall = block.shape[0] + 2 * HALF + 2
     strips = pl.pallas_call(
         strip_kernel,
@@ -364,29 +435,25 @@
         name="strips",
         compiler_params=PARAMS,
     )(even, south, block, north)
-    swapped = lax.ppermute(strips, "lon", [(i, i ^ 1) for i in range(count)])
-    onward = [(i, (i + 2) % count) for i in range(0, count, 2)] + [(i, (i - 2) % count) for i in range(1, count, 2)]
-    got = lax.ppermute(swapped[1], "lon", onward)
+    swapped = lax.ppermute(strips, "lon", [(i, i ^ 1) for i in range(lax.axis_size("lon"))])
+    got = lax.ppermute(swapped[1], "lon", onward_pairs())
     return swapped[0], got
 
 
-def first_conv(flip, south, block, north, kernel, keep_tiles):
+def first_conv(south, block, north, kernel, rows):
     height, across, channels = block.shape
     tiles = (height + 2 * HALF + 2) * WIDE * SUB
-    out = (pltpu.VMEM((height * across, channels), jnp.float32),)
-    scratch = [pltpu.VMEM((SUB * SUB + 2 * SUB, channels), jnp.float32)]
-    if keep_tiles:
-        out = out + (pltpu.VMEM((tiles, channels), jnp.float32),)
-    else:
-        scratch = [pltpu.VMEM((tiles, channels), jnp.float32)] + scratch
     return pl.pallas_call(
-        functools.partial(conv_kernel, flip, keep_tiles),
-        out_shape=out,
+        functools.partial(conv_kernel, rows),
+        out_shape=(
+            pltpu.VMEM((height * across, channels), jnp.float32),
+            pltpu.VMEM((tiles, channels), jnp.float32),
+        ),
         in_specs=[VMEM] * 4,
-        out_specs=[VMEM] * len(out),
-        scratch_shapes=scratch,
-        name="back_conv" if flip else "conv",
-        compiler_params=PARAMS,
+        out_specs=[VMEM] * 2,
+        scratch_shapes=[pltpu.VMEM((SUB * SUB + 2 * SUB, channels), jnp.float32)],
+        compiler_params=PARAMS,
+        name="conv",
     )(south, block, north, kernel)
 
 
@@ -400,9 +467,40 @@
     masked = cells * ocean
     out_grad = cotangent * ocean
     even = (1 - lax.axis_index("lon") % 2).astype(jnp.int32).reshape(1)
-    south, north = lat_halo(masked)
-    keep, got = lon_halo(even, south, masked, north)
-    conv, tiles = first_conv(False, south, masked, north, kernel, True)
+    south, north = lat_halo(cells[-HALF:] * ocean[-HALF:], cells[:HALF] * ocean[:HALF])
+    sides = pl.pallas_call(
+        side_kernel,
+        out_shape=jax.ShapeDtypeStruct((2, 2, HALF, height, channels), jnp.bfloat16),
+        in_specs=[VMEM],
+        out_specs=VMEM,
+        scratch_shapes=[pltpu.VMEM((height * SUB, channels), jnp.float32)] * 2,
+        compiler_params=PARAMS,
+        name="sides",
+    )(masked)
+    swapped = swap(sides)
+    corner_south, corner_north = lat_halo(swapped[..., -HALF:, :], swapped[..., :HALF, :])
+    tall = jax.ShapeDtypeStruct((HALF, height + 2 * HALF + 2, channels), jnp.bfloat16)
+    keep, onward = pl.pallas_call(
+        tall_kernel,
+        out_shape=(tall, tall),
+        in_specs=[SMEM] + [VMEM] * 3,
+        out_specs=[VMEM] * 2,
+        scratch_shapes=[pltpu.VMEM(tall.shape[1:], jnp.float32)],
+        compiler_params=PARAMS,
+        name="tall",
+    )(even, swapped, corner_south, corner_north)
+    got = lax.ppermute(onward, "lon", onward_pairs())
+    early = height * 3 // 4
+    conv, tiles = first_conv(south, masked, north, kernel, early)
+    conv = pl.pallas_call(
+        functools.partial(rest_kernel, early),
+        out_shape=pltpu.VMEM(conv.shape, jnp.float32),
+        in_specs=[VMEM] * 3,
+        out_specs=VMEM,
+        input_output_aliases={0: 0},
+        compiler_params=PARAMS,
+        name="rest",
+    )(*[pltpu.with_memory_space_constraint(x, pltpu.VMEM) for x in (conv, tiles)], kernel)
     parts = lax.axis_size("lon")
     hidden = w_in.shape[1]
     _, _, conv_grad, packed = pl.pallas_call(
@@ -410,7 +508,7 @@
         out_shape=(
             pltpu.VMEM(conv.shape, jnp.float32), pltpu.VMEM(tiles.shape, jnp.float32),
             jax.ShapeDtypeStruct(cells.shape, jnp.bfloat16),
-            jax.ShapeDtypeStruct((parts, 1024 // parts + max(8, SMALL // parts), channels), jnp.bfloat16),
+            jax.ShapeDtypeStruct((parts, 1024 // parts + max(8, 2 * SMALL // parts), channels), jnp.bfloat16),
         ),
         in_specs=[SMEM] + [VMEM] * 12,
         out_specs=[VMEM] * 4,
@@ -435,9 +533,20 @@
         shift.reshape(1, -1), w_in, b_in.reshape(1, -1), w_out,
     )
     total = summed(packed)
-    south, north = lat_halo(conv_grad)
+    south, north = lat_halo(conv_grad[-HALF:], conv_grad[:HALF])
     keep, got = lon_halo(even, south, conv_grad, north)
-    (spread,) = first_conv(True, south, conv_grad, north, kernel, False)
+    spread = pl.pallas_call(
+        back_conv_kernel,
+        out_shape=pltpu.VMEM((height * across, channels), jnp.float32),
+        in_specs=[VMEM] * 4,
+        out_specs=VMEM,
+        scratch_shapes=[
+            pltpu.VMEM(((height + 2 * HALF + 2) * WIDE * SUB, channels), jnp.float32),
+            pltpu.VMEM((SUB * SUB + 2 * SUB, channels), jnp.float32),
+        ],
+        compiler_params=PARAMS,
+        name="back_conv",
+    )(south, conv_grad, north, kernel)
     _, cells_grad = pl.pallas_call(
         back_kernel,
         out_shape=(pltpu.VMEM(spread.shape, jnp.float32), jax.ShapeDtypeStruct(cells.shape, jnp.bfloat16)),

time: 149 us -> 159 us (1.067)
  blocking collectives: 16.3 us -> 50.1 us
  starting transfers between devices: 58.7 us -> 43.4 us
  waiting for transfers between devices: 23.6 us -> 14.1 us
    all_to_all x0 -> x1, blocking collectives: none -> 32.5 us  [swap(): lax.all_to_all(sides, 'lon', 0, 0, tiled=True, axis_index_groups=pairs)]
    ppermute x8 -> x9, waiting for transfers between devices: 23.6 us -> 14.1 us  [the longest x3 7.72 us: lat_halo(): north = lax.ppermute(bottom, 'lat', down)]
    ppermute x8 -> x9, starting transfers between devices: 40.9 us -> 31.9 us  [the longest x1 10.3 us: lon_halo(): lax.ppermute(strips, 'lon', [(i, i ^ 1) for i in range(lax.axis_size('lon...]
    all_to_all x2, starting transfers between devices: 17.7 us -> 11.6 us  [exchange(): lax.all_to_all(parts, ('lon', 'lat'), 0, 0, tiled=True, axis_index_groups...]
    pallas_call x4 -> x7, Pallas kernels: 23.2 us -> 23.3 us  [the longest x1 10.9 us: body(): pl.pallas_call(back_conv_kernel, out_shape=pltpu.VMEM((height * across, c...]
  transfers between devices with their start and end apart: 10 -> 11, of which waited for: 5 -> 5; matrix products, arithmetic and copies ran while one was open for 0% -> 1% of each run, Pallas kernels for 17% -> 16%
where the time goes in v5:
time: 159 us
  blocking collectives  50.1 us (32%)
  Pallas kernels  45.9 us (29%)
  starting transfers between devices  43.4 us (27%)
  waiting for transfers between devices  14.1 us (9%)
  other arithmetic  3.61 us (2%)
    all_to_all x1, blocking collectives, swap(): lax.all_to_all(sides, 'lon', 0, 0, tiled=True, axis_index_groups=pairs)  32.5 us
    pallas_call x1, Pallas kernels, body(): pl.pallas_call(functools.partial(block_kernel, chunk), out_shape=(pltpu.V...  18.9 us
    all_to_all x1, blocking collectives, exchange(): lax.all_to_all(parts, ('lon', 'lat'), 0, 0, tiled=True, axis_index_groups...  17.6 us
    all_to_all x2, starting transfers between devices, exchange(): lax.all_to_all(parts, ('lon', 'lat'), 0, 0, tiled=True, axis_index_groups...  11.6 us
    pallas_call x1, Pallas kernels, body(): pl.pallas_call(back_conv_kernel, out_shape=pltpu.VMEM((height * across, c...  10.9 us
    ppermute x1, starting transfers between devices, lon_halo(): lax.ppermute(strips, 'lon', [(i, i ^ 1) for i in range(lax.axis_size('lon...  10.3 us
    ppermute x3, starting transfers between devices, lat_halo(): north = lax.ppermute(bottom, 'lat', down)  8.55 us
    pallas_call x1, Pallas kernels, first_conv(): pl.pallas_call(functools.partial(conv_kernel, rows), out_shape=(pltpu.VME...  8.43 us
  transfers between devices with their start and end apart: 11, of which 5 were waited for; matrix products, arithmetic and copies ran while one was open for 1% of the time, Pallas kernels for 16%

profile of v5, /device:TPU:33, one launch (start us, length us, event | category | flops | bytes accessed | tf_op | source)
XLA Modules:
  0.0 158.7 jit_solution(18230716261225149725)
XLA Ops:
  0.6 0.8 convert_element_type.3
  1.4 1.9 %broadcast_multiply_fusion = (bf16[64,64,128]{2,1,0:T(8,128)(2,1)S(1)}, bf16[64,64,128]{2,1,0:T(8,128)(2,1)S(1)}) fusion(bf16[64,64,128]{2,1,0:T(8,128)(2,1)} %cot_ref.1, bf16[64,64]{1,0:T(8,128)(2,1)S(1)} %convert_element_type.3, bf16[64,64,128]{2,1,0:T(8,128)(2,1)} %param.10), kind=kLoop, calls=%fused_computation | loop fusion | flops 1048576 | bytes 4202496 | tf_op jit(solution)/shard_map/mul | solution.py:468
  3.3 0.0 copy-start.1
  3.3 0.1 sides.1
  3.4 32.5 %all_to_all.20.body_ref = bf16[2,2,3,64,128]{4,3,2,1,0:T(8,128)(2,1)S(1)} all-to-all(bf16[2,2,3,64,128]{4,3,2,1,0:T(8,128)(2,1)S(1)} %sides.1), channel_id=1, replica_groups={{0,16},{32,48},{64,80},{96,112},{128,144},{160,176},{192,208},{224,240}..., dimensions={0} | all-to-all | bytes 393216 | tf_op jit(solution)/shard_map/all_to_all | solution.py:419
  35.9 1.9 %collective-permute-start.2 = (bf16[2,2,3,3,128]{4,3,2,1,0:T(4,128)(2,1)S(1)}, bf16[2,2,3,3,128]{4,3,2,1,0:T(4,128)(2,1)S(1)}, u32[]{:S(2)}, u32[]{:S(2)}) collective-permute-start(bf16[2,2,3,3,128]{4,3,2,1,0:T(4,128)(2,1)S(1)} %get-tuple-element.41), channel_id=1, source_target_pairs={{0,1},{1,2},{2,3},{3,4},{4,5},{5,6},{6,7},{7,8},{8,9},{9,10},{10,1... | collective-permute-start | bytes 27656 | tf_op jit(solution)/shard_map/ppermute | solution.py:412
  37.9 3.3 %collective-permute-start.3 = (bf16[2,2,3,3,128]{4,3,2,1,0:T(4,128)(2,1)S(1)}, bf16[2,2,3,3,128]{4,3,2,1,0:T(4,128)(2,1)S(1)}, u32[]{:S(2)}, u32[]{:S(2)}) collective-permute-start(bf16[2,2,3,3,128]{4,3,2,1,0:T(4,128)(2,1)S(1)} %get-tuple-element.40), channel_id=1, source_target_pairs={{1,0},{2,1},{3,2},{4,3},{5,4},{6,5},{7,6},{8,7},{9,8},{10,9},{11,1... | collective-permute-start | bytes 27656 | tf_op jit(solution)/shard_map/ppermute | solution.py:413
  41.2 0.0 collective-permute-done.2.south_ref
  41.2 1.7 %collective-permute-done.3.north_ref = bf16[2,2,3,3,128]{4,3,2,1,0:T(4,128)(2,1)S(1)} collective-permute-done((bf16[2,2,3,3,128]{4,3,2,1,0:T(4,128)(2,1)S(1)}, bf16[2,2,3,3,128]{4,3,2,1,0:T(4,128)(2,1)S(1)}, u32[]{:S(2)}, u32[]{:S(2)}) %collective-permute-start.3) | collective-permute-done | bytes 9248 | tf_op jit(solution)/shard_map/ppermute | solution.py:413
  42.9 0.1 tall.1
  42.9 3.2 %collective-permute-start.4 = (bf16[3,72,128]{2,1,0:T(8,128)(2,1)S(1)}, bf16[3,72,128]{2,1,0:T(8,128)(2,1)S(1)}, u32[]{:S(2)}, u32[]{:S(2)}) collective-permute-start(bf16[3,72,128]{2,1,0:T(8,128)(2,1)S(1)} %get-tuple-element.25), channel_id=1, source_target_pairs={{0,32},{32,64},{64,96},{96,128},{128,160},{160,192},{192,224},{224... | collective-permute-start | bytes 165896 | tf_op jit(solution)/shard_map/ppermute | solution.py:492
  46.2 0.9 slice_multiply_fusion
  47.1 2.2 %collective-permute-start = (bf16[3,64,128]{2,1,0:T(8,128)(2,1)S(1)}, bf16[3,64,128]{2,1,0:T(8,128)(2,1)S(1)}, u32[]{:S(2)}, u32[]{:S(2)}) collective-permute-start(bf16[3,64,128]{2,1,0:T(8,128)(2,1)S(1)} %get-tuple-element.39), channel_id=1, source_target_pairs={{0,1},{1,2},{2,3},{3,4},{4,5},{5,6},{6,7},{7,8},{8,9},{9,10},{10,1... | collective-permute-start | bytes 147464 | tf_op jit(solution)/shard_map/ppermute | solution.py:412
  49.3 3.3 %collective-permute-start.1 = (bf16[3,64,128]{2,1,0:T(8,128)(2,1)S(1)}, bf16[3,64,128]{2,1,0:T(8,128)(2,1)S(1)}, u32[]{:S(2)}, u32[]{:S(2)}) collective-permute-start(bf16[3,64,128]{2,1,0:T(8,128)(2,1)S(1)} %get-tuple-element.38), channel_id=1, source_target_pairs={{1,0},{2,1},{3,2},{4,3},{5,4},{6,5},{7,6},{8,7},{9,8},{10,9},{11,1... | collective-permute-start | bytes 147464 | tf_op jit(solution)/shard_map/ppermute | solution.py:413
  52.6 0.0 collective-permute-done.south_ref
  52.7 2.1 %collective-permute-done.1.north_ref = bf16[3,64,128]{2,1,0:T(8,128)(2,1)S(1)} collective-permute-done((bf16[3,64,128]{2,1,0:T(8,128)(2,1)S(1)}, bf16[3,64,128]{2,1,0:T(8,128)(2,1)S(1)}, u32[]{:S(2)}, u32[]{:S(2)}) %collective-permute-start.1) | collective-permute-done | bytes 49184 | tf_op jit(solution)/shard_map/ppermute | solution.py:413
  54.7 0.0 copy-done.1
  54.7 8.4 %conv.1 = (f32[4096,128]{1,0:T(8,128)S(1)}, f32[8064,128]{1,0:T(8,128)S(1)}) custom-call(bf16[3,64,128]{2,1,0:T(8,128)(2,1)S(1)} %collective-permute-done.south_ref, bf16[64,64,128]{2,1,0:T(8,128)(2,1)S(1)} %get-tuple-element.45.block_ref, bf16[3,64,128]{2,1,0:T(8,128)(2,1)S(1)} %collective-permute-done.1.north_ref, f32[7,7,128]{2,1,0:T(8,128)S(1)} %copy-done.1), custom_call_target="tpu_custom_call" | custom-call | tf_op jit(solution)/shard_map/conv/pallas_call | solution.py:446
  63.2 0.0 copy-start.2
  63.2 0.0 copy-start.3
  63.2 0.0 copy-start.4
  63.2 0.0 copy-start.5
  63.2 0.0 copy-start.6
  63.2 0.0 copy-start.7
  63.2 2.4 %rest.1.conv_in = f32[4096,128]{1,0:T(8,128)S(1)} custom-call(f32[4096,128]{1,0:T(8,128)S(1)} %get-tuple-element.22.conv_in, f32[8064,128]{1,0:T(8,128)S(1)} %get-tuple-element.23.tiles_ref.tiles_in, f32[7,7,128]{2,1,0:T(8,128)S(1)} %copy-done.1), custom_call_target="tpu_custom_call", output_to_operand_aliasing={{}: (0, {})} | custom-call | tf_op jit(solution)/shard_map/rest/pallas_call | solution.py:495
  65.6 0.0 collective-permute-done.4.got_ref
  65.6 0.0 copy-done.2
  65.6 0.0 copy-done.3
  65.7 0.0 copy-done.4
  65.7 0.0 copy-done.5
  65.7 0.0 copy-done.6
  65.7 0.0 copy-done.7
  65.7 18.9 %block.1 = (f32[4096,128]{1,0:T(8,128)S(1)}, f32[8064,128]{1,0:T(8,128)S(1)}, bf16[64,64,128]{2,1,0:T(8,128)(2,1)S(1)}, bf16[32,40,128]{2,1,0:T(8,128)(2,1)S(1)}) custom-call(s32[1]{0:T(128)} %bitcast.even_ref, f32[4096,128]{1,0:T(8,128)S(1)} %rest.1.conv_in, ...), custom_call_target="tpu_custom_call", output_to_operand_aliasing={{0}: (1, {}), {1}: (2, {})} | custom-call | tf_op jit(solution)/shard_map/block/pallas_call | solution.py:506
  84.6 17.6 %all_to_all.21.parts_ref = bf16[32,40,128]{2,1,0:T(8,128)(2,1)S(1)} all-to-all(bf16[32,40,128]{2,1,0:T(8,128)(2,1)S(1)} %get-tuple-element.28), channel_id=1, replica_groups={{0,1,32,33,64,65,96,97,128,129,160,161,192,193,224,225,256,257,288,289,..., dimensions={0} | all-to-all | bytes 655360 | tf_op jit(solution)/shard_map/all_to_all | solution.py:384
  102.2 0.7 fold.2
  102.9 6.5 %all-to-all-start.2 = ((bf16[16,40,128]{2,1,0:T(8,128)(2,1)}), bf16[16,40,128]{2,1,0:T(8,128)(2,1)S(1)}, u32[]{:S(2)}, u32[]{:S(2)}) async-start(bf16[16,40,128]{2,1,0:T(8,128)(2,1)} %fold.2), calls=%async_computation.2 | async-start | bytes 327680 | tf_op jit(solution)/shard_map/all_to_all | solution.py:384
  109.4 3.6 %collective-permute-start.5 = (bf16[3,64,128]{2,1,0:T(8,128)(2,1)S(1)}, bf16[3,64,128]{2,1,0:T(8,128)(2,1)S(1)}, u32[]{:S(2)}, u32[]{:S(2)}) collective-permute-start(bf16[3,64,128]{2,1,0:T(8,128)(2,1)S(1)} %get-tuple-element.37), channel_id=1, source_target_pairs={{0,1},{1,2},{2,3},{3,4},{4,5},{5,6},{6,7},{7,8},{8,9},{9,10},{10,1... | collective-permute-start | bytes 147464 | tf_op jit(solution)/shard_map/ppermute | solution.py:412
  113.1 1.9 %collective-permute-start.6 = (bf16[3,64,128]{2,1,0:T(8,128)(2,1)S(1)}, bf16[3,64,128]{2,1,0:T(8,128)(2,1)S(1)}, u32[]{:S(2)}, u32[]{:S(2)}) collective-permute-start(bf16[3,64,128]{2,1,0:T(8,128)(2,1)S(1)} %get-tuple-element.36), channel_id=1, source_target_pairs={{1,0},{2,1},{3,2},{4,3},{5,4},{6,5},{7,6},{8,7},{9,8},{10,9},{11,1... | collective-permute-start | bytes 147464 | tf_op jit(solution)/shard_map/ppermute | solution.py:413
  115.0 0.3 collective-permute-done.5.south_ref
  115.3 4.0 %collective-permute-done.6.north_ref = bf16[3,64,128]{2,1,0:T(8,128)(2,1)S(1)} collective-permute-done((bf16[3,64,128]{2,1,0:T(8,128)(2,1)S(1)}, bf16[3,64,128]{2,1,0:T(8,128)(2,1)S(1)}, u32[]{:S(2)}, u32[]{:S(2)}) %collective-permute-start.6) | collective-permute-done | bytes 49184 | tf_op jit(solution)/shard_map/ppermute | solution.py:413
  119.3 0.1 strips.1
  119.4 10.3 %collective-permute-start.7 = (bf16[2,3,72,128]{3,2,1,0:T(8,128)(2,1)S(1)}, bf16[2,3,72,128]{3,2,1,0:T(8,128)(2,1)S(1)}, u32[]{:S(2)}, u32[]{:S(2)}) collective-permute-start(bf16[2,3,72,128]{3,2,1,0:T(8,128)(2,1)S(1)} %strips.1), channel_id=1, source_target_pairs={{0,16},{16,0},{32,48},{48,32},{64,80},{80,64},{96,112},{112,96},{1... | collective-permute-start | bytes 331784 | tf_op jit(solution)/shard_map/ppermute | solution.py:438
  129.7 0.0 all-to-all-done.2.parts_ref
  129.7 0.8 fold.3
  130.5 5.1 %all-to-all-start.3 = ((bf16[32,40,128]{2,1,0:T(8,128)(2,1)}), bf16[32,40,128]{2,1,0:T(8,128)(2,1)S(1)}, u32[]{:S(2)}, u32[]{:S(2)}) async-start(bf16[32,40,128]{2,1,0:T(8,128)(2,1)} %fold.3), calls=%async_computation.3 | async-start | bytes 655360 | tf_op jit(solution)/shard_map/all_to_all | solution.py:384
  135.6 6.0 %collective-permute-done.7 = bf16[2,3,72,128]{3,2,1,0:T(8,128)(2,1)S(1)} collective-permute-done((bf16[2,3,72,128]{3,2,1,0:T(8,128)(2,1)S(1)}, bf16[2,3,72,128]{3,2,1,0:T(8,128)(2,1)S(1)}, u32[]{:S(2)}, u32[]{:S(2)}) %collective-permute-start.7) | collective-permute-done | bytes 110624 | tf_op jit(solution)/shard_map/ppermute | solution.py:438
  141.6 0.0 copy-start
  141.6 2.1 %collective-permute-start.8 = (bf16[3,72,128]{2,1,0:T(8,128)(2,1)S(1)}, bf16[3,72,128]{2,1,0:T(8,128)(2,1)S(1)}, u32[]{:S(2)}, u32[]{:S(2)}) collective-permute-start(bf16[3,72,128]{2,1,0:T(8,128)(2,1)S(1)} %get-tuple-element.42), channel_id=1, source_target_pairs={{0,32},{32,64},{64,96},{96,128},{128,160},{160,192},{192,224},{224... | collective-permute-start | bytes 165896 | tf_op jit(solution)/shard_map/ppermute | solution.py:439
  143.7 10.9 %back_conv.1.spread_in = f32[4096,128]{1,0:T(8,128)S(1)} custom-call(bf16[3,64,128]{2,1,0:T(8,128)(2,1)S(1)} %collective-permute-done.5.south_ref, bf16[64,64,128]{2,1,0:T(8,128)(2,1)S(1)} %get-tuple-element.26.block_ref, bf16[3,64,128]{2,1,0:T(8,128)(2,1)S(1)} %collective-permute-done.6.north_ref, f32[7,7,128]{2,1,0:T(8,128)S(1)} %copy-done.1), custom_call_target="tpu_custom_call" | custom-call | tf_op jit(solution)/shard_map/back_conv/pallas_call | solution.py:538
  154.6 0.0 collective-permute-done.8.got_ref
  154.6 0.6 broadcast_in_dim.11.mask_ref
  155.2 0.0 copy-done
  155.2 2.6 %back.1 = (f32[4096,128]{1,0:T(8,128)S(1)}, bf16[64,64,128]{2,1,0:T(8,128)(2,1)}) custom-call(s32[1]{0:T(128)} %bitcast.even_ref, f32[4096,128]{1,0:T(8,128)S(1)} %back_conv.1.spread_in, bf16[3,72,128]{2,1,0:T(8,128)(2,1)S(1)} %get-tuple-element.43.keep_ref, bf16[3,72,128]{2,1,0:T(8,128)(2,1)S(1)} %collective-permute-done.8.got_ref, ...), custom_call_target="tpu_custom_call", output_to_operand_aliasing={{0}: (1, {})} | custom-call | tf_op jit(solution)/shard_map/back/pallas_call | solution.py:550
  157.8 0.0 all-to-all-done.3.all_ref
  157.8 0.9 unpack.1
  (4 shorter events, 0.0 us)
Async XLA Ops:
  3.3 51.4 %copy-start.1 = (f32[7,7,128]{2,1,0:T(8,128)S(1)}, f32[7,7,128]{2,1,0:T(8,128)}, u32[]{:S(2)}) copy-start(f32[7,7,128]{2,1,0:T(8,128)} %kernel_ref.9) | copy-start | bytes 75268
  35.9 5.3 %collective-permute-start.2 = (bf16[2,2,3,3,128]{4,3,2,1,0:T(4,128)(2,1)S(1)}, bf16[2,2,3,3,128]{4,3,2,1,0:T(4,128)(2,1)S(1)}, u32[]{:S(2)}, u32[]{:S(2)}) collective-permute-start(bf16[2,2,3,3,128]{4,3,2,1,0:T(4,128)(2,1)S(1)} %get-tuple-element.41), channel_id=1, source_target_pairs={{0,1},{1,2},{2,3},{3,4},{4,5},{5,6},{6,7},{7,8},{8,9},{9,10},{10,1... | collective-permute-start | bytes 27656 | tf_op jit(solution)/shard_map/ppermute | solution.py:412
  37.9 5.0 %collective-permute-start.3 = (bf16[2,2,3,3,128]{4,3,2,1,0:T(4,128)(2,1)S(1)}, bf16[2,2,3,3,128]{4,3,2,1,0:T(4,128)(2,1)S(1)}, u32[]{:S(2)}, u32[]{:S(2)}) collective-permute-start(bf16[2,2,3,3,128]{4,3,2,1,0:T(4,128)(2,1)S(1)} %get-tuple-element.40), channel_id=1, source_target_pairs={{1,0},{2,1},{3,2},{4,3},{5,4},{6,5},{7,6},{8,7},{9,8},{10,9},{11,1... | collective-permute-start | bytes 27656 | tf_op jit(solution)/shard_map/ppermute | solution.py:413
  42.9 22.7 %collective-permute-start.4 = (bf16[3,72,128]{2,1,0:T(8,128)(2,1)S(1)}, bf16[3,72,128]{2,1,0:T(8,128)(2,1)S(1)}, u32[]{:S(2)}, u32[]{:S(2)}) collective-permute-start(bf16[3,72,128]{2,1,0:T(8,128)(2,1)S(1)} %get-tuple-element.25), channel_id=1, source_target_pairs={{0,32},{32,64},{64,96},{96,128},{128,160},{160,192},{192,224},{224... | collective-permute-start | bytes 165896 | tf_op jit(solution)/shard_map/ppermute | solution.py:492
  47.1 5.5 %collective-permute-start = (bf16[3,64,128]{2,1,0:T(8,128)(2,1)S(1)}, bf16[3,64,128]{2,1,0:T(8,128)(2,1)S(1)}, u32[]{:S(2)}, u32[]{:S(2)}) collective-permute-start(bf16[3,64,128]{2,1,0:T(8,128)(2,1)S(1)} %get-tuple-element.39), channel_id=1, source_target_pairs={{0,1},{1,2},{2,3},{3,4},{4,5},{5,6},{6,7},{7,8},{8,9},{9,10},{10,1... | collective-permute-start | bytes 147464 | tf_op jit(solution)/shard_map/ppermute | solution.py:412
  49.3 5.4 %collective-permute-start.1 = (bf16[3,64,128]{2,1,0:T(8,128)(2,1)S(1)}, bf16[3,64,128]{2,1,0:T(8,128)(2,1)S(1)}, u32[]{:S(2)}, u32[]{:S(2)}) collective-permute-start(bf16[3,64,128]{2,1,0:T(8,128)(2,1)S(1)} %get-tuple-element.38), channel_id=1, source_target_pairs={{1,0},{2,1},{3,2},{4,3},{5,4},{6,5},{7,6},{8,7},{9,8},{10,9},{11,1... | collective-permute-start | bytes 147464 | tf_op jit(solution)/shard_map/ppermute | solution.py:413
  63.2 2.5 %copy-start.2 = (bf16[128,512]{1,0:T(8,128)(2,1)S(1)}, bf16[128,512]{1,0:T(8,128)(2,1)}, u32[]{:S(2)}) copy-start(bf16[128,512]{1,0:T(8,128)(2,1)} %w_in_ref.1) | copy-start | bytes 393220
  63.2 2.5 %copy-start.3 = (bf16[512,128]{1,0:T(8,128)(2,1)S(1)}, bf16[512,128]{1,0:T(8,128)(2,1)}, u32[]{:S(2)}) copy-start(bf16[512,128]{1,0:T(8,128)(2,1)} %w_out_ref.1) | copy-start | bytes 393220
  63.2 2.5 %copy-start.4 = (f32[512]{0:T(512)S(1)}, f32[512]{0:T(512)}, u32[]{:S(2)}) copy-start(f32[512]{0:T(512)} %param.18) | copy-start | bytes 6148
  63.2 2.5 %copy-start.5 = (f32[128]{0:T(128)S(1)}, f32[128]{0:T(128)}, u32[]{:S(2)}) copy-start(f32[128]{0:T(128)} %param.14) | copy-start | bytes 1540
  63.2 2.5 %copy-start.6 = (f32[128]{0:T(128)S(1)}, f32[128]{0:T(128)}, u32[]{:S(2)}) copy-start(f32[128]{0:T(128)} %param.15) | copy-start | bytes 1540
  63.2 2.5 %copy-start.7 = (f32[128]{0:T(128)S(1)}, f32[128]{0:T(128)}, u32[]{:S(2)}) copy-start(f32[128]{0:T(128)} %param.16) | copy-start | bytes 1540
  102.9 26.8 %all-to-all-start.2 = ((bf16[16,40,128]{2,1,0:T(8,128)(2,1)}), bf16[16,40,128]{2,1,0:T(8,128)(2,1)S(1)}, u32[]{:S(2)}, u32[]{:S(2)}) async-start(bf16[16,40,128]{2,1,0:T(8,128)(2,1)} %fold.2), calls=%async_computation.2 | async-start | bytes 327680 | tf_op jit(solution)/shard_map/all_to_all | solution.py:384
  109.4 5.9 %collective-permute-start.5 = (bf16[3,64,128]{2,1,0:T(8,128)(2,1)S(1)}, bf16[3,64,128]{2,1,0:T(8,128)(2,1)S(1)}, u32[]{:S(2)}, u32[]{:S(2)}) collective-permute-start(bf16[3,64,128]{2,1,0:T(8,128)(2,1)S(1)} %get-tuple-element.37), channel_id=1, source_target_pairs={{0,1},{1,2},{2,3},{3,4},{4,5},{5,6},{6,7},{7,8},{8,9},{9,10},{10,1... | collective-permute-start | bytes 147464 | tf_op jit(solution)/shard_map/ppermute | solution.py:412
  113.1 6.2 %collective-permute-start.6 = (bf16[3,64,128]{2,1,0:T(8,128)(2,1)S(1)}, bf16[3,64,128]{2,1,0:T(8,128)(2,1)S(1)}, u32[]{:S(2)}, u32[]{:S(2)}) collective-permute-start(bf16[3,64,128]{2,1,0:T(8,128)(2,1)S(1)} %get-tuple-element.36), channel_id=1, source_target_pairs={{1,0},{2,1},{3,2},{4,3},{5,4},{6,5},{7,6},{8,7},{9,8},{10,9},{11,1... | collective-permute-start | bytes 147464 | tf_op jit(solution)/shard_map/ppermute | solution.py:413
  119.4 22.2 %collective-permute-start.7 = (bf16[2,3,72,128]{3,2,1,0:T(8,128)(2,1)S(1)}, bf16[2,3,72,128]{3,2,1,0:T(8,128)(2,1)S(1)}, u32[]{:S(2)}, u32[]{:S(2)}) collective-permute-start(bf16[2,3,72,128]{3,2,1,0:T(8,128)(2,1)S(1)} %strips.1), channel_id=1, source_target_pairs={{0,16},{16,0},{32,48},{48,32},{64,80},{80,64},{96,112},{112,96},{1... | collective-permute-start | bytes 331784 | tf_op jit(solution)/shard_map/ppermute | solution.py:438
  130.5 27.4 %all-to-all-start.3 = ((bf16[32,40,128]{2,1,0:T(8,128)(2,1)}), bf16[32,40,128]{2,1,0:T(8,128)(2,1)S(1)}, u32[]{:S(2)}, u32[]{:S(2)}) async-start(bf16[32,40,128]{2,1,0:T(8,128)(2,1)} %fold.3), calls=%async_computation.3 | async-start | bytes 655360 | tf_op jit(solution)/shard_map/all_to_all | solution.py:384
  141.6 13.6 %copy-start = (bf16[64,64,128]{2,1,0:T(8,128)(2,1)S(1)}, bf16[64,64,128]{2,1,0:T(8,128)(2,1)}, u32[]{:S(2)}) copy-start(bf16[64,64,128]{2,1,0:T(8,128)(2,1)} %cot_ref.1) | copy-start | bytes 3145732
  141.6 12.9 %collective-permute-start.8 = (bf16[3,72,128]{2,1,0:T(8,128)(2,1)S(1)}, bf16[3,72,128]{2,1,0:T(8,128)(2,1)S(1)}, u32[]{:S(2)}, u32[]{:S(2)}) collective-permute-start(bf16[3,72,128]{2,1,0:T(8,128)(2,1)S(1)} %get-tuple-element.42), channel_id=1, source_target_pairs={{0,32},{32,64},{64,96},{96,128},{128,160},{160,192},{192,224},{224... | collective-permute-start | bytes 165896 | tf_op jit(solution)/shard_map/ppermute | solution.py:439

commit v6 on v5

--- a/solution.py
+++ b/solution.py
@@ -104,15 +104,6 @@
     return buf_ref[0 : SUB * SUB, :]
 
 
-def put_sides(low_ref, high_ref, out_ref, rows):
-    for c in range(HALF):
-        west = low_ref[pl.ds(c, rows, stride=SUB), :].astype(jnp.bfloat16)
-        east = high_ref[pl.ds(SUB - HALF + c, rows, stride=SUB), :].astype(jnp.bfloat16)
-        for member in range(2):
-            out_ref[member, 0, c] = west
-            out_ref[member, 1, c] = east
-
-
 def strip_kernel(even_ref, south_ref, block_ref, north_ref, out_ref, low_ref, high_ref):
     height = block_ref.shape[0]
 
@@ -144,36 +135,6 @@
 def back_conv_kernel(south_ref, block_ref, north_ref, kernel_ref, out_ref, tiles_ref, buf_ref):
     spread_all(south_ref, block_ref, north_ref, tiles_ref, buf_ref)
     conv_rows(tiles_ref, kernel_ref, out_ref, 0, block_ref.shape[0], True)
-
-
-def side_kernel(block_ref, out_ref, low_ref, high_ref):
-    height = block_ref.shape[0]
-
-    def one(step, _):
-        for r in range(SUB):
-            row_of = block_ref[step * SUB + r]
-            at = pl.ds((step * SUB + r) * SUB, SUB)
-            low_ref[at, :] = row_of[0:SUB].astype(jnp.float32)
-            high_ref[at, :] = row_of[64 - SUB : 64].astype(jnp.float32)
-        return 0
-
-    lax.fori_loop(0, height // SUB, one, 0)
-    put_sides(low_ref, high_ref, out_ref, height)
-
-
-def tall_kernel(even_ref, body_ref, south_ref, north_ref, keep_ref, pass_ref, buf_ref):
-    height = body_ref.shape[3]
-    even = even_ref[0] == 1
-    buf_ref[...] = jnp.zeros_like(buf_ref)
-    for at, ref in enumerate((keep_ref, pass_ref)):
-        for c in range(HALF):
-            def pick(of_ref):
-                return jnp.where(even, of_ref[1, at, c].astype(jnp.float32), of_ref[0, 1 - at, c].astype(jnp.float32))
-
-            buf_ref[0:HALF, :] = pick(south_ref)
-            buf_ref[HALF : HALF + height, :] = pick(body_ref)
-            buf_ref[HALF + height : 2 * HALF + height, :] = pick(north_ref)
-            ref[c] = buf_ref[...].astype(jnp.bfloat16)
 
 
 def rest_kernel(start, conv_in, tiles_ref, kernel_ref, out_ref):
@@ -414,11 +375,6 @@
     return south, north
 
 
-def swap(sides):
-    pairs = [[i, i + 1] for i in range(0, lax.axis_size("lon"), 2)]
-    return lax.all_to_all(sides, "lon", 0, 0, tiled=True, axis_index_groups=pairs)
-
-
 def onward_pairs():
     count = lax.axis_size("lon")
     return [(i, (i + 2) % count) for i in range(0, count, 2)] + [(i, (i - 2) % count) for i in range(1, count, 2)]
@@ -467,30 +423,9 @@
     masked = cells * ocean
     out_grad = cotangent * ocean
     even = (1 - lax.axis_index("lon") % 2).astype(jnp.int32).reshape(1)
-    south, north = lat_halo(cells[-HALF:] * ocean[-HALF:], cells[:HALF] * ocean[:HALF])
-    sides = pl.pallas_call(
-        side_kernel,
-        out_shape=jax.ShapeDtypeStruct((2, 2, HALF, height, channels), jnp.bfloat16),
-        in_specs=[VMEM],
-        out_specs=VMEM,
-        scratch_shapes=[pltpu.VMEM((height * SUB, channels), jnp.float32)] * 2,
-        compiler_params=PARAMS,
-        name="sides",
-    )(masked)
-    swapped = swap(sides)
-    corner_south, corner_north = lat_halo(swapped[..., -HALF:, :], swapped[..., :HALF, :])
-    tall = jax.ShapeDtypeStruct((HALF, height + 2 * HALF + 2, channels), jnp.bfloat16)
-    keep, onward = pl.pallas_call(
-        tall_kernel,
-        out_shape=(tall, tall),
-        in_specs=[SMEM] + [VMEM] * 3,
-        out_specs=[VMEM] * 2,
-        scratch_shapes=[pltpu.VMEM(tall.shape[1:], jnp.float32)],
-        compiler_params=PARAMS,
-        name="tall",
-    )(even, swapped, corner_south, corner_north)
-    got = lax.ppermute(onward, "lon", onward_pairs())
-    early = height * 3 // 4
+    south, north = lat_halo(masked[-HALF:], masked[:HALF])
+    keep, got = lon_halo(even, south, masked, north)
+    early = height * 9 // 16
     conv, tiles = first_conv(south, masked, north, kernel, early)
     conv = pl.pallas_call(
         functools.partial(rest_kernel, early),

time: 159 us -> 149 us (0.937)
  blocking collectives: 50.1 us -> 16.3 us
  starting transfers between devices: 43.4 us -> 58.5 us
  waiting for transfers between devices: 14.1 us -> 23.6 us
    all_to_all x1 -> x0, blocking collectives: 32.5 us -> none  [swap(): lax.all_to_all(sides, 'lon', 0, 0, tiled=True, axis_index_groups=pairs)]
    ppermute x1 -> x2, starting transfers between devices: 10.3 us -> 23.9 us  [lon_halo(): lax.ppermute(strips, 'lon', [(i, i ^ 1) for i in range(lax.axis_size('lon...]
    ppermute x1 -> x2, waiting for transfers between devices: 6.01 us -> 15.8 us  [lon_halo(): lax.ppermute(strips, 'lon', [(i, i ^ 1) for i in range(lax.axis_size('lon...]
    all_to_all x2, starting transfers between devices: 11.6 us -> 17.7 us  [exchange(): lax.all_to_all(parts, ('lon', 'lat'), 0, 0, tiled=True, axis_index_groups...]
    ppermute x3 -> x2, starting transfers between devices: 8.55 us -> 3.84 us  [lat_halo(): north = lax.ppermute(bottom, 'lat', down)]
    ppermute x1 -> x0, starting transfers between devices: 3.2 us -> none  [body(): got = lax.ppermute(onward, 'lon', onward_pairs())]
    ppermute x1 -> x2, starting transfers between devices: 2.07 us -> 5.27 us  [lon_halo(): got = lax.ppermute(swapped[1], 'lon', onward_pairs())]
    pallas_call x1, Pallas kernels: 2.39 us -> 4.18 us  [body(): pl.pallas_call(functools.partial(rest_kernel, early), out_shape=pltpu.VME...]
  transfers between devices with their start and end apart: 11 -> 10, of which waited for: 5 -> 5; matrix products, arithmetic and copies ran while one was open for 1% -> 0% of each run, Pallas kernels for 16% -> 17%
where the time goes in v6:
time: 149 us
  starting transfers between devices  58.5 us (39%)
  Pallas kernels  45.8 us (31%)
  waiting for transfers between devices  23.6 us (16%)
  blocking collectives  16.3 us (11%)
  other arithmetic  2.68 us (2%)
    ppermute x2, starting transfers between devices, lon_halo(): lax.ppermute(strips, 'lon', [(i, i ^ 1) for i in range(lax.axis_size('lon...  23.9 us
    pallas_call x1, Pallas kernels, body(): pl.pallas_call(functools.partial(block_kernel, chunk), out_shape=(pltpu.V...  18.9 us
    all_to_all x2, starting transfers between devices, exchange(): lax.all_to_all(parts, ('lon', 'lat'), 0, 0, tiled=True, axis_index_groups...  17.7 us
    all_to_all x1, blocking collectives, exchange(): lax.all_to_all(parts, ('lon', 'lat'), 0, 0, tiled=True, axis_index_groups...  16.3 us
    ppermute x2, waiting for transfers between devices, lon_halo(): lax.ppermute(strips, 'lon', [(i, i ^ 1) for i in range(lax.axis_size('lon...  15.8 us
    pallas_call x1, Pallas kernels, body(): pl.pallas_call(back_conv_kernel, out_shape=pltpu.VMEM((height * across, c...  10.9 us
    ppermute x2, starting transfers between devices, lat_halo(): south = lax.ppermute(top, 'lat', up)  7.75 us
    ppermute x2, waiting for transfers between devices, lat_halo(): north = lax.ppermute(bottom, 'lat', down)  7.44 us
  transfers between devices with their start and end apart: 10, of which 5 were waited for; matrix products, arithmetic and copies ran while one was open for 0% of the time, Pallas kernels for 17%

profile of v6, /device:TPU:33, one launch (start us, length us, event | category | flops | bytes accessed | tf_op | source)
XLA Modules:
  0.0 148.5 jit_solution(12926121734422069282)
XLA Ops:
  0.6 0.8 convert_element_type.3
  1.4 0.0 copy-start.1
  1.4 1.9 %broadcast_multiply_fusion = (bf16[64,64,128]{2,1,0:T(8,128)(2,1)S(1)}, bf16[64,64,128]{2,1,0:T(8,128)(2,1)S(1)}) fusion(bf16[64,64,128]{2,1,0:T(8,128)(2,1)} %cot_ref.1, bf16[64,64]{1,0:T(8,128)(2,1)S(1)} %convert_element_type.3, bf16[64,64,128]{2,1,0:T(8,128)(2,1)} %param.10), kind=kLoop, calls=%fused_computation | loop fusion | flops 1048576 | bytes 4202496 | tf_op jit(solution)/shard_map/mul | solution.py:424
  3.3 4.1 %collective-permute-start = (bf16[3,64,128]{2,1,0:T(8,128)(2,1)S(1)}, bf16[3,64,128]{2,1,0:T(8,128)(2,1)S(1)}, u32[]{:S(2)}, u32[]{:S(2)}) collective-permute-start(bf16[3,64,128]{2,1,0:T(8,128)(2,1)S(1)} %get-tuple-element.35), channel_id=1, source_target_pairs={{0,1},{1,2},{2,3},{3,4},{4,5},{5,6},{6,7},{7,8},{8,9},{9,10},{10,1... | collective-permute-start | bytes 147464 | tf_op jit(solution)/shard_map/ppermute | solution.py:373
  7.5 1.9 %collective-permute-start.1 = (bf16[3,64,128]{2,1,0:T(8,128)(2,1)S(1)}, bf16[3,64,128]{2,1,0:T(8,128)(2,1)S(1)}, u32[]{:S(2)}, u32[]{:S(2)}) collective-permute-start(bf16[3,64,128]{2,1,0:T(8,128)(2,1)S(1)} %get-tuple-element.34), channel_id=1, source_target_pairs={{1,0},{2,1},{3,2},{4,3},{5,4},{6,5},{7,6},{8,7},{9,8},{10,9},{11,1... | collective-permute-start | bytes 147464 | tf_op jit(solution)/shard_map/ppermute | solution.py:374
  9.4 0.0 collective-permute-done.south_ref
  9.4 3.5 %collective-permute-done.1.north_ref = bf16[3,64,128]{2,1,0:T(8,128)(2,1)S(1)} collective-permute-done((bf16[3,64,128]{2,1,0:T(8,128)(2,1)S(1)}, bf16[3,64,128]{2,1,0:T(8,128)(2,1)S(1)}, u32[]{:S(2)}, u32[]{:S(2)}) %collective-permute-start.1) | collective-permute-done | bytes 49184 | tf_op jit(solution)/shard_map/ppermute | solution.py:374
  12.9 0.1 strips.2
  13.0 13.6 %collective-permute-start.2 = (bf16[2,3,72,128]{3,2,1,0:T(8,128)(2,1)S(1)}, bf16[2,3,72,128]{3,2,1,0:T(8,128)(2,1)S(1)}, u32[]{:S(2)}, u32[]{:S(2)}) collective-permute-start(bf16[2,3,72,128]{3,2,1,0:T(8,128)(2,1)S(1)} %strips.2), channel_id=1, source_target_pairs={{0,16},{16,0},{32,48},{48,32},{64,80},{80,64},{96,112},{112,96},{1... | collective-permute-start | bytes 331784 | tf_op jit(solution)/shard_map/ppermute | solution.py:394
  26.6 9.8 %collective-permute-done.2 = bf16[2,3,72,128]{3,2,1,0:T(8,128)(2,1)S(1)} collective-permute-done((bf16[2,3,72,128]{3,2,1,0:T(8,128)(2,1)S(1)}, bf16[2,3,72,128]{3,2,1,0:T(8,128)(2,1)S(1)}, u32[]{:S(2)}, u32[]{:S(2)}) %collective-permute-start.2) | collective-permute-done | bytes 110624 | tf_op jit(solution)/shard_map/ppermute | solution.py:394
  36.4 3.2 %collective-permute-start.3 = (bf16[3,72,128]{2,1,0:T(8,128)(2,1)S(1)}, bf16[3,72,128]{2,1,0:T(8,128)(2,1)S(1)}, u32[]{:S(2)}, u32[]{:S(2)}) collective-permute-start(bf16[3,72,128]{2,1,0:T(8,128)(2,1)S(1)} %get-tuple-element.38), channel_id=1, source_target_pairs={{0,32},{32,64},{64,96},{96,128},{128,160},{160,192},{192,224},{224... | collective-permute-start | bytes 165896 | tf_op jit(solution)/shard_map/ppermute | solution.py:395
  39.6 0.0 copy-done.1
  39.6 6.6 %conv.1 = (f32[4096,128]{1,0:T(8,128)S(1)}, f32[8064,128]{1,0:T(8,128)S(1)}) custom-call(bf16[3,64,128]{2,1,0:T(8,128)(2,1)S(1)} %collective-permute-done.south_ref, bf16[64,64,128]{2,1,0:T(8,128)(2,1)S(1)} %get-tuple-element.41.block_ref, bf16[3,64,128]{2,1,0:T(8,128)(2,1)S(1)} %collective-permute-done.1.north_ref, f32[7,7,128]{2,1,0:T(8,128)S(1)} %copy-done.1), custom_call_target="tpu_custom_call" | custom-call | tf_op jit(solution)/shard_map/conv/pallas_call | solution.py:402
  46.3 0.0 copy-start.2
  46.3 0.0 copy-start.3
  46.3 0.0 copy-start.4
  46.3 0.0 copy-start.5
  46.3 0.0 copy-start.6
  46.4 0.0 copy-start.7
  46.4 4.2 %rest.1.conv_in = f32[4096,128]{1,0:T(8,128)S(1)} custom-call(f32[4096,128]{1,0:T(8,128)S(1)} %get-tuple-element.20.conv_in, f32[8064,128]{1,0:T(8,128)S(1)} %get-tuple-element.21.tiles_ref.tiles_in, f32[7,7,128]{2,1,0:T(8,128)S(1)} %copy-done.1), custom_call_target="tpu_custom_call", output_to_operand_aliasing={{}: (0, {})} | custom-call | tf_op jit(solution)/shard_map/rest/pallas_call | solution.py:430
  50.5 0.0 collective-permute-done.3.got_ref
  50.6 0.0 copy-done.2
  50.6 0.0 copy-done.3
  50.6 0.0 copy-done.4
  50.6 0.0 copy-done.5
  50.6 0.0 copy-done.6
  50.6 0.0 copy-done.7
  50.6 18.9 %block.1 = (f32[4096,128]{1,0:T(8,128)S(1)}, f32[8064,128]{1,0:T(8,128)S(1)}, bf16[64,64,128]{2,1,0:T(8,128)(2,1)S(1)}, bf16[32,40,128]{2,1,0:T(8,128)(2,1)S(1)}) custom-call(s32[1]{0:T(128)} %bitcast.even_ref, f32[4096,128]{1,0:T(8,128)S(1)} %rest.1.conv_in, ...), custom_call_target="tpu_custom_call", output_to_operand_aliasing={{0}: (1, {}), {1}: (2, {})} | custom-call | tf_op jit(solution)/shard_map/block/pallas_call | solution.py:441
  69.6 16.3 %all_to_all.15.parts_ref = bf16[32,40,128]{2,1,0:T(8,128)(2,1)S(1)} all-to-all(bf16[32,40,128]{2,1,0:T(8,128)(2,1)S(1)} %get-tuple-element.24), channel_id=1, replica_groups={{0,1,32,33,64,65,96,97,128,129,160,161,192,193,224,225,256,257,288,289,..., dimensions={0} | all-to-all | bytes 655360 | tf_op jit(solution)/shard_map/all_to_all | solution.py:345
  85.9 0.7 fold.2
  86.6 12.6 %all-to-all-start.1 = ((bf16[16,40,128]{2,1,0:T(8,128)(2,1)}), bf16[16,40,128]{2,1,0:T(8,128)(2,1)S(1)}, u32[]{:S(2)}, u32[]{:S(2)}) async-start(bf16[16,40,128]{2,1,0:T(8,128)(2,1)} %fold.2), calls=%async_computation.1 | async-start | bytes 327680 | tf_op jit(solution)/shard_map/all_to_all | solution.py:345
  99.3 3.6 %collective-permute-start.4 = (bf16[3,64,128]{2,1,0:T(8,128)(2,1)S(1)}, bf16[3,64,128]{2,1,0:T(8,128)(2,1)S(1)}, u32[]{:S(2)}, u32[]{:S(2)}) collective-permute-start(bf16[3,64,128]{2,1,0:T(8,128)(2,1)S(1)} %get-tuple-element.33), channel_id=1, source_target_pairs={{0,1},{1,2},{2,3},{3,4},{4,5},{5,6},{6,7},{7,8},{8,9},{9,10},{10,1... | collective-permute-start | bytes 147464 | tf_op jit(solution)/shard_map/ppermute | solution.py:373
  102.9 1.9 %collective-permute-start.5 = (bf16[3,64,128]{2,1,0:T(8,128)(2,1)S(1)}, bf16[3,64,128]{2,1,0:T(8,128)(2,1)S(1)}, u32[]{:S(2)}, u32[]{:S(2)}) collective-permute-start(bf16[3,64,128]{2,1,0:T(8,128)(2,1)S(1)} %get-tuple-element.32), channel_id=1, source_target_pairs={{1,0},{2,1},{3,2},{4,3},{5,4},{6,5},{7,6},{8,7},{9,8},{10,9},{11,1... | collective-permute-start | bytes 147464 | tf_op jit(solution)/shard_map/ppermute | solution.py:374
  104.8 0.3 collective-permute-done.4.south_ref
  105.2 4.0 %collective-permute-done.5.north_ref = bf16[3,64,128]{2,1,0:T(8,128)(2,1)S(1)} collective-permute-done((bf16[3,64,128]{2,1,0:T(8,128)(2,1)S(1)}, bf16[3,64,128]{2,1,0:T(8,128)(2,1)S(1)}, u32[]{:S(2)}, u32[]{:S(2)}) %collective-permute-start.5) | collective-permute-done | bytes 49184 | tf_op jit(solution)/shard_map/ppermute | solution.py:374
  109.2 0.1 strips.3
  109.3 10.3 %collective-permute-start.6 = (bf16[2,3,72,128]{3,2,1,0:T(8,128)(2,1)S(1)}, bf16[2,3,72,128]{3,2,1,0:T(8,128)(2,1)S(1)}, u32[]{:S(2)}, u32[]{:S(2)}) collective-permute-start(bf16[2,3,72,128]{3,2,1,0:T(8,128)(2,1)S(1)} %strips.3), channel_id=1, source_target_pairs={{0,16},{16,0},{32,48},{48,32},{64,80},{80,64},{96,112},{112,96},{1... | collective-permute-start | bytes 331784 | tf_op jit(solution)/shard_map/ppermute | solution.py:394
  119.5 0.0 all-to-all-done.1.parts_ref
  119.6 0.8 fold.3
  120.3 5.1 %all-to-all-start.2 = ((bf16[32,40,128]{2,1,0:T(8,128)(2,1)}), bf16[32,40,128]{2,1,0:T(8,128)(2,1)S(1)}, u32[]{:S(2)}, u32[]{:S(2)}) async-start(bf16[32,40,128]{2,1,0:T(8,128)(2,1)} %fold.3), calls=%async_computation.2 | async-start | bytes 655360 | tf_op jit(solution)/shard_map/all_to_all | solution.py:345
  125.4 6.0 %collective-permute-done.6 = bf16[2,3,72,128]{3,2,1,0:T(8,128)(2,1)S(1)} collective-permute-done((bf16[2,3,72,128]{3,2,1,0:T(8,128)(2,1)S(1)}, bf16[2,3,72,128]{3,2,1,0:T(8,128)(2,1)S(1)}, u32[]{:S(2)}, u32[]{:S(2)}) %collective-permute-start.6) | collective-permute-done | bytes 110624 | tf_op jit(solution)/shard_map/ppermute | solution.py:394
  131.5 0.0 copy-start
  131.5 2.1 %collective-permute-start.7 = (bf16[3,72,128]{2,1,0:T(8,128)(2,1)S(1)}, bf16[3,72,128]{2,1,0:T(8,128)(2,1)S(1)}, u32[]{:S(2)}, u32[]{:S(2)}) collective-permute-start(bf16[3,72,128]{2,1,0:T(8,128)(2,1)S(1)} %get-tuple-element.36), channel_id=1, source_target_pairs={{0,32},{32,64},{64,96},{96,128},{128,160},{160,192},{192,224},{224... | collective-permute-start | bytes 165896 | tf_op jit(solution)/shard_map/ppermute | solution.py:395
  133.5 10.9 %back_conv.1.spread_in = f32[4096,128]{1,0:T(8,128)S(1)} custom-call(bf16[3,64,128]{2,1,0:T(8,128)(2,1)S(1)} %collective-permute-done.4.south_ref, bf16[64,64,128]{2,1,0:T(8,128)(2,1)S(1)} %get-tuple-element.22.block_ref, bf16[3,64,128]{2,1,0:T(8,128)(2,1)S(1)} %collective-permute-done.5.north_ref, f32[7,7,128]{2,1,0:T(8,128)S(1)} %copy-done.1), custom_call_target="tpu_custom_call" | custom-call | tf_op jit(solution)/shard_map/back_conv/pallas_call | solution.py:473
  144.4 0.0 collective-permute-done.7.got_ref
  144.4 0.6 broadcast_in_dim.2.mask_ref
  145.0 0.0 copy-done
  145.0 2.6 %back.1 = (f32[4096,128]{1,0:T(8,128)S(1)}, bf16[64,64,128]{2,1,0:T(8,128)(2,1)}) custom-call(s32[1]{0:T(128)} %bitcast.even_ref, f32[4096,128]{1,0:T(8,128)S(1)} %back_conv.1.spread_in, bf16[3,72,128]{2,1,0:T(8,128)(2,1)S(1)} %get-tuple-element.37.keep_ref, bf16[3,72,128]{2,1,0:T(8,128)(2,1)S(1)} %collective-permute-done.7.got_ref, ...), custom_call_target="tpu_custom_call", output_to_operand_aliasing={{0}: (1, {})} | custom-call | tf_op jit(solution)/shard_map/back/pallas_call | solution.py:485
  147.7 0.0 all-to-all-done.2.all_ref
  147.7 0.9 unpack.1
  (4 shorter events, 0.0 us)
Async XLA Ops:
  1.4 38.2 %copy-start.1 = (f32[7,7,128]{2,1,0:T(8,128)S(1)}, f32[7,7,128]{2,1,0:T(8,128)}, u32[]{:S(2)}) copy-start(f32[7,7,128]{2,1,0:T(8,128)} %kernel_ref.9) | copy-start | bytes 75268
  3.3 6.1 %collective-permute-start = (bf16[3,64,128]{2,1,0:T(8,128)(2,1)S(1)}, bf16[3,64,128]{2,1,0:T(8,128)(2,1)S(1)}, u32[]{:S(2)}, u32[]{:S(2)}) collective-permute-start(bf16[3,64,128]{2,1,0:T(8,128)(2,1)S(1)} %get-tuple-element.35), channel_id=1, source_target_pairs={{0,1},{1,2},{2,3},{3,4},{4,5},{5,6},{6,7},{7,8},{8,9},{9,10},{10,1... | collective-permute-start | bytes 147464 | tf_op jit(solution)/shard_map/ppermute | solution.py:373
  7.5 5.4 %collective-permute-start.1 = (bf16[3,64,128]{2,1,0:T(8,128)(2,1)S(1)}, bf16[3,64,128]{2,1,0:T(8,128)(2,1)S(1)}, u32[]{:S(2)}, u32[]{:S(2)}) collective-permute-start(bf16[3,64,128]{2,1,0:T(8,128)(2,1)S(1)} %get-tuple-element.34), channel_id=1, source_target_pairs={{1,0},{2,1},{3,2},{4,3},{5,4},{6,5},{7,6},{8,7},{9,8},{10,9},{11,1... | collective-permute-start | bytes 147464 | tf_op jit(solution)/shard_map/ppermute | solution.py:374
  13.0 23.4 %collective-permute-start.2 = (bf16[2,3,72,128]{3,2,1,0:T(8,128)(2,1)S(1)}, bf16[2,3,72,128]{3,2,1,0:T(8,128)(2,1)S(1)}, u32[]{:S(2)}, u32[]{:S(2)}) collective-permute-start(bf16[2,3,72,128]{3,2,1,0:T(8,128)(2,1)S(1)} %strips.2), channel_id=1, source_target_pairs={{0,16},{16,0},{32,48},{48,32},{64,80},{80,64},{96,112},{112,96},{1... | collective-permute-start | bytes 331784 | tf_op jit(solution)/shard_map/ppermute | solution.py:394
  36.4 14.1 %collective-permute-start.3 = (bf16[3,72,128]{2,1,0:T(8,128)(2,1)S(1)}, bf16[3,72,128]{2,1,0:T(8,128)(2,1)S(1)}, u32[]{:S(2)}, u32[]{:S(2)}) collective-permute-start(bf16[3,72,128]{2,1,0:T(8,128)(2,1)S(1)} %get-tuple-element.38), channel_id=1, source_target_pairs={{0,32},{32,64},{64,96},{96,128},{128,160},{160,192},{192,224},{224... | collective-permute-start | bytes 165896 | tf_op jit(solution)/shard_map/ppermute | solution.py:395
  46.3 4.3 %copy-start.2 = (bf16[128,512]{1,0:T(8,128)(2,1)S(1)}, bf16[128,512]{1,0:T(8,128)(2,1)}, u32[]{:S(2)}) copy-start(bf16[128,512]{1,0:T(8,128)(2,1)} %w_in_ref.1) | copy-start | bytes 393220
  46.3 4.3 %copy-start.3 = (bf16[512,128]{1,0:T(8,128)(2,1)S(1)}, bf16[512,128]{1,0:T(8,128)(2,1)}, u32[]{:S(2)}) copy-start(bf16[512,128]{1,0:T(8,128)(2,1)} %w_out_ref.1) | copy-start | bytes 393220
  46.3 4.3 %copy-start.4 = (f32[512]{0:T(512)S(1)}, f32[512]{0:T(512)}, u32[]{:S(2)}) copy-start(f32[512]{0:T(512)} %param.18) | copy-start | bytes 6148
  46.3 4.3 %copy-start.5 = (f32[128]{0:T(128)S(1)}, f32[128]{0:T(128)}, u32[]{:S(2)}) copy-start(f32[128]{0:T(128)} %param.14) | copy-start | bytes 1540
  46.3 4.3 %copy-start.6 = (f32[128]{0:T(128)S(1)}, f32[128]{0:T(128)}, u32[]{:S(2)}) copy-start(f32[128]{0:T(128)} %param.15) | copy-start | bytes 1540
  46.4 4.3 %copy-start.7 = (f32[128]{0:T(128)S(1)}, f32[128]{0:T(128)}, u32[]{:S(2)}) copy-start(f32[128]{0:T(128)} %param.16) | copy-start | bytes 1540
  86.6 32.9 %all-to-all-start.1 = ((bf16[16,40,128]{2,1,0:T(8,128)(2,1)}), bf16[16,40,128]{2,1,0:T(8,128)(2,1)S(1)}, u32[]{:S(2)}, u32[]{:S(2)}) async-start(bf16[16,40,128]{2,1,0:T(8,128)(2,1)} %fold.2), calls=%async_computation.1 | async-start | bytes 327680 | tf_op jit(solution)/shard_map/all_to_all | solution.py:345
  99.3 5.9 %collective-permute-start.4 = (bf16[3,64,128]{2,1,0:T(8,128)(2,1)S(1)}, bf16[3,64,128]{2,1,0:T(8,128)(2,1)S(1)}, u32[]{:S(2)}, u32[]{:S(2)}) collective-permute-start(bf16[3,64,128]{2,1,0:T(8,128)(2,1)S(1)} %get-tuple-element.33), channel_id=1, source_target_pairs={{0,1},{1,2},{2,3},{3,4},{4,5},{5,6},{6,7},{7,8},{8,9},{9,10},{10,1... | collective-permute-start | bytes 147464 | tf_op jit(solution)/shard_map/ppermute | solution.py:373
  102.9 6.2 %collective-permute-start.5 = (bf16[3,64,128]{2,1,0:T(8,128)(2,1)S(1)}, bf16[3,64,128]{2,1,0:T(8,128)(2,1)S(1)}, u32[]{:S(2)}, u32[]{:S(2)}) collective-permute-start(bf16[3,64,128]{2,1,0:T(8,128)(2,1)S(1)} %get-tuple-element.32), channel_id=1, source_target_pairs={{1,0},{2,1},{3,2},{4,3},{5,4},{6,5},{7,6},{8,7},{9,8},{10,9},{11,1... | collective-permute-start | bytes 147464 | tf_op jit(solution)/shard_map/ppermute | solution.py:374
  109.3 22.2 %collective-permute-start.6 = (bf16[2,3,72,128]{3,2,1,0:T(8,128)(2,1)S(1)}, bf16[2,3,72,128]{3,2,1,0:T(8,128)(2,1)S(1)}, u32[]{:S(2)}, u32[]{:S(2)}) collective-permute-start(bf16[2,3,72,128]{3,2,1,0:T(8,128)(2,1)S(1)} %strips.3), channel_id=1, source_target_pairs={{0,16},{16,0},{32,48},{48,32},{64,80},{80,64},{96,112},{112,96},{1... | collective-permute-start | bytes 331784 | tf_op jit(solution)/shard_map/ppermute | solution.py:394
  120.3 27.3 %all-to-all-start.2 = ((bf16[32,40,128]{2,1,0:T(8,128)(2,1)}), bf16[32,40,128]{2,1,0:T(8,128)(2,1)S(1)}, u32[]{:S(2)}, u32[]{:S(2)}) async-start(bf16[32,40,128]{2,1,0:T(8,128)(2,1)} %fold.3), calls=%async_computation.2 | async-start | bytes 655360 | tf_op jit(solution)/shard_map/all_to_all | solution.py:345
  131.5 13.6 %copy-start = (bf16[64,64,128]{2,1,0:T(8,128)(2,1)S(1)}, bf16[64,64,128]{2,1,0:T(8,128)(2,1)}, u32[]{:S(2)}) copy-start(bf16[64,64,128]{2,1,0:T(8,128)(2,1)} %cot_ref.1) | copy-start | bytes 3145732
  131.5 12.9 %collective-permute-start.7 = (bf16[3,72,128]{2,1,0:T(8,128)(2,1)S(1)}, bf16[3,72,128]{2,1,0:T(8,128)(2,1)S(1)}, u32[]{:S(2)}, u32[]{:S(2)}) collective-permute-start(bf16[3,72,128]{2,1,0:T(8,128)(2,1)S(1)} %get-tuple-element.36), channel_id=1, source_target_pairs={{0,32},{32,64},{64,96},{96,128},{128,160},{160,192},{192,224},{224... | collective-permute-start | bytes 165896 | tf_op jit(solution)/shard_map/ppermute | solution.py:395

commit v7 on v6

--- a/solution.py
+++ b/solution.py
@@ -12,7 +12,6 @@
 HALF = 3
 SMALL = 64
 WIDE = 14
-DEEP = 8
 SUB = 8
 ROOT = 0.7978845608028654
 CUBE = 0.044715
@@ -27,18 +26,21 @@
         tiles_ref[pl.ds(row * (WIDE * SUB) + tap * SUB, SUB), :] = buf_ref[pl.ds(tap, SUB, stride=SUB), :]
 
 
-def spread_all(south_ref, block_ref, north_ref, tiles_ref, buf_ref):
+def spread_all(south_ref, block_ref, north_ref, tiles_ref, buf_ref, rows=None):
     height = block_ref.shape[0]
     buf_ref[...] = jnp.zeros_like(buf_ref)
     for row in range(HALF):
         spread_row(south_ref[row], row, tiles_ref, buf_ref)
-        spread_row(north_ref[row], height + HALF + row, tiles_ref, buf_ref)
+        if rows is None:
+            spread_row(north_ref[row], height + HALF + row, tiles_ref, buf_ref)
 
     def one(row, _):
         spread_row(block_ref[row], row + HALF, tiles_ref, buf_ref)
         return 0
 
-    lax.fori_loop(0, height, one, 0)
+    lax.fori_loop(0, height if rows is None else rows, one, 0)
+    if rows is not None:
+        return
     last = (height + 2 * HALF) * WIDE * SUB
     tiles_ref[last:, :] = jnp.zeros((2 * WIDE * SUB, 128), jnp.float32)
 
@@ -53,11 +55,11 @@
     return jnp.broadcast_to(kernel_ref[a, b : b + 1, :], (SUB, 128))
 
 
-def conv_rows(tiles_ref, kernel_ref, out_ref, start, stop, flip):
+def conv_rows(tiles_ref, kernel_ref, out_ref, start, stop, flip, base=0):
     def one(row, _):
         total = [None] * SUB
         for a in range(KS):
-            cells = [tile(tiles_ref, row + a, t) for t in range(WIDE)]
+            cells = [tile(tiles_ref, row + a - base, t) for t in range(WIDE)]
             for b in range(KS):
                 weight = tap_weight(kernel_ref, a, b, flip)
                 for t in range(SUB):
@@ -78,11 +80,10 @@
         cols_ref[HALF + c] = jnp.where(even, keep, got)
 
 
-def add_edges(cols_ref, kernel_ref, out_ref, height, flip, depth=SUB):
+def add_edges(cols_ref, kernel_ref, out_ref, height, flip):
     for west in (True, False):
         for at in range(HALF):
-            across = 64 // depth
-            first = at * depth if west else (across - HALF + at) * depth + depth - 1
+            first = at * SUB if west else (SUB - HALF + at) * SUB + SUB - 1
             totals = [None] * (height // SUB)
             for a in range(KS):
                 for b in range(KS):
@@ -104,6 +105,18 @@
     return buf_ref[0 : SUB * SUB, :]
 
 
+def mask_kernel(cells_ref, mask_ref, cot_ref, masked_ref, out_grad_ref, ocean_ref, top_ref, bottom_ref):
+    height = cells_ref.shape[0]
+    columns = mask_ref[...].astype(jnp.float32).T
+    for row in range(height):
+        ocean = jnp.broadcast_to(columns[:, row : row + 1], cells_ref.shape[1:])
+        masked_ref[row] = (cells_ref[row].astype(jnp.float32) * ocean).astype(jnp.bfloat16)
+        out_grad_ref[row] = (cot_ref[row].astype(jnp.float32) * ocean).astype(jnp.bfloat16)
+        ocean_ref[row] = ocean.astype(jnp.bfloat16)
+    top_ref[...] = masked_ref[height - HALF :]
+    bottom_ref[...] = masked_ref[0:HALF]
+
+
 def strip_kernel(even_ref, south_ref, block_ref, north_ref, out_ref, low_ref, high_ref):
     height = block_ref.shape[0]
 
@@ -132,26 +145,36 @@
         out_ref[1, c] = jnp.where(even, west, east).astype(jnp.bfloat16)
 
 
-def back_conv_kernel(south_ref, block_ref, north_ref, kernel_ref, out_ref, tiles_ref, buf_ref):
-    spread_all(south_ref, block_ref, north_ref, tiles_ref, buf_ref)
-    conv_rows(tiles_ref, kernel_ref, out_ref, 0, block_ref.shape[0], True)
-
-
-def rest_kernel(start, conv_in, tiles_ref, kernel_ref, out_ref):
+def rest_kernel(start, flip, conv_in, tiles_ref, kernel_ref, out_ref):
     del conv_in
-    conv_rows(tiles_ref, kernel_ref, out_ref, start, out_ref.shape[0] // 64, False)
-
-
-def conv_kernel(rows, south_ref, block_ref, north_ref, kernel_ref, out_ref, tiles_ref, buf_ref):
-    spread_all(south_ref, block_ref, north_ref, tiles_ref, buf_ref)
-    conv_rows(tiles_ref, kernel_ref, out_ref, 0, rows, False)
+    conv_rows(tiles_ref, kernel_ref, out_ref, start, out_ref.shape[0] // 64, flip)
+
+
+def back_rest_kernel(start, spread_in, block_ref, north_ref, kernel_ref, out_ref, tiles_ref, buf_ref):
+    del spread_in
+    height = block_ref.shape[0]
+    buf_ref[...] = jnp.zeros_like(buf_ref)
+
+    def one(row, _):
+        spread_row(block_ref[row], row + HALF - start, tiles_ref, buf_ref)
+        return 0
+
+    lax.fori_loop(start - HALF, height, one, 0)
+    for row in range(HALF):
+        spread_row(north_ref[row], height + HALF + row - start, tiles_ref, buf_ref)
+    conv_rows(tiles_ref, kernel_ref, out_ref, start, height, True, start)
+
+
+def conv_kernel(rows, flip, south_ref, block_ref, north_ref, kernel_ref, out_ref, tiles_ref, buf_ref):
+    spread_all(south_ref, block_ref, north_ref, tiles_ref, buf_ref, rows + HALF if flip else None)
+    conv_rows(tiles_ref, kernel_ref, out_ref, 0, rows, flip)
 
 
 def block_kernel(
     chunk,
     even_ref, conv_in, tiles_in, keep_ref, got_ref, out_grad_ref,
     kernel_ref, bias_ref, gain_ref, shift_ref, w_in_ref, b_in_ref, w_out_ref,
-    conv_ref, tiles_ref, conv_grad_ref, packed_ref,
+    conv_ref, tiles_ref, conv_grad_ref, top_ref, bottom_ref, packed_ref,
     cols_ref, buf_ref, og_tiles, round_ref, taps_ref, small_ref,
     bias_sum, gain_sum, shift_sum, grad_in, grad_out,
 ):
@@ -246,6 +269,8 @@
 
     one(0, None)
     lax.fori_loop(1, height // chunk, one, 0)
+    top_ref[...] = conv_grad_ref[height - HALF :]
+    bottom_ref[...] = conv_grad_ref[0:HALF]
     taps(height - chunk)
     pack(taps_ref, bias_sum, gain_sum, shift_sum, grad_in, grad_out, packed_ref, small_ref)
 
@@ -278,18 +303,22 @@
     del spread_in
     height = cot_ref.shape[0]
     edge_columns(even_ref[0] == 1, keep_ref, got_ref, cols_ref)
-    add_edges(cols_ref, kernel_ref, spread_ref, height, True, DEEP)
-
-    def one(row, _):
-        for t in range(64 // DEEP):
-            buf_ref[pl.ds(t, DEEP, stride=64 // DEEP), :] = spread_ref[pl.ds(row * 64 + t * DEEP, DEEP), :]
-        spread = buf_ref[0:64, :]
-        out_ref[row] = (
-            (cot_ref[row].astype(jnp.float32) + spread) * mask_ref[row].astype(jnp.float32)
-        ).astype(jnp.bfloat16)
+    add_edges(cols_ref, kernel_ref, spread_ref, height, True)
+
+    def one(step, _):
+        for r in range(4):
+            row = step * 4 + r
+            for t in range(SUB):
+                buf_ref[pl.ds(r * 64 + t, SUB, stride=SUB), :] = spread_ref[pl.ds(row * 64 + t * SUB, SUB), :]
+        for r in range(4):
+            row = step * 4 + r
+            spread = buf_ref[r * 64 : (r + 1) * 64, :]
+            out_ref[row] = (
+                (cot_ref[row].astype(jnp.float32) + spread) * mask_ref[row].astype(jnp.float32)
+            ).astype(jnp.bfloat16)
         return 0
 
-    lax.fori_loop(0, height, one, 0)
+    lax.fori_loop(0, height // 4, one, 0)
 
 
 def fold_kernel(rows, per, parts_ref, out_ref):
@@ -396,57 +425,68 @@
     return swapped[0], got
 
 
-def first_conv(south, block, north, kernel, rows):
+def first_conv(south, block, north, kernel, rows, flip):
     height, across, channels = block.shape
-    tiles = (height + 2 * HALF + 2) * WIDE * SUB
+    tiles = pltpu.VMEM(((height + 2 * HALF + 2) * WIDE * SUB, channels), jnp.float32)
+    out = pltpu.VMEM((height * across, channels), jnp.float32)
+    buf = pltpu.VMEM((SUB * SUB + 2 * SUB, channels), jnp.float32)
     return pl.pallas_call(
-        functools.partial(conv_kernel, rows),
-        out_shape=(
-            pltpu.VMEM((height * across, channels), jnp.float32),
-            pltpu.VMEM((tiles, channels), jnp.float32),
-        ),
+        functools.partial(conv_kernel, rows, flip),
+        out_shape=out if flip else (out, tiles),
         in_specs=[VMEM] * 4,
-        out_specs=[VMEM] * 2,
-        scratch_shapes=[pltpu.VMEM((SUB * SUB + 2 * SUB, channels), jnp.float32)],
-        compiler_params=PARAMS,
-        name="conv",
+        out_specs=VMEM if flip else [VMEM] * 2,
+        scratch_shapes=[tiles, buf] if flip else [buf],
+        compiler_params=PARAMS,
+        name="back_conv" if flip else "conv",
     )(south, block, north, kernel)
 
 
-def f32(*shape):
-    return jax.ShapeDtypeStruct(shape, jnp.float32)
-
-
-def body(cells, ocean_mask, cotangent, kernel, conv_bias, gain, shift, w_in, b_in, w_out, chunk=8):
-    height, across, channels = cells.shape
-    ocean = jnp.broadcast_to(ocean_mask.astype(jnp.bfloat16)[..., None], cells.shape)
-    masked = cells * ocean
-    out_grad = cotangent * ocean
-    even = (1 - lax.axis_index("lon") % 2).astype(jnp.int32).reshape(1)
-    south, north = lat_halo(masked[-HALF:], masked[:HALF])
-    keep, got = lon_halo(even, south, masked, north)
-    early = height * 9 // 16
-    conv, tiles = first_conv(south, masked, north, kernel, early)
-    conv = pl.pallas_call(
-        functools.partial(rest_kernel, early),
+def last_conv(conv, tiles, kernel, rows, flip):
+    return pl.pallas_call(
+        functools.partial(rest_kernel, rows, flip),
         out_shape=pltpu.VMEM(conv.shape, jnp.float32),
         in_specs=[VMEM] * 3,
         out_specs=VMEM,
         input_output_aliases={0: 0},
         compiler_params=PARAMS,
-        name="rest",
+        name="back_rest" if flip else "rest",
     )(*[pltpu.with_memory_space_constraint(x, pltpu.VMEM) for x in (conv, tiles)], kernel)
+
+
+def f32(*shape):
+    return jax.ShapeDtypeStruct(shape, jnp.float32)
+
+
+def body(cells, ocean_mask, cotangent, kernel, conv_bias, gain, shift, w_in, b_in, w_out, chunk=8):
+    height, across, channels = cells.shape
+    whole = jax.ShapeDtypeStruct(cells.shape, jnp.bfloat16)
+    strip = jax.ShapeDtypeStruct((HALF, across, channels), jnp.bfloat16)
+    masked, out_grad, ocean, top, bottom = pl.pallas_call(
+        mask_kernel,
+        out_shape=(whole, whole, whole, strip, strip),
+        in_specs=[VMEM] * 3,
+        out_specs=[VMEM] * 5,
+        compiler_params=PARAMS,
+        name="mask",
+    )(cells, ocean_mask, cotangent)
+    even = (1 - lax.axis_index("lon") % 2).astype(jnp.int32).reshape(1)
+    south, north = lat_halo(top, bottom)
+    keep, got = lon_halo(even, south, masked, north)
+    early = height * 9 // 16
+    conv, tiles = first_conv(south, masked, north, kernel, early, False)
+    conv = last_conv(conv, tiles, kernel, early, False)
     parts = lax.axis_size("lon")
     hidden = w_in.shape[1]
-    _, _, conv_grad, packed = pl.pallas_call(
+    _, _, conv_grad, top, bottom, packed = pl.pallas_call(
         functools.partial(block_kernel, chunk),
         out_shape=(
             pltpu.VMEM(conv.shape, jnp.float32), pltpu.VMEM(tiles.shape, jnp.float32),
             jax.ShapeDtypeStruct(cells.shape, jnp.bfloat16),
+            strip, strip,
             jax.ShapeDtypeStruct((parts, 1024 // parts + max(8, 2 * SMALL // parts), channels), jnp.bfloat16),
         ),
         in_specs=[SMEM] + [VMEM] * 12,
-        out_specs=[VMEM] * 4,
+        out_specs=[VMEM] * 6,
         scratch_shapes=[
             pltpu.VMEM((2 * HALF, height + 2 * HALF + 2, channels), jnp.float32),
             pltpu.VMEM((80, channels), jnp.float32),
@@ -468,20 +508,23 @@
         shift.reshape(1, -1), w_in, b_in.reshape(1, -1), w_out,
     )
     total = summed(packed)
-    south, north = lat_halo(conv_grad[-HALF:], conv_grad[:HALF])
+    south, north = lat_halo(top, bottom)
     keep, got = lon_halo(even, south, conv_grad, north)
+    half = height * 15 // 32
+    spread = first_conv(south, conv_grad, north, kernel, half, True)
     spread = pl.pallas_call(
-        back_conv_kernel,
-        out_shape=pltpu.VMEM((height * across, channels), jnp.float32),
+        functools.partial(back_rest_kernel, half),
+        out_shape=pltpu.VMEM(spread.shape, jnp.float32),
         in_specs=[VMEM] * 4,
         out_specs=VMEM,
         scratch_shapes=[
-            pltpu.VMEM(((height + 2 * HALF + 2) * WIDE * SUB, channels), jnp.float32),
+            pltpu.VMEM(((height + 2 * HALF - half) * WIDE * SUB, channels), jnp.float32),
             pltpu.VMEM((SUB * SUB + 2 * SUB, channels), jnp.float32),
         ],
-        compiler_params=PARAMS,
-        name="back_conv",
-    )(south, conv_grad, north, kernel)
+        input_output_aliases={0: 0},
+        compiler_params=PARAMS,
+        name="back_rest",
+    )(pltpu.with_memory_space_constraint(spread, pltpu.VMEM), conv_grad, north, kernel)
     _, cells_grad = pl.pallas_call(
         back_kernel,
         out_shape=(pltpu.VMEM(spread.shape, jnp.float32), jax.ShapeDtypeStruct(cells.shape, jnp.bfloat16)),
@@ -489,7 +532,7 @@
         out_specs=[VMEM] * 2,
         scratch_shapes=[
             pltpu.VMEM((2 * HALF, height + 2 * HALF + 2, channels), jnp.float32),
-            pltpu.VMEM((80, channels), jnp.float32),
+            pltpu.VMEM((4 * 64, channels), jnp.float32),
         ],
         input_output_aliases={1: 0},
         name="back",

time: 149 us -> 149 us (level)
  other arithmetic: 2.68 us -> 0 us
  local copies, waits for them, and re-layouts: 0.69 us -> 3.27 us
    unnamed x16 -> x22, local copies, waits for them, and re-layouts: 0.05 us -> 3.25 us
    mul x1 -> x0, other arithmetic: 1.92 us -> none  [body(): out_grad = cotangent * ocean]
    pallas_call x3 -> x5, Pallas kernels: 21.7 us -> 22.6 us  [the longest x2 11.8 us: first_conv(): pl.pallas_call(functools.partial(conv_kernel, rows, flip), out_shape=out...]
where the time goes in v7:
time: 149 us
  starting transfers between devices  58.4 us (39%)
  Pallas kernels  46.3 us (31%)
  waiting for transfers between devices  23.6 us (16%)
  blocking collectives  16.3 us (11%)
  local copies, waits for them, and re-layouts  3.27 us (2%)
    ppermute x2, starting transfers between devices, lon_halo(): lax.ppermute(strips, 'lon', [(i, i ^ 1) for i in range(lax.axis_size('lon...  23.9 us
    pallas_call x1, Pallas kernels, body(): pl.pallas_call(functools.partial(block_kernel, chunk), out_shape=(pltpu.V...  18.9 us
    all_to_all x2, starting transfers between devices, exchange(): lax.all_to_all(parts, ('lon', 'lat'), 0, 0, tiled=True, axis_index_groups...  17.7 us
    all_to_all x1, blocking collectives, exchange(): lax.all_to_all(parts, ('lon', 'lat'), 0, 0, tiled=True, axis_index_groups...  16.3 us
    ppermute x2, waiting for transfers between devices, lon_halo(): lax.ppermute(strips, 'lon', [(i, i ^ 1) for i in range(lax.axis_size('lon...  15.8 us
    pallas_call x2, Pallas kernels, first_conv(): pl.pallas_call(functools.partial(conv_kernel, rows, flip), out_shape=out...  11.8 us
    ppermute x2, starting transfers between devices, lat_halo(): south = lax.ppermute(top, 'lat', up)  7.74 us
    ppermute x2, waiting for transfers between devices, lat_halo(): north = lax.ppermute(bottom, 'lat', down)  7.42 us
  transfers between devices with their start and end apart: 10, of which 5 were waited for; matrix products, arithmetic and copies ran while one was open for 0% of the time, Pallas kernels for 17%

profile of v7, /device:TPU:33, one launch (start us, length us, event | category | flops | bytes accessed | tf_op | source)
XLA Modules:
  0.0 148.8 jit_solution(4968862572939122191)
XLA Ops:
  0.6 0.0 copy-start
  0.6 1.2 copy-done
  1.9 0.0 copy-start.2
  1.9 1.2 copy-done.2
  3.1 0.0 copy-start.6
  3.1 0.8 copy-done.6
  3.8 0.0 copy-start.3
  3.8 0.8 mask.1
  4.7 4.1 %collective-permute-start = (bf16[3,64,128]{2,1,0:T(8,128)(2,1)S(1)}, bf16[3,64,128]{2,1,0:T(8,128)(2,1)S(1)}, u32[]{:S(2)}, u32[]{:S(2)}) collective-permute-start(bf16[3,64,128]{2,1,0:T(8,128)(2,1)S(1)} %get-tuple-element.27), channel_id=1, source_target_pairs={{0,1},{1,2},{2,3},{3,4},{4,5},{5,6},{6,7},{7,8},{8,9},{9,10},{10,1... | collective-permute-start | bytes 147464 | tf_op jit(solution)/shard_map/ppermute | solution.py:402
  8.8 1.9 %collective-permute-start.1 = (bf16[3,64,128]{2,1,0:T(8,128)(2,1)S(1)}, bf16[3,64,128]{2,1,0:T(8,128)(2,1)S(1)}, u32[]{:S(2)}, u32[]{:S(2)}) collective-permute-start(bf16[3,64,128]{2,1,0:T(8,128)(2,1)S(1)} %get-tuple-element.29), channel_id=1, source_target_pairs={{1,0},{2,1},{3,2},{4,3},{5,4},{6,5},{7,6},{8,7},{9,8},{10,9},{11,1... | collective-permute-start | bytes 147464 | tf_op jit(solution)/shard_map/ppermute | solution.py:403
  10.7 0.0 collective-permute-done.south_ref
  10.7 3.5 %collective-permute-done.1.north_ref = bf16[3,64,128]{2,1,0:T(8,128)(2,1)S(1)} collective-permute-done((bf16[3,64,128]{2,1,0:T(8,128)(2,1)S(1)}, bf16[3,64,128]{2,1,0:T(8,128)(2,1)S(1)}, u32[]{:S(2)}, u32[]{:S(2)}) %collective-permute-start.1) | collective-permute-done | bytes 49184 | tf_op jit(solution)/shard_map/ppermute | solution.py:403
  14.2 0.1 strips.2
  14.3 13.6 %collective-permute-start.2 = (bf16[2,3,72,128]{3,2,1,0:T(8,128)(2,1)S(1)}, bf16[2,3,72,128]{3,2,1,0:T(8,128)(2,1)S(1)}, u32[]{:S(2)}, u32[]{:S(2)}) collective-permute-start(bf16[2,3,72,128]{3,2,1,0:T(8,128)(2,1)S(1)} %strips.2), channel_id=1, source_target_pairs={{0,16},{16,0},{32,48},{48,32},{64,80},{80,64},{96,112},{112,96},{1... | collective-permute-start | bytes 331784 | tf_op jit(solution)/shard_map/ppermute | solution.py:423
  28.0 9.8 %collective-permute-done.2 = bf16[2,3,72,128]{3,2,1,0:T(8,128)(2,1)S(1)} collective-permute-done((bf16[2,3,72,128]{3,2,1,0:T(8,128)(2,1)S(1)}, bf16[2,3,72,128]{3,2,1,0:T(8,128)(2,1)S(1)}, u32[]{:S(2)}, u32[]{:S(2)}) %collective-permute-start.2) | collective-permute-done | bytes 110624 | tf_op jit(solution)/shard_map/ppermute | solution.py:423
  37.8 3.2 %collective-permute-start.3 = (bf16[3,72,128]{2,1,0:T(8,128)(2,1)S(1)}, bf16[3,72,128]{2,1,0:T(8,128)(2,1)S(1)}, u32[]{:S(2)}, u32[]{:S(2)}) collective-permute-start(bf16[3,72,128]{2,1,0:T(8,128)(2,1)S(1)} %get-tuple-element.48), channel_id=1, source_target_pairs={{0,32},{32,64},{64,96},{96,128},{128,160},{160,192},{192,224},{224... | collective-permute-start | bytes 165896 | tf_op jit(solution)/shard_map/ppermute | solution.py:424
  41.0 0.0 copy-done.3
  41.0 6.6 %conv.1 = (f32[4096,128]{1,0:T(8,128)S(1)}, f32[8064,128]{1,0:T(8,128)S(1)}) custom-call(bf16[3,64,128]{2,1,0:T(8,128)(2,1)S(1)} %collective-permute-done.south_ref, bf16[64,64,128]{2,1,0:T(8,128)(2,1)S(1)} %get-tuple-element.28.block_ref, bf16[3,64,128]{2,1,0:T(8,128)(2,1)S(1)} %collective-permute-done.1.north_ref, f32[7,7,128]{2,1,0:T(8,128)S(1)} %copy-done.3), custom_call_target="tpu_custom_call" | custom-call | tf_op jit(solution)/shard_map/conv/pallas_call | solution.py:433
  47.6 0.0 copy-start.4
  47.7 0.0 copy-start.5
  47.7 0.0 copy-start.7
  47.7 0.0 copy-start.8
  47.7 0.0 copy-start.9
  47.7 0.0 copy-start.10
  47.7 4.2 %rest.1.conv_in = f32[4096,128]{1,0:T(8,128)S(1)} custom-call(f32[4096,128]{1,0:T(8,128)S(1)} %get-tuple-element.30.conv_in, f32[8064,128]{1,0:T(8,128)S(1)} %get-tuple-element.31.tiles_ref.tiles_in, f32[7,7,128]{2,1,0:T(8,128)S(1)} %copy-done.3), custom_call_target="tpu_custom_call", output_to_operand_aliasing={{}: (0, {})} | custom-call | tf_op jit(solution)/shard_map/rest/pallas_call | solution.py:445
  51.9 0.0 collective-permute-done.3.got_ref
  51.9 0.0 copy-done.4
  51.9 0.0 copy-done.5
  51.9 0.0 copy-done.7
  51.9 0.0 copy-done.8
  51.9 0.0 copy-done.9
  51.9 0.0 copy-done.10
  52.0 18.9 %block.1 = (f32[4096,128]{1,0:T(8,128)S(1)}, f32[8064,128]{1,0:T(8,128)S(1)}, bf16[64,64,128]{2,1,0:T(8,128)(2,1)S(1)}, bf16[3,64,128]{2,1,0:T(8,128)(2,1)S(1)},...) custom-call(s32[1]{0:T(128)} %bitcast.even_ref, ...), custom_call_target="tpu_custom_call", output_to_operand_aliasing={{0}: (1, {}), {1}: (2, {})} | custom-call | tf_op jit(solution)/shard_map/block/pallas_call | solution.py:480
  70.9 16.3 %all_to_all.15.parts_ref = bf16[32,40,128]{2,1,0:T(8,128)(2,1)S(1)} all-to-all(bf16[32,40,128]{2,1,0:T(8,128)(2,1)S(1)} %get-tuple-element.38), channel_id=1, replica_groups={{0,1,32,33,64,65,96,97,128,129,160,161,192,193,224,225,256,257,288,289,..., dimensions={0} | all-to-all | bytes 655360 | tf_op jit(solution)/shard_map/all_to_all | solution.py:374
  87.2 0.7 fold.2
  88.0 12.6 %all-to-all-start.1 = ((bf16[16,40,128]{2,1,0:T(8,128)(2,1)}), bf16[16,40,128]{2,1,0:T(8,128)(2,1)S(1)}, u32[]{:S(2)}, u32[]{:S(2)}) async-start(bf16[16,40,128]{2,1,0:T(8,128)(2,1)} %fold.2), calls=%async_computation.1 | async-start | bytes 327680 | tf_op jit(solution)/shard_map/all_to_all | solution.py:374
  100.6 3.6 %collective-permute-start.4 = (bf16[3,64,128]{2,1,0:T(8,128)(2,1)S(1)}, bf16[3,64,128]{2,1,0:T(8,128)(2,1)S(1)}, u32[]{:S(2)}, u32[]{:S(2)}) collective-permute-start(bf16[3,64,128]{2,1,0:T(8,128)(2,1)S(1)} %get-tuple-element.33), channel_id=1, source_target_pairs={{0,1},{1,2},{2,3},{3,4},{4,5},{5,6},{6,7},{7,8},{8,9},{9,10},{10,1... | collective-permute-start | bytes 147464 | tf_op jit(solution)/shard_map/ppermute | solution.py:402
  104.2 1.9 %collective-permute-start.5 = (bf16[3,64,128]{2,1,0:T(8,128)(2,1)S(1)}, bf16[3,64,128]{2,1,0:T(8,128)(2,1)S(1)}, u32[]{:S(2)}, u32[]{:S(2)}) collective-permute-start(bf16[3,64,128]{2,1,0:T(8,128)(2,1)S(1)} %get-tuple-element.35), channel_id=1, source_target_pairs={{1,0},{2,1},{3,2},{4,3},{5,4},{6,5},{7,6},{8,7},{9,8},{10,9},{11,1... | collective-permute-start | bytes 147464 | tf_op jit(solution)/shard_map/ppermute | solution.py:403
  106.2 0.4 collective-permute-done.4.south_ref
  106.5 4.0 %collective-permute-done.5.north_ref = bf16[3,64,128]{2,1,0:T(8,128)(2,1)S(1)} collective-permute-done((bf16[3,64,128]{2,1,0:T(8,128)(2,1)S(1)}, bf16[3,64,128]{2,1,0:T(8,128)(2,1)S(1)}, u32[]{:S(2)}, u32[]{:S(2)}) %collective-permute-start.5) | collective-permute-done | bytes 49184 | tf_op jit(solution)/shard_map/ppermute | solution.py:403
  110.5 0.1 strips.3
  110.6 10.3 %collective-permute-start.6 = (bf16[2,3,72,128]{3,2,1,0:T(8,128)(2,1)S(1)}, bf16[2,3,72,128]{3,2,1,0:T(8,128)(2,1)S(1)}, u32[]{:S(2)}, u32[]{:S(2)}) collective-permute-start(bf16[2,3,72,128]{3,2,1,0:T(8,128)(2,1)S(1)} %strips.3), channel_id=1, source_target_pairs={{0,16},{16,0},{32,48},{48,32},{64,80},{80,64},{96,112},{112,96},{1... | collective-permute-start | bytes 331784 | tf_op jit(solution)/shard_map/ppermute | solution.py:423
  120.9 0.0 all-to-all-done.1.parts_ref
  120.9 0.8 fold.3
  121.7 5.1 %all-to-all-start.2 = ((bf16[32,40,128]{2,1,0:T(8,128)(2,1)}), bf16[32,40,128]{2,1,0:T(8,128)(2,1)S(1)}, u32[]{:S(2)}, u32[]{:S(2)}) async-start(bf16[32,40,128]{2,1,0:T(8,128)(2,1)} %fold.3), calls=%async_computation.2 | async-start | bytes 655360 | tf_op jit(solution)/shard_map/all_to_all | solution.py:374
  126.8 6.0 %collective-permute-done.6 = bf16[2,3,72,128]{3,2,1,0:T(8,128)(2,1)S(1)} collective-permute-done((bf16[2,3,72,128]{3,2,1,0:T(8,128)(2,1)S(1)}, bf16[2,3,72,128]{3,2,1,0:T(8,128)(2,1)S(1)}, u32[]{:S(2)}, u32[]{:S(2)}) %collective-permute-start.6) | collective-permute-done | bytes 110624 | tf_op jit(solution)/shard_map/ppermute | solution.py:423
  132.8 1.9 %collective-permute-start.7 = (bf16[3,72,128]{2,1,0:T(8,128)(2,1)S(1)}, bf16[3,72,128]{2,1,0:T(8,128)(2,1)S(1)}, u32[]{:S(2)}, u32[]{:S(2)}) collective-permute-start(bf16[3,72,128]{2,1,0:T(8,128)(2,1)S(1)} %get-tuple-element.46), channel_id=1, source_target_pairs={{0,32},{32,64},{64,96},{96,128},{128,160},{160,192},{192,224},{224... | collective-permute-start | bytes 165896 | tf_op jit(solution)/shard_map/ppermute | solution.py:424
  134.8 5.2 %back_conv.1.spread_in = f32[4096,128]{1,0:T(8,128)S(1)} custom-call(bf16[3,64,128]{2,1,0:T(8,128)(2,1)S(1)} %collective-permute-done.4.south_ref, bf16[64,64,128]{2,1,0:T(8,128)(2,1)S(1)} %get-tuple-element.34.block_ref, bf16[3,64,128]{2,1,0:T(8,128)(2,1)S(1)} %collective-permute-done.5.north_ref, f32[7,7,128]{2,1,0:T(8,128)S(1)} %copy-done.3), custom_call_target="tpu_custom_call" | custom-call | tf_op jit(solution)/shard_map/back_conv/pallas_call | solution.py:433
  139.9 0.0 copy-start.1
  139.9 5.8 %back_rest.1.spread_in = f32[4096,128]{1,0:T(8,128)S(1)} custom-call(f32[4096,128]{1,0:T(8,128)S(1)} %back_conv.1.spread_in, bf16[64,64,128]{2,1,0:T(8,128)(2,1)S(1)} %get-tuple-element.34.block_ref, bf16[3,64,128]{2,1,0:T(8,128)(2,1)S(1)} %collective-permute-done.5.north_ref, f32[7,7,128]{2,1,0:T(8,128)S(1)} %copy-done.3), custom_call_target="tpu_custom_call", output_to_operand_aliasing={{}: (0, {})} | custom-call | tf_op jit(solution)/shard_map/back_rest/pallas_call | solution.py:515
  145.7 0.0 collective-permute-done.7.got_ref
  145.8 0.0 copy-done.1
  145.8 2.2 %back.1 = (f32[4096,128]{1,0:T(8,128)S(1)}, bf16[64,64,128]{2,1,0:T(8,128)(2,1)}) custom-call(s32[1]{0:T(128)} %bitcast.even_ref, f32[4096,128]{1,0:T(8,128)S(1)} %back_rest.1.spread_in, bf16[3,72,128]{2,1,0:T(8,128)(2,1)S(1)} %get-tuple-element.47.keep_ref, bf16[3,72,128]{2,1,0:T(8,128)(2,1)S(1)} %collective-permute-done.7.got_ref, ...), custom_call_target="tpu_custom_call", output_to_operand_aliasing={{0}: (1, {})} | custom-call | tf_op jit(solution)/shard_map/back/pallas_call | solution.py:528
  148.0 0.0 all-to-all-done.2.all_ref
  148.0 0.9 unpack.1
  (2 shorter events, 0.0 us)
Async XLA Ops:
  0.6 1.2 copy-start
  1.9 1.2 copy-start.2
  3.1 0.8 copy-start.6
  3.8 37.1 %copy-start.3 = (f32[7,7,128]{2,1,0:T(8,128)S(1)}, f32[7,7,128]{2,1,0:T(8,128)}, u32[]{:S(2)}) copy-start(f32[7,7,128]{2,1,0:T(8,128)} %kernel_ref.11) | copy-start | bytes 75268
  4.7 6.1 %collective-permute-start = (bf16[3,64,128]{2,1,0:T(8,128)(2,1)S(1)}, bf16[3,64,128]{2,1,0:T(8,128)(2,1)S(1)}, u32[]{:S(2)}, u32[]{:S(2)}) collective-permute-start(bf16[3,64,128]{2,1,0:T(8,128)(2,1)S(1)} %get-tuple-element.27), channel_id=1, source_target_pairs={{0,1},{1,2},{2,3},{3,4},{4,5},{5,6},{6,7},{7,8},{8,9},{9,10},{10,1... | collective-permute-start | bytes 147464 | tf_op jit(solution)/shard_map/ppermute | solution.py:402
  8.8 5.4 %collective-permute-start.1 = (bf16[3,64,128]{2,1,0:T(8,128)(2,1)S(1)}, bf16[3,64,128]{2,1,0:T(8,128)(2,1)S(1)}, u32[]{:S(2)}, u32[]{:S(2)}) collective-permute-start(bf16[3,64,128]{2,1,0:T(8,128)(2,1)S(1)} %get-tuple-element.29), channel_id=1, source_target_pairs={{1,0},{2,1},{3,2},{4,3},{5,4},{6,5},{7,6},{8,7},{9,8},{10,9},{11,1... | collective-permute-start | bytes 147464 | tf_op jit(solution)/shard_map/ppermute | solution.py:403
  14.3 23.4 %collective-permute-start.2 = (bf16[2,3,72,128]{3,2,1,0:T(8,128)(2,1)S(1)}, bf16[2,3,72,128]{3,2,1,0:T(8,128)(2,1)S(1)}, u32[]{:S(2)}, u32[]{:S(2)}) collective-permute-start(bf16[2,3,72,128]{3,2,1,0:T(8,128)(2,1)S(1)} %strips.2), channel_id=1, source_target_pairs={{0,16},{16,0},{32,48},{48,32},{64,80},{80,64},{96,112},{112,96},{1... | collective-permute-start | bytes 331784 | tf_op jit(solution)/shard_map/ppermute | solution.py:423
  37.8 14.1 %collective-permute-start.3 = (bf16[3,72,128]{2,1,0:T(8,128)(2,1)S(1)}, bf16[3,72,128]{2,1,0:T(8,128)(2,1)S(1)}, u32[]{:S(2)}, u32[]{:S(2)}) collective-permute-start(bf16[3,72,128]{2,1,0:T(8,128)(2,1)S(1)} %get-tuple-element.48), channel_id=1, source_target_pairs={{0,32},{32,64},{64,96},{96,128},{128,160},{160,192},{192,224},{224... | collective-permute-start | bytes 165896 | tf_op jit(solution)/shard_map/ppermute | solution.py:424
  47.6 4.3 %copy-start.4 = (bf16[128,512]{1,0:T(8,128)(2,1)S(1)}, bf16[128,512]{1,0:T(8,128)(2,1)}, u32[]{:S(2)}) copy-start(bf16[128,512]{1,0:T(8,128)(2,1)} %w_in_ref.1) | copy-start | bytes 393220
  47.7 4.3 %copy-start.5 = (bf16[512,128]{1,0:T(8,128)(2,1)S(1)}, bf16[512,128]{1,0:T(8,128)(2,1)}, u32[]{:S(2)}) copy-start(bf16[512,128]{1,0:T(8,128)(2,1)} %w_out_ref.1) | copy-start | bytes 393220
  47.7 4.3 %copy-start.7 = (f32[512]{0:T(512)S(1)}, f32[512]{0:T(512)}, u32[]{:S(2)}) copy-start(f32[512]{0:T(512)} %param.18) | copy-start | bytes 6148
  47.7 4.3 %copy-start.8 = (f32[128]{0:T(128)S(1)}, f32[128]{0:T(128)}, u32[]{:S(2)}) copy-start(f32[128]{0:T(128)} %param.14) | copy-start | bytes 1540
  47.7 4.3 %copy-start.9 = (f32[128]{0:T(128)S(1)}, f32[128]{0:T(128)}, u32[]{:S(2)}) copy-start(f32[128]{0:T(128)} %param.15) | copy-start | bytes 1540
  47.7 4.3 %copy-start.10 = (f32[128]{0:T(128)S(1)}, f32[128]{0:T(128)}, u32[]{:S(2)}) copy-start(f32[128]{0:T(128)} %param.16) | copy-start | bytes 1540
  88.0 32.9 %all-to-all-start.1 = ((bf16[16,40,128]{2,1,0:T(8,128)(2,1)}), bf16[16,40,128]{2,1,0:T(8,128)(2,1)S(1)}, u32[]{:S(2)}, u32[]{:S(2)}) async-start(bf16[16,40,128]{2,1,0:T(8,128)(2,1)} %fold.2), calls=%async_computation.1 | async-start | bytes 327680 | tf_op jit(solution)/shard_map/all_to_all | solution.py:374
  100.6 5.9 %collective-permute-start.4 = (bf16[3,64,128]{2,1,0:T(8,128)(2,1)S(1)}, bf16[3,64,128]{2,1,0:T(8,128)(2,1)S(1)}, u32[]{:S(2)}, u32[]{:S(2)}) collective-permute-start(bf16[3,64,128]{2,1,0:T(8,128)(2,1)S(1)} %get-tuple-element.33), channel_id=1, source_target_pairs={{0,1},{1,2},{2,3},{3,4},{4,5},{5,6},{6,7},{7,8},{8,9},{9,10},{10,1... | collective-permute-start | bytes 147464 | tf_op jit(solution)/shard_map/ppermute | solution.py:402
  104.2 6.3 %collective-permute-start.5 = (bf16[3,64,128]{2,1,0:T(8,128)(2,1)S(1)}, bf16[3,64,128]{2,1,0:T(8,128)(2,1)S(1)}, u32[]{:S(2)}, u32[]{:S(2)}) collective-permute-start(bf16[3,64,128]{2,1,0:T(8,128)(2,1)S(1)} %get-tuple-element.35), channel_id=1, source_target_pairs={{1,0},{2,1},{3,2},{4,3},{5,4},{6,5},{7,6},{8,7},{9,8},{10,9},{11,1... | collective-permute-start | bytes 147464 | tf_op jit(solution)/shard_map/ppermute | solution.py:403
  110.6 22.2 %collective-permute-start.6 = (bf16[2,3,72,128]{3,2,1,0:T(8,128)(2,1)S(1)}, bf16[2,3,72,128]{3,2,1,0:T(8,128)(2,1)S(1)}, u32[]{:S(2)}, u32[]{:S(2)}) collective-permute-start(bf16[2,3,72,128]{3,2,1,0:T(8,128)(2,1)S(1)} %strips.3), channel_id=1, source_target_pairs={{0,16},{16,0},{32,48},{48,32},{64,80},{80,64},{96,112},{112,96},{1... | collective-permute-start | bytes 331784 | tf_op jit(solution)/shard_map/ppermute | solution.py:423
  121.7 26.3 %all-to-all-start.2 = ((bf16[32,40,128]{2,1,0:T(8,128)(2,1)}), bf16[32,40,128]{2,1,0:T(8,128)(2,1)S(1)}, u32[]{:S(2)}, u32[]{:S(2)}) async-start(bf16[32,40,128]{2,1,0:T(8,128)(2,1)} %fold.3), calls=%async_computation.2 | async-start | bytes 655360 | tf_op jit(solution)/shard_map/all_to_all | solution.py:374
  132.8 12.9 %collective-permute-start.7 = (bf16[3,72,128]{2,1,0:T(8,128)(2,1)S(1)}, bf16[3,72,128]{2,1,0:T(8,128)(2,1)S(1)}, u32[]{:S(2)}, u32[]{:S(2)}) collective-permute-start(bf16[3,72,128]{2,1,0:T(8,128)(2,1)S(1)} %get-tuple-element.46), channel_id=1, source_target_pairs={{0,32},{32,64},{64,96},{96,128},{128,160},{160,192},{192,224},{224... | collective-permute-start | bytes 165896 | tf_op jit(solution)/shard_map/ppermute | solution.py:424
  139.9 5.9 %copy-start.1 = (bf16[64,64,128]{2,1,0:T(8,128)(2,1)S(1)}, bf16[64,64,128]{2,1,0:T(8,128)(2,1)}, u32[]{:S(2)}) copy-start(bf16[64,64,128]{2,1,0:T(8,128)(2,1)} %cot_ref.3) | copy-start | bytes 3145732

commit v8 on v7

--- a/solution.py
+++ b/solution.py
@@ -17,6 +17,7 @@
 CUBE = 0.044715
 VMEM = pl.BlockSpec(memory_space=pltpu.VMEM)
 PARAMS = pltpu.CompilerParams(vmem_limit_bytes=28 << 20)
+CONV_PARAMS = pltpu.CompilerParams(vmem_limit_bytes=28 << 20)
 SMEM = pl.BlockSpec(memory_space=pltpu.SMEM)
 
 
@@ -56,25 +57,32 @@
 
 
 def conv_rows(tiles_ref, kernel_ref, out_ref, start, stop, flip, base=0):
-    def one(row, _):
-        total = [None] * SUB
-        for a in range(KS):
-            cells = [tile(tiles_ref, row + a - base, t) for t in range(WIDE)]
-            for b in range(KS):
-                weight = tap_weight(kernel_ref, a, b, flip)
-                for t in range(SUB):
-                    term = weight * cells[t + b]
-                    total[t] = term if total[t] is None else total[t] + term
-        for t in range(SUB):
-            out_ref[pl.ds(row * 64 + t * SUB, SUB), :] = total[t]
+    def one(step, _):
+        first = start + 2 * step
+        totals = [[None] * SUB, [None] * SUB]
+        for near in range(KS + 1):
+            cells = [tile(tiles_ref, first + near - base, t) for t in range(WIDE)]
+            for r in range(2):
+                a = near - r
+                if not 0 <= a < KS:
+                    continue
+                total = totals[r]
+                for b in range(KS):
+                    weight = tap_weight(kernel_ref, a, b, flip)
+                    for t in range(SUB):
+                        term = weight * cells[t + b]
+                        total[t] = term if total[t] is None else total[t] + term
+        for r in range(2):
+            for t in range(SUB):
+                out_ref[pl.ds((first + r) * 64 + t * SUB, SUB), :] = totals[r][t]
         return 0
 
-    lax.fori_loop(start, stop, one, 0)
+    lax.fori_loop(0, (stop - start) // 2, one, 0)
 
 
 def edge_columns(even, keep_ref, got_ref, cols_ref):
     for c in range(HALF):
-        keep = keep_ref[c].astype(jnp.float32)
+        keep = keep_ref[0, c].astype(jnp.float32)
         got = got_ref[c].astype(jnp.float32)
         cols_ref[c] = jnp.where(even, got, keep)
         cols_ref[HALF + c] = jnp.where(even, keep, got)
@@ -105,16 +113,8 @@
     return buf_ref[0 : SUB * SUB, :]
 
 
-def mask_kernel(cells_ref, mask_ref, cot_ref, masked_ref, out_grad_ref, ocean_ref, top_ref, bottom_ref):
-    height = cells_ref.shape[0]
-    columns = mask_ref[...].astype(jnp.float32).T
-    for row in range(height):
-        ocean = jnp.broadcast_to(columns[:, row : row + 1], cells_ref.shape[1:])
-        masked_ref[row] = (cells_ref[row].astype(jnp.float32) * ocean).astype(jnp.bfloat16)
-        out_grad_ref[row] = (cot_ref[row].astype(jnp.float32) * ocean).astype(jnp.bfloat16)
-        ocean_ref[row] = ocean.astype(jnp.bfloat16)
-    top_ref[...] = masked_ref[height - HALF :]
-    bottom_ref[...] = masked_ref[0:HALF]
+def onward_kernel(both_ref, out_ref):
+    out_ref[...] = both_ref[1]
 
 
 def strip_kernel(even_ref, south_ref, block_ref, north_ref, out_ref, low_ref, high_ref):
@@ -421,8 +421,16 @@
         compiler_params=PARAMS,
     )(even, south, block, north)
     swapped = lax.ppermute(strips, "lon", [(i, i ^ 1) for i in range(lax.axis_size("lon"))])
-    got = lax.ppermute(swapped[1], "lon", onward_pairs())
-    return swapped[0], got
+    onward = pl.pallas_call(
+        onward_kernel,
+        out_shape=jax.ShapeDtypeStruct(swapped.shape[1:], jnp.bfloat16),
+        in_specs=[VMEM],
+        out_specs=VMEM,
+        compiler_params=PARAMS,
+        name="onward",
+    )(swapped)
+    got = lax.ppermute(onward, "lon", onward_pairs())
+    return swapped, got
 
 
 def first_conv(south, block, north, kernel, rows, flip):
@@ -436,7 +444,7 @@
         in_specs=[VMEM] * 4,
         out_specs=VMEM if flip else [VMEM] * 2,
         scratch_shapes=[tiles, buf] if flip else [buf],
-        compiler_params=PARAMS,
+        compiler_params=CONV_PARAMS,
         name="back_conv" if flip else "conv",
     )(south, block, north, kernel)
 
@@ -448,7 +456,7 @@
         in_specs=[VMEM] * 3,
         out_specs=VMEM,
         input_output_aliases={0: 0},
-        compiler_params=PARAMS,
+        compiler_params=CONV_PARAMS,
         name="back_rest" if flip else "rest",
     )(*[pltpu.with_memory_space_constraint(x, pltpu.VMEM) for x in (conv, tiles)], kernel)
 
@@ -459,18 +467,12 @@
 
 def body(cells, ocean_mask, cotangent, kernel, conv_bias, gain, shift, w_in, b_in, w_out, chunk=8):
     height, across, channels = cells.shape
-    whole = jax.ShapeDtypeStruct(cells.shape, jnp.bfloat16)
+    ocean = jnp.broadcast_to(ocean_mask.astype(jnp.bfloat16)[..., None], cells.shape)
+    masked = cells * ocean
+    out_grad = cotangent * ocean
     strip = jax.ShapeDtypeStruct((HALF, across, channels), jnp.bfloat16)
-    masked, out_grad, ocean, top, bottom = pl.pallas_call(
-        mask_kernel,
-        out_shape=(whole, whole, whole, strip, strip),
-        in_specs=[VMEM] * 3,
-        out_specs=[VMEM] * 5,
-        compiler_params=PARAMS,
-        name="mask",
-    )(cells, ocean_mask, cotangent)
     even = (1 - lax.axis_index("lon") % 2).astype(jnp.int32).reshape(1)
-    south, north = lat_halo(top, bottom)
+    south, north = lat_halo(masked[-HALF:], masked[:HALF])
     keep, got = lon_halo(even, south, masked, north)
     early = height * 9 // 16
     conv, tiles = first_conv(south, masked, north, kernel, early, False)
@@ -510,7 +512,7 @@
     total = summed(packed)
     south, north = lat_halo(top, bottom)
     keep, got = lon_halo(even, south, conv_grad, north)
-    half = height * 15 // 32
+    half = height * 9 // 16
     spread = first_conv(south, conv_grad, north, kernel, half, True)
     spread = pl.pallas_call(
         functools.partial(back_rest_kernel, half),
@@ -522,7 +524,7 @@
             pltpu.VMEM((SUB * SUB + 2 * SUB, channels), jnp.float32),
         ],
         input_output_aliases={0: 0},
-        compiler_params=PARAMS,
+        compiler_params=CONV_PARAMS,
         name="back_rest",
     )(pltpu.with_memory_space_constraint(spread, pltpu.VMEM), conv_grad, north, kernel)
     _, cells_grad = pl.pallas_call(

time: 149 us -> 164 us (1.10)
  the two profiles are of different devices: /device:TPU:33 before, /device:TPU:103 now
where the time goes in v8:
time: 164 us; the launch traced here: 163 us
  Pallas kernels  43.5 us (27%)
  starting transfers between devices  42.7 us (26%)
  blocking collectives  41.9 us (26%)
  waiting for transfers between devices  31 us (19%)
  other arithmetic  2.68 us (2%)
    all_to_all x2, blocking collectives, exchange(): lax.all_to_all(parts, ('lon', 'lat'), 0, 0, tiled=True, axis_index_groups...  41.9 us
    ppermute x2, waiting for transfers between devices, lon_halo(): lax.ppermute(strips, 'lon', [(i, i ^ 1) for i in range(lax.axis_size('lon...  21.7 us
    pallas_call x1, Pallas kernels, body(): pl.pallas_call(functools.partial(block_kernel, chunk), out_shape=(pltpu.V...  19.4 us
    ppermute x2, starting transfers between devices, lon_halo(): lax.ppermute(strips, 'lon', [(i, i ^ 1) for i in range(lax.axis_size('lon...  17.5 us
    pallas_call x2, Pallas kernels, first_conv(): pl.pallas_call(functools.partial(conv_kernel, rows, flip), out_shape=out...  11.8 us
    ppermute x2, waiting for transfers between devices, lat_halo(): north = lax.ppermute(bottom, 'lat', down)  9.35 us
    ppermute x2, starting transfers between devices, lat_halo(): south = lax.ppermute(top, 'lat', up)  7.94 us
    all_to_all x1, starting transfers between devices, exchange(): lax.all_to_all(parts, ('lon', 'lat'), 0, 0, tiled=True, axis_index_groups...  7.13 us
  transfers between devices with their start and end apart: 9, of which 4 were waited for; matrix products, arithmetic and copies ran while one was open for 0% of the time, Pallas kernels for 14%

profile of v8, /device:TPU:103, one launch (start us, length us, event | category | flops | bytes accessed | tf_op | source)
XLA Modules:
  0.0 163.4 jit_solution(9163616798303636794)
XLA Ops:
  0.6 0.8 convert_element_type.3
  1.4 0.0 copy-start.1
  1.4 1.9 %broadcast_multiply_fusion = (bf16[64,64,128]{2,1,0:T(8,128)(2,1)S(1)}, bf16[64,64,128]{2,1,0:T(8,128)(2,1)S(1)}) fusion(bf16[64,64,128]{2,1,0:T(8,128)(2,1)} %cot_ref.1, bf16[64,64]{1,0:T(8,128)(2,1)S(1)} %convert_element_type.3, bf16[64,64,128]{2,1,0:T(8,128)(2,1)} %param.10), kind=kLoop, calls=%fused_computation | loop fusion | flops 1048576 | bytes 4202496 | tf_op jit(solution)/shard_map/mul | solution.py:472
  3.3 5.3 %collective-permute-start = (bf16[3,64,128]{2,1,0:T(8,128)(2,1)S(1)}, bf16[3,64,128]{2,1,0:T(8,128)(2,1)S(1)}, u32[]{:S(2)}, u32[]{:S(2)}) collective-permute-start(bf16[3,64,128]{2,1,0:T(8,128)(2,1)S(1)} %get-tuple-element.37), channel_id=1, source_target_pairs={{0,1},{1,2},{2,3},{3,4},{4,5},{5,6},{6,7},{7,8},{8,9},{9,10},{10,1... | collective-permute-start | bytes 147464 | tf_op jit(solution)/shard_map/ppermute | solution.py:402
  8.7 1.9 %collective-permute-start.1 = (bf16[3,64,128]{2,1,0:T(8,128)(2,1)S(1)}, bf16[3,64,128]{2,1,0:T(8,128)(2,1)S(1)}, u32[]{:S(2)}, u32[]{:S(2)}) collective-permute-start(bf16[3,64,128]{2,1,0:T(8,128)(2,1)S(1)} %get-tuple-element.36), channel_id=1, source_target_pairs={{1,0},{2,1},{3,2},{4,3},{5,4},{6,5},{7,6},{8,7},{9,8},{10,9},{11,1... | collective-permute-start | bytes 147464 | tf_op jit(solution)/shard_map/ppermute | solution.py:403
  10.6 0.0 collective-permute-done.south_ref
  10.6 4.7 %collective-permute-done.1.north_ref = bf16[3,64,128]{2,1,0:T(8,128)(2,1)S(1)} collective-permute-done((bf16[3,64,128]{2,1,0:T(8,128)(2,1)S(1)}, bf16[3,64,128]{2,1,0:T(8,128)(2,1)S(1)}, u32[]{:S(2)}, u32[]{:S(2)}) %collective-permute-start.1) | collective-permute-done | bytes 49184 | tf_op jit(solution)/shard_map/ppermute | solution.py:403
  15.3 0.1 strips.2
  15.4 10.6 %collective-permute-start.2 = (bf16[2,3,72,128]{3,2,1,0:T(8,128)(2,1)S(1)}, bf16[2,3,72,128]{3,2,1,0:T(8,128)(2,1)S(1)}, u32[]{:S(2)}, u32[]{:S(2)}) collective-permute-start(bf16[2,3,72,128]{3,2,1,0:T(8,128)(2,1)S(1)} %strips.2), channel_id=1, source_target_pairs={{0,16},{16,0},{32,48},{48,32},{64,80},{80,64},{96,112},{112,96},{1... | collective-permute-start | bytes 331784 | tf_op jit(solution)/shard_map/ppermute | solution.py:423
  26.0 8.3 %collective-permute-done.2.both_ref.keep_ref = bf16[2,3,72,128]{3,2,1,0:T(8,128)(2,1)S(1)} collective-permute-done((bf16[2,3,72,128]{3,2,1,0:T(8,128)(2,1)S(1)}, bf16[2,3,72,128]{3,2,1,0:T(8,128)(2,1)S(1)}, u32[]{:S(2)}, u32[]{:S(2)}) %collective-permute-start.2) | collective-permute-done | bytes 110624 | tf_op jit(solution)/shard_map/ppermute | solution.py:423
  34.3 3.2 %collective-permute-start.3 = (bf16[3,72,128]{2,1,0:T(8,128)(2,1)S(1)}, bf16[3,72,128]{2,1,0:T(8,128)(2,1)S(1)}, u32[]{:S(2)}, u32[]{:S(2)}) collective-permute-start(bf16[3,72,128]{2,1,0:T(8,128)(2,1)S(1)} %onward.2), channel_id=1, source_target_pairs={{0,32},{32,64},{64,96},{96,128},{128,160},{160,192},{192,224},{224... | collective-permute-start | bytes 165896 | tf_op jit(solution)/shard_map/ppermute | solution.py:432
  37.5 0.0 copy-done.1
  37.6 6.4 %conv.1 = (f32[4096,128]{1,0:T(8,128)S(1)}, f32[8064,128]{1,0:T(8,128)S(1)}) custom-call(bf16[3,64,128]{2,1,0:T(8,128)(2,1)S(1)} %collective-permute-done.south_ref, bf16[64,64,128]{2,1,0:T(8,128)(2,1)S(1)} %get-tuple-element.39.block_ref, bf16[3,64,128]{2,1,0:T(8,128)(2,1)S(1)} %collective-permute-done.1.north_ref, f32[7,7,128]{2,1,0:T(8,128)S(1)} %copy-done.1), custom_call_target="tpu_custom_call" | custom-call | tf_op jit(solution)/shard_map/conv/pallas_call | solution.py:441
  43.9 0.0 copy-start.2
  44.0 0.0 copy-start.3
  44.0 0.0 copy-start.4
  44.0 0.0 copy-start.5
  44.0 0.0 copy-start.6
  44.0 0.0 copy-start.7
  44.0 3.9 %rest.1.conv_in = f32[4096,128]{1,0:T(8,128)S(1)} custom-call(f32[4096,128]{1,0:T(8,128)S(1)} %get-tuple-element.22.conv_in, f32[8064,128]{1,0:T(8,128)S(1)} %get-tuple-element.23.tiles_ref.tiles_in, f32[7,7,128]{2,1,0:T(8,128)S(1)} %copy-done.1), custom_call_target="tpu_custom_call", output_to_operand_aliasing={{}: (0, {})} | custom-call | tf_op jit(solution)/shard_map/rest/pallas_call | solution.py:453
  48.0 0.0 collective-permute-done.3.got_ref
  48.0 0.0 copy-done.2
  48.0 0.0 copy-done.3
  48.0 0.0 copy-done.4
  48.0 0.0 copy-done.5
  48.0 0.0 copy-done.6
  48.0 0.0 copy-done.7
  48.0 19.4 %block.1 = (f32[4096,128]{1,0:T(8,128)S(1)}, f32[8064,128]{1,0:T(8,128)S(1)}, bf16[64,64,128]{2,1,0:T(8,128)(2,1)S(1)}, bf16[3,64,128]{2,1,0:T(8,128)(2,1)S(1)},...) custom-call(s32[1]{0:T(128)} %bitcast.even_ref, ...), custom_call_target="tpu_custom_call", output_to_operand_aliasing={{0}: (1, {}), {1}: (2, {})} | custom-call | tf_op jit(solution)/shard_map/block/pallas_call | solution.py:482
  67.5 14.6 %all_to_all.15.parts_ref = bf16[32,40,128]{2,1,0:T(8,128)(2,1)S(1)} all-to-all(bf16[32,40,128]{2,1,0:T(8,128)(2,1)S(1)} %get-tuple-element.28), channel_id=1, replica_groups={{0,1,32,33,64,65,96,97,128,129,160,161,192,193,224,225,256,257,288,289,..., dimensions={0} | all-to-all | bytes 655360 | tf_op jit(solution)/shard_map/all_to_all | solution.py:374
  82.1 0.1 fold.2
  82.2 27.3 %all_to_all.16.parts_ref = bf16[16,40,128]{2,1,0:T(8,128)(2,1)S(1)} all-to-all(bf16[16,40,128]{2,1,0:T(8,128)(2,1)S(1)} %fold.2), channel_id=1, replica_groups={{0,2,4,6,8,10,12,14,16,18,20,22,24,26,28,30},{1,3,5,7,9,11,13,15,17,19,..., dimensions={0} | all-to-all | bytes 327680 | tf_op jit(solution)/shard_map/all_to_all | solution.py:374
  109.5 0.8 fold.3
  110.2 7.1 %all-to-all-start.2 = ((bf16[32,40,128]{2,1,0:T(8,128)(2,1)}), bf16[32,40,128]{2,1,0:T(8,128)(2,1)S(1)}, u32[]{:S(2)}, u32[]{:S(2)}) async-start(bf16[32,40,128]{2,1,0:T(8,128)(2,1)} %fold.3), calls=%async_computation.2 | async-start | bytes 655360 | tf_op jit(solution)/shard_map/all_to_all | solution.py:374
  117.4 2.6 %collective-permute-start.4 = (bf16[3,64,128]{2,1,0:T(8,128)(2,1)S(1)}, bf16[3,64,128]{2,1,0:T(8,128)(2,1)S(1)}, u32[]{:S(2)}, u32[]{:S(2)}) collective-permute-start(bf16[3,64,128]{2,1,0:T(8,128)(2,1)S(1)} %get-tuple-element.24), channel_id=1, source_target_pairs={{0,1},{1,2},{2,3},{3,4},{4,5},{5,6},{6,7},{7,8},{8,9},{9,10},{10,1... | collective-permute-start | bytes 147464 | tf_op jit(solution)/shard_map/ppermute | solution.py:402
  120.0 1.9 %collective-permute-start.5 = (bf16[3,64,128]{2,1,0:T(8,128)(2,1)S(1)}, bf16[3,64,128]{2,1,0:T(8,128)(2,1)S(1)}, u32[]{:S(2)}, u32[]{:S(2)}) collective-permute-start(bf16[3,64,128]{2,1,0:T(8,128)(2,1)S(1)} %get-tuple-element.26), channel_id=1, source_target_pairs={{1,0},{2,1},{3,2},{4,3},{5,4},{6,5},{7,6},{8,7},{9,8},{10,9},{11,1... | collective-permute-start | bytes 147464 | tf_op jit(solution)/shard_map/ppermute | solution.py:403
  121.9 0.0 collective-permute-done.4.south_ref
  122.0 4.7 %collective-permute-done.5.north_ref = bf16[3,64,128]{2,1,0:T(8,128)(2,1)S(1)} collective-permute-done((bf16[3,64,128]{2,1,0:T(8,128)(2,1)S(1)}, bf16[3,64,128]{2,1,0:T(8,128)(2,1)S(1)}, u32[]{:S(2)}, u32[]{:S(2)}) %collective-permute-start.5) | collective-permute-done | bytes 49184 | tf_op jit(solution)/shard_map/ppermute | solution.py:403
  126.6 0.1 strips.3
  126.7 6.9 %collective-permute-start.6 = (bf16[2,3,72,128]{3,2,1,0:T(8,128)(2,1)S(1)}, bf16[2,3,72,128]{3,2,1,0:T(8,128)(2,1)S(1)}, u32[]{:S(2)}, u32[]{:S(2)}) collective-permute-start(bf16[2,3,72,128]{3,2,1,0:T(8,128)(2,1)S(1)} %strips.3), channel_id=1, source_target_pairs={{0,16},{16,0},{32,48},{48,32},{64,80},{80,64},{96,112},{112,96},{1... | collective-permute-start | bytes 331784 | tf_op jit(solution)/shard_map/ppermute | solution.py:423
  133.7 13.4 %collective-permute-done.6.both_ref.keep_ref = bf16[2,3,72,128]{3,2,1,0:T(8,128)(2,1)S(1)} collective-permute-done((bf16[2,3,72,128]{3,2,1,0:T(8,128)(2,1)S(1)}, bf16[2,3,72,128]{3,2,1,0:T(8,128)(2,1)S(1)}, u32[]{:S(2)}, u32[]{:S(2)}) %collective-permute-start.6) | collective-permute-done | bytes 110624 | tf_op jit(solution)/shard_map/ppermute | solution.py:423
  147.0 3.1 %collective-permute-start.7 = (bf16[3,72,128]{2,1,0:T(8,128)(2,1)S(1)}, bf16[3,72,128]{2,1,0:T(8,128)(2,1)S(1)}, u32[]{:S(2)}, u32[]{:S(2)}) collective-permute-start(bf16[3,72,128]{2,1,0:T(8,128)(2,1)S(1)} %onward.3), channel_id=1, source_target_pairs={{0,32},{32,64},{64,96},{96,128},{128,160},{160,192},{192,224},{224... | collective-permute-start | bytes 165896 | tf_op jit(solution)/shard_map/ppermute | solution.py:432
  150.1 5.4 %back_conv.1.spread_in = f32[4096,128]{1,0:T(8,128)S(1)} custom-call(bf16[3,64,128]{2,1,0:T(8,128)(2,1)S(1)} %collective-permute-done.4.south_ref, bf16[64,64,128]{2,1,0:T(8,128)(2,1)S(1)} %get-tuple-element.25.block_ref, bf16[3,64,128]{2,1,0:T(8,128)(2,1)S(1)} %collective-permute-done.5.north_ref, f32[7,7,128]{2,1,0:T(8,128)S(1)} %copy-done.1), custom_call_target="tpu_custom_call" | custom-call | tf_op jit(solution)/shard_map/back_conv/pallas_call | solution.py:441
  155.5 0.0 copy-start
  155.5 4.2 %back_rest.1.spread_in = f32[4096,128]{1,0:T(8,128)S(1)} custom-call(f32[4096,128]{1,0:T(8,128)S(1)} %back_conv.1.spread_in, bf16[64,64,128]{2,1,0:T(8,128)(2,1)S(1)} %get-tuple-element.25.block_ref, bf16[3,64,128]{2,1,0:T(8,128)(2,1)S(1)} %collective-permute-done.5.north_ref, f32[7,7,128]{2,1,0:T(8,128)S(1)} %copy-done.1), custom_call_target="tpu_custom_call", output_to_operand_aliasing={{}: (0, {})} | custom-call | tf_op jit(solution)/shard_map/back_rest/pallas_call | solution.py:517
  159.7 0.0 collective-permute-done.7.got_ref
  159.7 0.6 broadcast_in_dim.2.mask_ref
  160.3 0.0 copy-done
  160.3 2.3 %back.1 = (f32[4096,128]{1,0:T(8,128)S(1)}, bf16[64,64,128]{2,1,0:T(8,128)(2,1)}) custom-call(s32[1]{0:T(128)} %bitcast.even_ref, f32[4096,128]{1,0:T(8,128)S(1)} %back_rest.1.spread_in, bf16[2,3,72,128]{3,2,1,0:T(8,128)(2,1)S(1)} %collective-permute-done.6.both_ref.keep_ref, ...), custom_call_target="tpu_custom_call", output_to_operand_aliasing={{0}: (1, {})} | custom-call | tf_op jit(solution)/shard_map/back/pallas_call | solution.py:530
  162.6 0.0 all-to-all-done.2.all_ref
  162.6 0.9 unpack.1
  (3 shorter events, 0.0 us)
Async XLA Ops:
  1.4 36.2 %copy-start.1 = (f32[7,7,128]{2,1,0:T(8,128)S(1)}, f32[7,7,128]{2,1,0:T(8,128)}, u32[]{:S(2)}) copy-start(f32[7,7,128]{2,1,0:T(8,128)} %kernel_ref.11) | copy-start | bytes 75268
  3.3 7.3 %collective-permute-start = (bf16[3,64,128]{2,1,0:T(8,128)(2,1)S(1)}, bf16[3,64,128]{2,1,0:T(8,128)(2,1)S(1)}, u32[]{:S(2)}, u32[]{:S(2)}) collective-permute-start(bf16[3,64,128]{2,1,0:T(8,128)(2,1)S(1)} %get-tuple-element.37), channel_id=1, source_target_pairs={{0,1},{1,2},{2,3},{3,4},{4,5},{5,6},{6,7},{7,8},{8,9},{9,10},{10,1... | collective-permute-start | bytes 147464 | tf_op jit(solution)/shard_map/ppermute | solution.py:402
  8.7 6.6 %collective-permute-start.1 = (bf16[3,64,128]{2,1,0:T(8,128)(2,1)S(1)}, bf16[3,64,128]{2,1,0:T(8,128)(2,1)S(1)}, u32[]{:S(2)}, u32[]{:S(2)}) collective-permute-start(bf16[3,64,128]{2,1,0:T(8,128)(2,1)S(1)} %get-tuple-element.36), channel_id=1, source_target_pairs={{1,0},{2,1},{3,2},{4,3},{5,4},{6,5},{7,6},{8,7},{9,8},{10,9},{11,1... | collective-permute-start | bytes 147464 | tf_op jit(solution)/shard_map/ppermute | solution.py:403
  15.4 18.9 %collective-permute-start.2 = (bf16[2,3,72,128]{3,2,1,0:T(8,128)(2,1)S(1)}, bf16[2,3,72,128]{3,2,1,0:T(8,128)(2,1)S(1)}, u32[]{:S(2)}, u32[]{:S(2)}) collective-permute-start(bf16[2,3,72,128]{3,2,1,0:T(8,128)(2,1)S(1)} %strips.2), channel_id=1, source_target_pairs={{0,16},{16,0},{32,48},{48,32},{64,80},{80,64},{96,112},{112,96},{1... | collective-permute-start | bytes 331784 | tf_op jit(solution)/shard_map/ppermute | solution.py:423
  34.3 13.6 %collective-permute-start.3 = (bf16[3,72,128]{2,1,0:T(8,128)(2,1)S(1)}, bf16[3,72,128]{2,1,0:T(8,128)(2,1)S(1)}, u32[]{:S(2)}, u32[]{:S(2)}) collective-permute-start(bf16[3,72,128]{2,1,0:T(8,128)(2,1)S(1)} %onward.2), channel_id=1, source_target_pairs={{0,32},{32,64},{64,96},{96,128},{128,160},{160,192},{192,224},{224... | collective-permute-start | bytes 165896 | tf_op jit(solution)/shard_map/ppermute | solution.py:432
  43.9 4.0 %copy-start.2 = (bf16[128,512]{1,0:T(8,128)(2,1)S(1)}, bf16[128,512]{1,0:T(8,128)(2,1)}, u32[]{:S(2)}) copy-start(bf16[128,512]{1,0:T(8,128)(2,1)} %w_in_ref.1) | copy-start | bytes 393220
  44.0 4.0 %copy-start.3 = (bf16[512,128]{1,0:T(8,128)(2,1)S(1)}, bf16[512,128]{1,0:T(8,128)(2,1)}, u32[]{:S(2)}) copy-start(bf16[512,128]{1,0:T(8,128)(2,1)} %w_out_ref.1) | copy-start | bytes 393220
  44.0 4.0 %copy-start.4 = (f32[512]{0:T(512)S(1)}, f32[512]{0:T(512)}, u32[]{:S(2)}) copy-start(f32[512]{0:T(512)} %param.18) | copy-start | bytes 6148
  44.0 4.0 %copy-start.5 = (f32[128]{0:T(128)S(1)}, f32[128]{0:T(128)}, u32[]{:S(2)}) copy-start(f32[128]{0:T(128)} %param.14) | copy-start | bytes 1540
  44.0 4.0 %copy-start.6 = (f32[128]{0:T(128)S(1)}, f32[128]{0:T(128)}, u32[]{:S(2)}) copy-start(f32[128]{0:T(128)} %param.15) | copy-start | bytes 1540
  44.0 4.0 %copy-start.7 = (f32[128]{0:T(128)S(1)}, f32[128]{0:T(128)}, u32[]{:S(2)}) copy-start(f32[128]{0:T(128)} %param.16) | copy-start | bytes 1540
  110.2 52.3 %all-to-all-start.2 = ((bf16[32,40,128]{2,1,0:T(8,128)(2,1)}), bf16[32,40,128]{2,1,0:T(8,128)(2,1)S(1)}, u32[]{:S(2)}, u32[]{:S(2)}) async-start(bf16[32,40,128]{2,1,0:T(8,128)(2,1)} %fold.3), calls=%async_computation.2 | async-start | bytes 655360 | tf_op jit(solution)/shard_map/all_to_all | solution.py:374
  117.4 4.6 %collective-permute-start.4 = (bf16[3,64,128]{2,1,0:T(8,128)(2,1)S(1)}, bf16[3,64,128]{2,1,0:T(8,128)(2,1)S(1)}, u32[]{:S(2)}, u32[]{:S(2)}) collective-permute-start(bf16[3,64,128]{2,1,0:T(8,128)(2,1)S(1)} %get-tuple-element.24), channel_id=1, source_target_pairs={{0,1},{1,2},{2,3},{3,4},{4,5},{5,6},{6,7},{7,8},{8,9},{9,10},{10,1... | collective-permute-start | bytes 147464 | tf_op jit(solution)/shard_map/ppermute | solution.py:402
  120.0 6.6 %collective-permute-start.5 = (bf16[3,64,128]{2,1,0:T(8,128)(2,1)S(1)}, bf16[3,64,128]{2,1,0:T(8,128)(2,1)S(1)}, u32[]{:S(2)}, u32[]{:S(2)}) collective-permute-start(bf16[3,64,128]{2,1,0:T(8,128)(2,1)S(1)} %get-tuple-element.26), channel_id=1, source_target_pairs={{1,0},{2,1},{3,2},{4,3},{5,4},{6,5},{7,6},{8,7},{9,8},{10,9},{11,1... | collective-permute-start | bytes 147464 | tf_op jit(solution)/shard_map/ppermute | solution.py:403
  126.7 20.3 %collective-permute-start.6 = (bf16[2,3,72,128]{3,2,1,0:T(8,128)(2,1)S(1)}, bf16[2,3,72,128]{3,2,1,0:T(8,128)(2,1)S(1)}, u32[]{:S(2)}, u32[]{:S(2)}) collective-permute-start(bf16[2,3,72,128]{3,2,1,0:T(8,128)(2,1)S(1)} %strips.3), channel_id=1, source_target_pairs={{0,16},{16,0},{32,48},{48,32},{64,80},{80,64},{96,112},{112,96},{1... | collective-permute-start | bytes 331784 | tf_op jit(solution)/shard_map/ppermute | solution.py:423
  147.0 12.7 %collective-permute-start.7 = (bf16[3,72,128]{2,1,0:T(8,128)(2,1)S(1)}, bf16[3,72,128]{2,1,0:T(8,128)(2,1)S(1)}, u32[]{:S(2)}, u32[]{:S(2)}) collective-permute-start(bf16[3,72,128]{2,1,0:T(8,128)(2,1)S(1)} %onward.3), channel_id=1, source_target_pairs={{0,32},{32,64},{64,96},{96,128},{128,160},{160,192},{192,224},{224... | collective-permute-start | bytes 165896 | tf_op jit(solution)/shard_map/ppermute | solution.py:432
  155.5 4.8 %copy-start = (bf16[64,64,128]{2,1,0:T(8,128)(2,1)S(1)}, bf16[64,64,128]{2,1,0:T(8,128)(2,1)}, u32[]{:S(2)}) copy-start(bf16[64,64,128]{2,1,0:T(8,128)(2,1)} %cot_ref.1) | copy-start | bytes 3145732

commit v9 on v8

--- a/solution.py
+++ b/solution.py
@@ -150,23 +150,8 @@
     conv_rows(tiles_ref, kernel_ref, out_ref, start, out_ref.shape[0] // 64, flip)
 
 
-def back_rest_kernel(start, spread_in, block_ref, north_ref, kernel_ref, out_ref, tiles_ref, buf_ref):
-    del spread_in
-    height = block_ref.shape[0]
-    buf_ref[...] = jnp.zeros_like(buf_ref)
-
-    def one(row, _):
-        spread_row(block_ref[row], row + HALF - start, tiles_ref, buf_ref)
-        return 0
-
-    lax.fori_loop(start - HALF, height, one, 0)
-    for row in range(HALF):
-        spread_row(north_ref[row], height + HALF + row - start, tiles_ref, buf_ref)
-    conv_rows(tiles_ref, kernel_ref, out_ref, start, height, True, start)
-
-
 def conv_kernel(rows, flip, south_ref, block_ref, north_ref, kernel_ref, out_ref, tiles_ref, buf_ref):
-    spread_all(south_ref, block_ref, north_ref, tiles_ref, buf_ref, rows + HALF if flip else None)
+    spread_all(south_ref, block_ref, north_ref, tiles_ref, buf_ref, None)
     conv_rows(tiles_ref, kernel_ref, out_ref, 0, rows, flip)
 
 
@@ -512,21 +497,7 @@
     total = summed(packed)
     south, north = lat_halo(top, bottom)
     keep, got = lon_halo(even, south, conv_grad, north)
-    half = height * 9 // 16
-    spread = first_conv(south, conv_grad, north, kernel, half, True)
-    spread = pl.pallas_call(
-        functools.partial(back_rest_kernel, half),
-        out_shape=pltpu.VMEM(spread.shape, jnp.float32),
-        in_specs=[VMEM] * 4,
-        out_specs=VMEM,
-        scratch_shapes=[
-            pltpu.VMEM(((height + 2 * HALF - half) * WIDE * SUB, channels), jnp.float32),
-            pltpu.VMEM((SUB * SUB + 2 * SUB, channels), jnp.float32),
-        ],
-        input_output_aliases={0: 0},
-        compiler_params=CONV_PARAMS,
-        name="back_rest",
-    )(pltpu.with_memory_space_constraint(spread, pltpu.VMEM), conv_grad, north, kernel)
+    spread = first_conv(south, conv_grad, north, kernel, height, True)
     _, cells_grad = pl.pallas_call(
         back_kernel,
         out_shape=(pltpu.VMEM(spread.shape, jnp.float32), jax.ShapeDtypeStruct(cells.shape, jnp.bfloat16)),

time: 164 us -> 164 us (level)
    pallas_call x1 -> x0, Pallas kernels: 4.2 us -> none  [body(): pl.pallas_call(functools.partial(back_rest_kernel, half), out_shape=pltpu...]
    pallas_call x2, Pallas kernels: 11.8 us -> 15.8 us  [first_conv(): pl.pallas_call(functools.partial(conv_kernel, rows, flip), out_shape=out...]
where the time goes in v9:
time: 164 us; the launch traced here: 163 us
  Pallas kernels  43.4 us (26%)
  starting transfers between devices  42.9 us (26%)
  blocking collectives  41.9 us (26%)
  waiting for transfers between devices  31 us (19%)
  other arithmetic  2.68 us (2%)
    all_to_all x2, blocking collectives, exchange(): lax.all_to_all(parts, ('lon', 'lat'), 0, 0, tiled=True, axis_index_groups...  41.9 us
    ppermute x2, waiting for transfers between devices, lon_halo(): lax.ppermute(strips, 'lon', [(i, i ^ 1) for i in range(lax.axis_size('lon...  21.7 us
    pallas_call x1, Pallas kernels, body(): pl.pallas_call(functools.partial(block_kernel, chunk), out_shape=(pltpu.V...  19.4 us
    ppermute x2, starting transfers between devices, lon_halo(): lax.ppermute(strips, 'lon', [(i, i ^ 1) for i in range(lax.axis_size('lon...  17.5 us
    pallas_call x2, Pallas kernels, first_conv(): pl.pallas_call(functools.partial(conv_kernel, rows, flip), out_shape=out...  15.8 us
    ppermute x2, waiting for transfers between devices, lat_halo(): north = lax.ppermute(bottom, 'lat', down)  9.35 us
    ppermute x2, starting transfers between devices, lat_halo(): south = lax.ppermute(top, 'lat', up)  7.94 us
    all_to_all x1, starting transfers between devices, exchange(): lax.all_to_all(parts, ('lon', 'lat'), 0, 0, tiled=True, axis_index_groups...  7.13 us
  transfers between devices with their start and end apart: 9, of which 4 were waited for; matrix products, arithmetic and copies ran while one was open for 0% of the time, Pallas kernels for 14%

profile of v9, /device:TPU:103, one launch (start us, length us, event | category | flops | bytes accessed | tf_op | source)
XLA Modules:
  0.0 163.5 jit_solution(673603981803431694)
XLA Ops:
  0.6 0.8 convert_element_type.3
  1.4 0.0 copy-start.1
  1.4 1.9 %broadcast_multiply_fusion = (bf16[64,64,128]{2,1,0:T(8,128)(2,1)S(1)}, bf16[64,64,128]{2,1,0:T(8,128)(2,1)S(1)}) fusion(bf16[64,64,128]{2,1,0:T(8,128)(2,1)} %cot_ref.1, bf16[64,64]{1,0:T(8,128)(2,1)S(1)} %convert_element_type.3, bf16[64,64,128]{2,1,0:T(8,128)(2,1)} %param.10), kind=kLoop, calls=%fused_computation | loop fusion | flops 1048576 | bytes 4202496 | tf_op jit(solution)/shard_map/mul | solution.py:457
  3.3 5.3 %collective-permute-start = (bf16[3,64,128]{2,1,0:T(8,128)(2,1)S(1)}, bf16[3,64,128]{2,1,0:T(8,128)(2,1)S(1)}, u32[]{:S(2)}, u32[]{:S(2)}) collective-permute-start(bf16[3,64,128]{2,1,0:T(8,128)(2,1)S(1)} %get-tuple-element.37), channel_id=1, source_target_pairs={{0,1},{1,2},{2,3},{3,4},{4,5},{5,6},{6,7},{7,8},{8,9},{9,10},{10,1... | collective-permute-start | bytes 147464 | tf_op jit(solution)/shard_map/ppermute | solution.py:387
  8.7 1.9 %collective-permute-start.1 = (bf16[3,64,128]{2,1,0:T(8,128)(2,1)S(1)}, bf16[3,64,128]{2,1,0:T(8,128)(2,1)S(1)}, u32[]{:S(2)}, u32[]{:S(2)}) collective-permute-start(bf16[3,64,128]{2,1,0:T(8,128)(2,1)S(1)} %get-tuple-element.36), channel_id=1, source_target_pairs={{1,0},{2,1},{3,2},{4,3},{5,4},{6,5},{7,6},{8,7},{9,8},{10,9},{11,1... | collective-permute-start | bytes 147464 | tf_op jit(solution)/shard_map/ppermute | solution.py:388
  10.6 0.0 collective-permute-done.south_ref
  10.6 4.7 %collective-permute-done.1.north_ref = bf16[3,64,128]{2,1,0:T(8,128)(2,1)S(1)} collective-permute-done((bf16[3,64,128]{2,1,0:T(8,128)(2,1)S(1)}, bf16[3,64,128]{2,1,0:T(8,128)(2,1)S(1)}, u32[]{:S(2)}, u32[]{:S(2)}) %collective-permute-start.1) | collective-permute-done | bytes 49184 | tf_op jit(solution)/shard_map/ppermute | solution.py:388
  15.3 0.1 strips.2
  15.4 10.6 %collective-permute-start.2 = (bf16[2,3,72,128]{3,2,1,0:T(8,128)(2,1)S(1)}, bf16[2,3,72,128]{3,2,1,0:T(8,128)(2,1)S(1)}, u32[]{:S(2)}, u32[]{:S(2)}) collective-permute-start(bf16[2,3,72,128]{3,2,1,0:T(8,128)(2,1)S(1)} %strips.2), channel_id=1, source_target_pairs={{0,16},{16,0},{32,48},{48,32},{64,80},{80,64},{96,112},{112,96},{1... | collective-permute-start | bytes 331784 | tf_op jit(solution)/shard_map/ppermute | solution.py:408
  26.0 8.3 %collective-permute-done.2.both_ref.keep_ref = bf16[2,3,72,128]{3,2,1,0:T(8,128)(2,1)S(1)} collective-permute-done((bf16[2,3,72,128]{3,2,1,0:T(8,128)(2,1)S(1)}, bf16[2,3,72,128]{3,2,1,0:T(8,128)(2,1)S(1)}, u32[]{:S(2)}, u32[]{:S(2)}) %collective-permute-start.2) | collective-permute-done | bytes 110624 | tf_op jit(solution)/shard_map/ppermute | solution.py:408
  34.3 3.2 %collective-permute-start.3 = (bf16[3,72,128]{2,1,0:T(8,128)(2,1)S(1)}, bf16[3,72,128]{2,1,0:T(8,128)(2,1)S(1)}, u32[]{:S(2)}, u32[]{:S(2)}) collective-permute-start(bf16[3,72,128]{2,1,0:T(8,128)(2,1)S(1)} %onward.2), channel_id=1, source_target_pairs={{0,32},{32,64},{64,96},{96,128},{128,160},{160,192},{192,224},{224... | collective-permute-start | bytes 165896 | tf_op jit(solution)/shard_map/ppermute | solution.py:417
  37.5 0.0 copy-done.1
  37.6 6.4 %conv.1 = (f32[4096,128]{1,0:T(8,128)S(1)}, f32[8064,128]{1,0:T(8,128)S(1)}) custom-call(bf16[3,64,128]{2,1,0:T(8,128)(2,1)S(1)} %collective-permute-done.south_ref, bf16[64,64,128]{2,1,0:T(8,128)(2,1)S(1)} %get-tuple-element.39.block_ref, bf16[3,64,128]{2,1,0:T(8,128)(2,1)S(1)} %collective-permute-done.1.north_ref, f32[7,7,128]{2,1,0:T(8,128)S(1)} %copy-done.1), custom_call_target="tpu_custom_call" | custom-call | tf_op jit(solution)/shard_map/conv/pallas_call | solution.py:426
  43.9 0.0 copy-start.2
  44.0 0.0 copy-start.3
  44.0 0.0 copy-start.4
  44.0 0.0 copy-start.5
  44.0 0.0 copy-start.6
  44.0 0.0 copy-start.7
  44.0 3.9 %rest.1.conv_in = f32[4096,128]{1,0:T(8,128)S(1)} custom-call(f32[4096,128]{1,0:T(8,128)S(1)} %get-tuple-element.22.conv_in, f32[8064,128]{1,0:T(8,128)S(1)} %get-tuple-element.23.tiles_ref.tiles_in, f32[7,7,128]{2,1,0:T(8,128)S(1)} %copy-done.1), custom_call_target="tpu_custom_call", output_to_operand_aliasing={{}: (0, {})} | custom-call | tf_op jit(solution)/shard_map/rest/pallas_call | solution.py:438
  48.0 0.0 collective-permute-done.3.got_ref
  48.0 0.0 copy-done.2
  48.0 0.0 copy-done.3
  48.0 0.0 copy-done.4
  48.0 0.0 copy-done.5
  48.0 0.0 copy-done.6
  48.0 0.0 copy-done.7
  48.0 19.4 %block.1 = (f32[4096,128]{1,0:T(8,128)S(1)}, f32[8064,128]{1,0:T(8,128)S(1)}, bf16[64,64,128]{2,1,0:T(8,128)(2,1)S(1)}, bf16[3,64,128]{2,1,0:T(8,128)(2,1)S(1)},...) custom-call(s32[1]{0:T(128)} %bitcast.even_ref, ...), custom_call_target="tpu_custom_call", output_to_operand_aliasing={{0}: (1, {}), {1}: (2, {})} | custom-call | tf_op jit(solution)/shard_map/block/pallas_call | solution.py:467
  67.5 14.6 %all_to_all.15.parts_ref = bf16[32,40,128]{2,1,0:T(8,128)(2,1)S(1)} all-to-all(bf16[32,40,128]{2,1,0:T(8,128)(2,1)S(1)} %get-tuple-element.28), channel_id=1, replica_groups={{0,1,32,33,64,65,96,97,128,129,160,161,192,193,224,225,256,257,288,289,..., dimensions={0} | all-to-all | bytes 655360 | tf_op jit(solution)/shard_map/all_to_all | solution.py:359
  82.1 0.1 fold.2
  82.2 27.3 %all_to_all.16.parts_ref = bf16[16,40,128]{2,1,0:T(8,128)(2,1)S(1)} all-to-all(bf16[16,40,128]{2,1,0:T(8,128)(2,1)S(1)} %fold.2), channel_id=1, replica_groups={{0,2,4,6,8,10,12,14,16,18,20,22,24,26,28,30},{1,3,5,7,9,11,13,15,17,19,..., dimensions={0} | all-to-all | bytes 327680 | tf_op jit(solution)/shard_map/all_to_all | solution.py:359
  109.5 0.8 fold.3
  110.2 7.1 %all-to-all-start.2 = ((bf16[32,40,128]{2,1,0:T(8,128)(2,1)}), bf16[32,40,128]{2,1,0:T(8,128)(2,1)S(1)}, u32[]{:S(2)}, u32[]{:S(2)}) async-start(bf16[32,40,128]{2,1,0:T(8,128)(2,1)} %fold.3), calls=%async_computation.2 | async-start | bytes 655360 | tf_op jit(solution)/shard_map/all_to_all | solution.py:359
  117.4 2.6 %collective-permute-start.4 = (bf16[3,64,128]{2,1,0:T(8,128)(2,1)S(1)}, bf16[3,64,128]{2,1,0:T(8,128)(2,1)S(1)}, u32[]{:S(2)}, u32[]{:S(2)}) collective-permute-start(bf16[3,64,128]{2,1,0:T(8,128)(2,1)S(1)} %get-tuple-element.24), channel_id=1, source_target_pairs={{0,1},{1,2},{2,3},{3,4},{4,5},{5,6},{6,7},{7,8},{8,9},{9,10},{10,1... | collective-permute-start | bytes 147464 | tf_op jit(solution)/shard_map/ppermute | solution.py:387
  120.0 1.9 %collective-permute-start.5 = (bf16[3,64,128]{2,1,0:T(8,128)(2,1)S(1)}, bf16[3,64,128]{2,1,0:T(8,128)(2,1)S(1)}, u32[]{:S(2)}, u32[]{:S(2)}) collective-permute-start(bf16[3,64,128]{2,1,0:T(8,128)(2,1)S(1)} %get-tuple-element.26), channel_id=1, source_target_pairs={{1,0},{2,1},{3,2},{4,3},{5,4},{6,5},{7,6},{8,7},{9,8},{10,9},{11,1... | collective-permute-start | bytes 147464 | tf_op jit(solution)/shard_map/ppermute | solution.py:388
  121.9 0.0 collective-permute-done.4.south_ref
  122.0 4.7 %collective-permute-done.5.north_ref = bf16[3,64,128]{2,1,0:T(8,128)(2,1)S(1)} collective-permute-done((bf16[3,64,128]{2,1,0:T(8,128)(2,1)S(1)}, bf16[3,64,128]{2,1,0:T(8,128)(2,1)S(1)}, u32[]{:S(2)}, u32[]{:S(2)}) %collective-permute-start.5) | collective-permute-done | bytes 49184 | tf_op jit(solution)/shard_map/ppermute | solution.py:388
  126.6 0.1 strips.3
  126.7 6.9 %collective-permute-start.6 = (bf16[2,3,72,128]{3,2,1,0:T(8,128)(2,1)S(1)}, bf16[2,3,72,128]{3,2,1,0:T(8,128)(2,1)S(1)}, u32[]{:S(2)}, u32[]{:S(2)}) collective-permute-start(bf16[2,3,72,128]{3,2,1,0:T(8,128)(2,1)S(1)} %strips.3), channel_id=1, source_target_pairs={{0,16},{16,0},{32,48},{48,32},{64,80},{80,64},{96,112},{112,96},{1... | collective-permute-start | bytes 331784 | tf_op jit(solution)/shard_map/ppermute | solution.py:408
  133.7 13.4 %collective-permute-done.6.both_ref.keep_ref = bf16[2,3,72,128]{3,2,1,0:T(8,128)(2,1)S(1)} collective-permute-done((bf16[2,3,72,128]{3,2,1,0:T(8,128)(2,1)S(1)}, bf16[2,3,72,128]{3,2,1,0:T(8,128)(2,1)S(1)}, u32[]{:S(2)}, u32[]{:S(2)}) %collective-permute-start.6) | collective-permute-done | bytes 110624 | tf_op jit(solution)/shard_map/ppermute | solution.py:408
  147.0 0.0 copy-start
  147.0 3.2 %collective-permute-start.7 = (bf16[3,72,128]{2,1,0:T(8,128)(2,1)S(1)}, bf16[3,72,128]{2,1,0:T(8,128)(2,1)S(1)}, u32[]{:S(2)}, u32[]{:S(2)}) collective-permute-start(bf16[3,72,128]{2,1,0:T(8,128)(2,1)S(1)} %onward.3), channel_id=1, source_target_pairs={{0,32},{32,64},{64,96},{96,128},{128,160},{160,192},{192,224},{224... | collective-permute-start | bytes 165896 | tf_op jit(solution)/shard_map/ppermute | solution.py:417
  150.3 9.5 %back_conv.1.spread_in = f32[4096,128]{1,0:T(8,128)S(1)} custom-call(bf16[3,64,128]{2,1,0:T(8,128)(2,1)S(1)} %collective-permute-done.4.south_ref, bf16[64,64,128]{2,1,0:T(8,128)(2,1)S(1)} %get-tuple-element.25.block_ref, bf16[3,64,128]{2,1,0:T(8,128)(2,1)S(1)} %collective-permute-done.5.north_ref, f32[7,7,128]{2,1,0:T(8,128)S(1)} %copy-done.1), custom_call_target="tpu_custom_call" | custom-call | tf_op jit(solution)/shard_map/back_conv/pallas_call | solution.py:426
  159.7 0.0 collective-permute-done.7.got_ref
  159.7 0.6 broadcast_in_dim.2.mask_ref
  160.3 0.0 copy-done
  160.3 2.3 %back.1 = (f32[4096,128]{1,0:T(8,128)S(1)}, bf16[64,64,128]{2,1,0:T(8,128)(2,1)}) custom-call(s32[1]{0:T(128)} %bitcast.even_ref, f32[4096,128]{1,0:T(8,128)S(1)} %back_conv.1.spread_in, bf16[2,3,72,128]{3,2,1,0:T(8,128)(2,1)S(1)} %collective-permute-done.6.both_ref.keep_ref, ...), custom_call_target="tpu_custom_call", output_to_operand_aliasing={{0}: (1, {})} | custom-call | tf_op jit(solution)/shard_map/back/pallas_call | solution.py:501
  162.6 0.0 all-to-all-done.2.all_ref
  162.6 0.9 unpack.1
  (3 shorter events, 0.0 us)
Async XLA Ops:
  1.4 36.2 %copy-start.1 = (f32[7,7,128]{2,1,0:T(8,128)S(1)}, f32[7,7,128]{2,1,0:T(8,128)}, u32[]{:S(2)}) copy-start(f32[7,7,128]{2,1,0:T(8,128)} %kernel_ref.9) | copy-start | bytes 75268
  3.3 7.3 %collective-permute-start = (bf16[3,64,128]{2,1,0:T(8,128)(2,1)S(1)}, bf16[3,64,128]{2,1,0:T(8,128)(2,1)S(1)}, u32[]{:S(2)}, u32[]{:S(2)}) collective-permute-start(bf16[3,64,128]{2,1,0:T(8,128)(2,1)S(1)} %get-tuple-element.37), channel_id=1, source_target_pairs={{0,1},{1,2},{2,3},{3,4},{4,5},{5,6},{6,7},{7,8},{8,9},{9,10},{10,1... | collective-permute-start | bytes 147464 | tf_op jit(solution)/shard_map/ppermute | solution.py:387
  8.7 6.6 %collective-permute-start.1 = (bf16[3,64,128]{2,1,0:T(8,128)(2,1)S(1)}, bf16[3,64,128]{2,1,0:T(8,128)(2,1)S(1)}, u32[]{:S(2)}, u32[]{:S(2)}) collective-permute-start(bf16[3,64,128]{2,1,0:T(8,128)(2,1)S(1)} %get-tuple-element.36), channel_id=1, source_target_pairs={{1,0},{2,1},{3,2},{4,3},{5,4},{6,5},{7,6},{8,7},{9,8},{10,9},{11,1... | collective-permute-start | bytes 147464 | tf_op jit(solution)/shard_map/ppermute | solution.py:388
  15.4 18.9 %collective-permute-start.2 = (bf16[2,3,72,128]{3,2,1,0:T(8,128)(2,1)S(1)}, bf16[2,3,72,128]{3,2,1,0:T(8,128)(2,1)S(1)}, u32[]{:S(2)}, u32[]{:S(2)}) collective-permute-start(bf16[2,3,72,128]{3,2,1,0:T(8,128)(2,1)S(1)} %strips.2), channel_id=1, source_target_pairs={{0,16},{16,0},{32,48},{48,32},{64,80},{80,64},{96,112},{112,96},{1... | collective-permute-start | bytes 331784 | tf_op jit(solution)/shard_map/ppermute | solution.py:408
  34.3 13.6 %collective-permute-start.3 = (bf16[3,72,128]{2,1,0:T(8,128)(2,1)S(1)}, bf16[3,72,128]{2,1,0:T(8,128)(2,1)S(1)}, u32[]{:S(2)}, u32[]{:S(2)}) collective-permute-start(bf16[3,72,128]{2,1,0:T(8,128)(2,1)S(1)} %onward.2), channel_id=1, source_target_pairs={{0,32},{32,64},{64,96},{96,128},{128,160},{160,192},{192,224},{224... | collective-permute-start | bytes 165896 | tf_op jit(solution)/shard_map/ppermute | solution.py:417
  43.9 4.0 %copy-start.2 = (bf16[128,512]{1,0:T(8,128)(2,1)S(1)}, bf16[128,512]{1,0:T(8,128)(2,1)}, u32[]{:S(2)}) copy-start(bf16[128,512]{1,0:T(8,128)(2,1)} %w_in_ref.1) | copy-start | bytes 393220
  44.0 4.0 %copy-start.3 = (bf16[512,128]{1,0:T(8,128)(2,1)S(1)}, bf16[512,128]{1,0:T(8,128)(2,1)}, u32[]{:S(2)}) copy-start(bf16[512,128]{1,0:T(8,128)(2,1)} %w_out_ref.1) | copy-start | bytes 393220
  44.0 4.0 %copy-start.4 = (f32[512]{0:T(512)S(1)}, f32[512]{0:T(512)}, u32[]{:S(2)}) copy-start(f32[512]{0:T(512)} %param.18) | copy-start | bytes 6148
  44.0 4.0 %copy-start.5 = (f32[128]{0:T(128)S(1)}, f32[128]{0:T(128)}, u32[]{:S(2)}) copy-start(f32[128]{0:T(128)} %param.14) | copy-start | bytes 1540
  44.0 4.0 %copy-start.6 = (f32[128]{0:T(128)S(1)}, f32[128]{0:T(128)}, u32[]{:S(2)}) copy-start(f32[128]{0:T(128)} %param.15) | copy-start | bytes 1540
  44.0 4.0 %copy-start.7 = (f32[128]{0:T(128)S(1)}, f32[128]{0:T(128)}, u32[]{:S(2)}) copy-start(f32[128]{0:T(128)} %param.16) | copy-start | bytes 1540
  110.2 52.4 %all-to-all-start.2 = ((bf16[32,40,128]{2,1,0:T(8,128)(2,1)}), bf16[32,40,128]{2,1,0:T(8,128)(2,1)S(1)}, u32[]{:S(2)}, u32[]{:S(2)}) async-start(bf16[32,40,128]{2,1,0:T(8,128)(2,1)} %fold.3), calls=%async_computation.2 | async-start | bytes 655360 | tf_op jit(solution)/shard_map/all_to_all | solution.py:359
  117.4 4.6 %collective-permute-start.4 = (bf16[3,64,128]{2,1,0:T(8,128)(2,1)S(1)}, bf16[3,64,128]{2,1,0:T(8,128)(2,1)S(1)}, u32[]{:S(2)}, u32[]{:S(2)}) collective-permute-start(bf16[3,64,128]{2,1,0:T(8,128)(2,1)S(1)} %get-tuple-element.24), channel_id=1, source_target_pairs={{0,1},{1,2},{2,3},{3,4},{4,5},{5,6},{6,7},{7,8},{8,9},{9,10},{10,1... | collective-permute-start | bytes 147464 | tf_op jit(solution)/shard_map/ppermute | solution.py:387
  120.0 6.6 %collective-permute-start.5 = (bf16[3,64,128]{2,1,0:T(8,128)(2,1)S(1)}, bf16[3,64,128]{2,1,0:T(8,128)(2,1)S(1)}, u32[]{:S(2)}, u32[]{:S(2)}) collective-permute-start(bf16[3,64,128]{2,1,0:T(8,128)(2,1)S(1)} %get-tuple-element.26), channel_id=1, source_target_pairs={{1,0},{2,1},{3,2},{4,3},{5,4},{6,5},{7,6},{8,7},{9,8},{10,9},{11,1... | collective-permute-start | bytes 147464 | tf_op jit(solution)/shard_map/ppermute | solution.py:388
  126.7 20.3 %collective-permute-start.6 = (bf16[2,3,72,128]{3,2,1,0:T(8,128)(2,1)S(1)}, bf16[2,3,72,128]{3,2,1,0:T(8,128)(2,1)S(1)}, u32[]{:S(2)}, u32[]{:S(2)}) collective-permute-start(bf16[2,3,72,128]{3,2,1,0:T(8,128)(2,1)S(1)} %strips.3), channel_id=1, source_target_pairs={{0,16},{16,0},{32,48},{48,32},{64,80},{80,64},{96,112},{112,96},{1... | collective-permute-start | bytes 331784 | tf_op jit(solution)/shard_map/ppermute | solution.py:408
  147.0 13.3 %copy-start = (bf16[64,64,128]{2,1,0:T(8,128)(2,1)S(1)}, bf16[64,64,128]{2,1,0:T(8,128)(2,1)}, u32[]{:S(2)}) copy-start(bf16[64,64,128]{2,1,0:T(8,128)(2,1)} %cot_ref.1) | copy-start | bytes 3145732
  147.0 12.7 %collective-permute-start.7 = (bf16[3,72,128]{2,1,0:T(8,128)(2,1)S(1)}, bf16[3,72,128]{2,1,0:T(8,128)(2,1)S(1)}, u32[]{:S(2)}, u32[]{:S(2)}) collective-permute-start(bf16[3,72,128]{2,1,0:T(8,128)(2,1)S(1)} %onward.3), channel_id=1, source_target_pairs={{0,32},{32,64},{64,96},{96,128},{128,160},{160,192},{192,224},{224... | collective-permute-start | bytes 165896 | tf_op jit(solution)/shard_map/ppermute | solution.py:417
